TPU v7x, 256 devices: a whole 4x4x8 slice. The times are simulated.
256 devices in a mesh: facet: 64 (over z, x_lo, y), col: 4 (over x_hi, core).
Axes of the slice: x: 4 (x_hi: 2, x_lo: 2; x = x_hi * 2 + x_lo), y: 4, z: 8, core: 2. Of those that a mesh axis runs over, the one named last changes fastest.
Arguments:
- prepared: bfloat16 [64, 2, 8192, 512], P('facet', None, None, 'col'), may hold values from -6 to 6
- sub_off: int32 [64, 4], P(None, 'col'), may hold values from 0 to 8191
- fac_off: int32 [64], replicated, may hold values from 0 to 511
- win_col: int32 [4, 128], replicated, may hold values from 0 to 255
- vis_weights: bfloat16 [64, 2, 512, 512], P('facet', None, None, 'col'), may hold values from -6 to 6
Outputs:
- facet_strips: bfloat16 [64, 2, 8192, 256], P('facet', None, 'col')
All inputs are finite; a program needn't handle non-finite values.
Results may differ from a plain program's by a relative error of at most 0.0093.
Values may be sent and summed in bfloat16 or wider, within the bound.
No kernel may reach another device: no remote copies, remote signals or barrier semaphores. Data moves between devices by JAX's collectives and lax.ppermute only.
A program may use at most 128 MiB of HBM per device.

v0:
```python
import math

import jax
import jax.numpy as jnp
from jax import lax
from jax.sharding import PartitionSpec as P

XM = 128


def taper_curve(length):
    position = (jnp.arange(length, dtype=jnp.float32) + 0.5) / length
    return 0.3 + 0.7 * jnp.sin(math.pi * position) ** 2


def phases(row_ids, col_ids, length, sign_factor, scaling):
    products = row_ids[:, None] * col_ids[None, :] % length
    angles = 2.0 * math.pi / length * products.astype(jnp.float32)
    return (jnp.cos(angles) * scaling, sign_factor * jnp.sin(angles) * scaling)


def complex_block(real_part, imag_part):
    upper_rows = jnp.concatenate([real_part, -imag_part], axis=1)
    lower_rows = jnp.concatenate([imag_part, real_part], axis=1)
    return jnp.concatenate([upper_rows, lower_rows], axis=0).astype(jnp.bfloat16)


def small_tables(length):
    positions = jnp.arange(length, dtype=jnp.int32)
    taper_vals = taper_curve(length)
    fwd_re, fwd_im = phases(positions, positions, length, -1.0, 1.0 / math.sqrt(length))
    back_re, back_im = phases(positions, positions, length, 1.0, 1.0 / math.sqrt(length))
    forward = complex_block(fwd_re * taper_vals[None, :], fwd_im * taper_vals[None, :])
    backward = complex_block(back_re * taper_vals[:, None], back_im * taper_vals[:, None])
    return (forward, backward)


def grid_tables(length, facet_count, contrib_len):
    positions = jnp.arange(length, dtype=jnp.int32)
    fwd_re, fwd_im = phases(
        positions, positions, length, -1.0, 1.0 / math.sqrt(facet_count * contrib_len)
    )
    back_re, back_im = phases(positions, positions, length, 1.0, 1.0 / math.sqrt(length))
    return (complex_block(fwd_re, fwd_im), complex_block(back_re, back_im))


def finish_map(columns, out_cols):
    frequency = jnp.arange(out_cols, dtype=jnp.int32)
    products = columns[:, None] * frequency[None, :] % out_cols
    angles = 2.0 * math.pi / out_cols * products.astype(jnp.float32)
    scaling = 1.0 / math.sqrt(2 * out_cols)
    real_part = jnp.cos(angles) * scaling
    imag_part = jnp.sin(angles) * scaling
    from_real = jnp.concatenate([real_part, imag_part], axis=1)
    from_imag = jnp.concatenate([-imag_part, real_part], axis=1)
    return jnp.stack([from_real, from_imag], axis=0).astype(jnp.bfloat16)


def apply_weights(spectrum, weights):
    spec_re = spectrum[..., 0, :, :]
    spec_im = spectrum[..., 1, :, :]
    weight_re = weights[..., 0, :, :].astype(jnp.float32)
    weight_im = weights[..., 1, :, :].astype(jnp.float32)
    joined = jnp.stack(
        [weight_re * spec_re - weight_im * spec_im, weight_re * spec_im + weight_im * spec_re],
        axis=-3,
    )
    return joined.astype(jnp.bfloat16)


def body(prepared, sub_off, fac_off, win_col, vis_weights):
    facet_count = fac_off.shape[0]
    group_count = lax.axis_size("facet")
    per_device = vis_weights.shape[0]
    grid_len = vis_weights.shape[2]
    facet_strip = prepared[0]
    facet_len = facet_strip.shape[1]
    strip_width = facet_strip.shape[2]
    window_pos = jnp.arange(XM, dtype=jnp.int32)
    forward_small, backward_small = small_tables(XM)
    forward_grid, backward_grid = grid_tables(grid_len, facet_count, XM)
    starts = sub_off[:, 0].reshape(group_count, per_device).T
    src_rows = (starts[:, :, None] + window_pos[None, None, :]) % facet_len
    picked = (
        facet_strip[:, src_rows]
        .transpose(1, 2, 0, 3, 4)
        .reshape(per_device, group_count, 2 * XM, strip_width)
    )
    payload = jnp.einsum(
        "ab,sfbc->sfac", forward_small, picked, preferred_element_type=jnp.float32
    ).astype(jnp.bfloat16)
    arrived = lax.all_to_all(payload, "facet", split_axis=1, concat_axis=1, tiled=True)
    dest_rows = ((fac_off[:, None] + window_pos[None, :]) % grid_len).reshape(-1)
    placement = (dest_rows[None, :] == jnp.arange(grid_len, dtype=jnp.int32)[:, None]).astype(
        jnp.bfloat16
    )
    flat_rows = arrived.reshape(per_device, facet_count, 2, XM, strip_width).transpose(
        0, 2, 1, 3, 4
    )
    flat_rows = flat_rows.reshape(per_device, 2, facet_count * XM, strip_width)
    assembled = jnp.einsum(
        "rq,spqc->sprc", placement, flat_rows, preferred_element_type=jnp.float32
    ).astype(jnp.bfloat16)
    spectrum = jnp.einsum(
        "ab,sbc->sac",
        forward_grid,
        assembled.reshape(per_device, 2 * grid_len, strip_width),
        preferred_element_type=jnp.float32,
    )
    weighted = apply_weights(spectrum.reshape(per_device, 2, grid_len, strip_width), vis_weights)
    grid_image = jnp.einsum(
        "ab,sbc->sac",
        backward_grid,
        weighted.reshape(per_device, 2 * grid_len, strip_width),
        preferred_element_type=jnp.float32,
    )
    grid_image = grid_image.astype(jnp.bfloat16).reshape(per_device, 2, grid_len, strip_width)
    back_rows = (
        grid_image[:, :, dest_rows]
        .reshape(per_device, 2, facet_count, XM, strip_width)
        .transpose(0, 2, 1, 3, 4)
    )
    back_rows = back_rows.reshape(per_device, facet_count, 2 * XM, strip_width)
    returned = lax.all_to_all(back_rows, "facet", split_axis=1, concat_axis=1, tiled=True)
    item_count = per_device * group_count
    returned_terms = jnp.einsum(
        "ab,sfbc->sfac", backward_small, returned, preferred_element_type=jnp.float32
    )
    returned_terms = returned_terms.reshape(item_count, 2, XM, strip_width)
    item_starts = starts.reshape(-1)
    row_shift = item_starts % XM
    block_ids = item_starts // XM
    block_count = facet_len // XM
    padded_terms = jnp.concatenate([returned_terms, jnp.zeros_like(returned_terms)], axis=2)
    frames = jax.vmap(lambda term, amount: jnp.roll(term, amount, axis=1))(padded_terms, row_shift)
    frames = frames.reshape(item_count, 2, 2, XM, strip_width)
    block_range = jnp.arange(block_count, dtype=jnp.int32)[:, None]
    lower_hits = (block_ids[None, :] == block_range).astype(jnp.float32)
    upper_hits = (((block_ids + 1) % block_count)[None, :] == block_range).astype(jnp.float32)
    accum = jnp.einsum(
        "bs,spyc->pbyc", lower_hits, frames[:, :, 0], precision=lax.Precision.HIGHEST
    )
    accum = accum + jnp.einsum(
        "bs,spyc->pbyc", upper_hits, frames[:, :, 1], precision=lax.Precision.HIGHEST
    )
    strip_sum = accum.reshape(2, facet_len, strip_width).astype(jnp.bfloat16)
    col_count = lax.axis_size("col")
    out_cols = strip_width * col_count // 2
    own_rows = facet_len // col_count
    own_map = finish_map(
        lax.dynamic_index_in_dim(win_col, lax.axis_index("col"), 0, keepdims=False), out_cols
    )
    summed = lax.psum_scatter(
        jnp.einsum("pyk,pkm->ym", strip_sum, own_map, preferred_element_type=jnp.float32),
        "col",
        scatter_dimension=0,
        tiled=True,
    )
    result = summed.astype(jnp.bfloat16).reshape(own_rows, 2, out_cols).transpose(1, 0, 2)
    return result.reshape(1, 2, own_rows, out_cols)


def solution(mesh):
    in_specs = (
        P("facet", None, None, "col"),
        P(None, "col"),
        P(),
        P(),
        P("facet", None, None, "col"),
    )
    out_specs = P("facet", None, "col", None)
    return jax.shard_map(body, mesh=mesh, in_specs=in_specs, out_specs=out_specs, check_vma=False)
```

profile of v0, /device:TPU:1, one launch (start us, length us, event | category | flops | bytes accessed | tf_op | source)
XLA Modules:
  0.0 705.0 jit_solution(9312600770579441535)
XLA Ops:
  6.5 0.0 copy-start
  6.5 0.1 broadcast_multiply_fusion
  6.6 0.1 broadcast_multiply_fusion.1
  6.6 0.0 copy-start.3
  6.7 10.1 %copy.61 = bf16[1,2,8192,128]{3,1,2,0:T(2,128)(2,1)} copy(bf16[1,2,8192,128]{3,2,1,0:T(8,128)(2,1)} %param.5) | data formatting | bytes 8388608 | tf_op args[0]
  16.8 0.0 copy-done.3
  16.8 0.1 fusion.86
  16.9 55.9 %gather_fusion = bf16[8192,2,128]{2,1,0:T(2,128)(2,1)} fusion(bf16[2,8192,128]{2,0,1:T(2,128)(2,1)} %bitcast.144, s32[8192]{0:T(1024)S(1)} %fusion.86), kind=kCustom, calls=%fused_computation | custom fusion | bytes 8421376 | tf_op jit(solution)/shard_map/gather | solution.py:85
  72.8 14.8 %copy.30 = bf16[1,64,2,128,128]{3,2,4,1,0:T(2,128)(2,1)} copy(bf16[1,64,2,128,128]{4,2,3,1,0:T(2,128)(2,1)} %bitcast.142) | data formatting | bytes 8388608 | tf_op jit(solution)/shard_map/transpose | solution.py:86
  87.6 7.6 %reshape.348 = bf16[64,256,128]{1,2,0:T(8,128)(2,1)} reshape(bf16[1,64,2,128,128]{3,2,4,1,0:T(2,128)(2,1)} %copy.30) | data formatting | bytes 8388608 | tf_op jit(solution)/shard_map/reshape.2
  95.2 0.3 negate_convert_fusion.3
  95.5 5.5 convert_bitcast_fusion
  100.9 0.0 copy-start.2
  100.9 14.2 %all-to-all-start = ((bf16[1,64,256,128]{2,3,0,1:T(8,128)(2,1)}), bf16[1,64,256,128]{2,3,0,1:T(8,128)(2,1)}, u32[]{:S(2)}, u32[]{:S(2)}) async-start(bf16[1,64,256,128]{2,3,0,1:T(8,128)(2,1)} %convert_bitcast_fusion), calls=%async_computation | async-start | bytes 8388608 | tf_op jit(solution)/shard_map/all_to_all | solution.py:92
  115.1 4.0 multiply_convert_fusion.3
  119.1 4.0 multiply_convert_fusion.2
  123.1 4.4 negate_convert_fusion.1
  127.5 4.4 negate_convert_fusion
  131.9 0.0 copy-done.2
  131.9 0.1 add_select_fusion.3
  132.0 0.1 iota_add_fusion
  132.1 0.1 compare_select_fusion
  132.2 75.0 %all-to-all-done = bf16[1,64,256,128]{2,3,0,1:T(8,128)(2,1)} async-done(((bf16[1,64,256,128]{2,3,0,1:T(8,128)(2,1)}), bf16[1,64,256,128]{2,3,0,1:T(8,128)(2,1)}, u32[]{:S(2)}, u32[]{:S(2)}) %all-to-all-start) | async-done | bytes 4194336 | tf_op jit(solution)/shard_map/all_to_all | solution.py:92
  207.2 6.9 reshape.349
  214.2 6.8 copy.60
  221.0 7.3 %reshape.350 = bf16[2,8192,128]{1,2,0:T(8,128)(2,1)} reshape(bf16[1,2,64,128,128]{3,2,4,1,0:T(8,128)(2,1)} %bitcast.145) | data formatting | bytes 8388608 | tf_op jit(solution)/shard_map/reshape.4
  228.3 6.0 fusion.37
  234.3 1.1 copy.33
  235.4 1.6 fusion.28
  237.1 1.2 copy.47
  238.3 1.1 fusion.52
  239.4 0.8 fusion.40
  240.2 0.2 reshape.369
  240.4 0.4 copy.36
  240.8 54.0 %gather_fusion.1 = bf16[8192,2,128]{2,1,0:T(2,128)(2,1)} fusion(bf16[2,512,128]{2,0,1:T(2,128)(2,1)S(1)} %copy.36, s32[8192]{0:T(1024)S(1)} %broadcast_clamp_fusion), kind=kCustom, calls=%fused_computation.1 | custom fusion | bytes 8421376 | tf_op jit(solution)/shard_map/gather | solution.py:119
  294.8 14.8 %copy.37 = bf16[1,64,2,128,128]{3,2,4,1,0:T(2,128)(2,1)} copy(bf16[1,64,2,128,128]{4,2,3,1,0:T(2,128)(2,1)} %bitcast.143) | data formatting | bytes 8388608 | tf_op jit(solution)/shard_map/transpose | solution.py:121
  309.6 8.0 %reshape.355 = bf16[1,64,256,128]{2,3,0,1:T(8,128)(2,1)} reshape(bf16[1,64,2,128,128]{3,2,4,1,0:T(2,128)(2,1)} %copy.37) | data formatting | bytes 8388608 | tf_op jit(solution)/shard_map/reshape | solution.py:123
  317.6 9.3 %all-to-all-start.1 = ((bf16[1,64,256,128]{2,3,0,1:T(8,128)(2,1)}), bf16[1,64,256,128]{2,3,0,1:T(8,128)(2,1)}, u32[]{:S(2)}, u32[]{:S(2)}) async-start(bf16[1,64,256,128]{2,3,0,1:T(8,128)(2,1)} %reshape.355), calls=%async_computation.1 | async-start | bytes 8388608 | tf_op jit(solution)/shard_map/all_to_all | solution.py:124
  326.9 0.0 reduce-scatter.2.cloned.1.call-start
  327.0 0.0 copy-done
  327.0 0.6 fusion.76
  327.7 91.4 %all-to-all-done.1 = bf16[1,64,256,128]{2,3,0,1:T(8,128)(2,1)} async-done(((bf16[1,64,256,128]{2,3,0,1:T(8,128)(2,1)}), bf16[1,64,256,128]{2,3,0,1:T(8,128)(2,1)}, u32[]{:S(2)}, u32[]{:S(2)}) %all-to-all-start.1) | async-done | bytes 4194336 | tf_op jit(solution)/shard_map/all_to_all | solution.py:124
  419.1 6.7 fusion.9
  425.8 10.8 %reshape.357 = f32[64,2,128,128]{2,1,3,0:T(2,128)} reshape(f32[1,64,256,128]{2,3,1,0:T(8,128)} %fusion.9) | data formatting | bytes 16777216 | tf_op jit(solution)/shard_map/reshape | solution.py:129
  436.6 16.0 %copy.38 = f32[64,2,128,128]{3,1,0,2:T(2,128)} copy(f32[64,2,128,128]{2,1,3,0:T(2,128)} %reshape.357) | data formatting | bytes 16777216 | tf_op jit(solution)/shard_map/reshape | solution.py:129
  452.6 7.4 %broadcast_in_dim.3 = f32[64,2,128,128]{3,1,0,2:T(2,128)} broadcast(f32[]{:T(128)} %constant.162.clone.1), dimensions={} | broadcast | bytes 8388612 | tf_op jit(solution)/shard_map/broadcast_in_dim | solution.py:134
  460.0 24.2 %pad_maximum_fusion = f32[64,2,512,128]{3,1,0,2:T(2,128)} fusion(f32[64,2,128,128]{3,1,0,2:T(2,128)} %broadcast_in_dim.3, f32[64,2,128,128]{3,1,0,2:T(2,128)} %copy.38), kind=kLoop, calls=%fused_computation.3 | loop fusion | flops 25165824 | bytes 50331648 | tf_op jit(solution)/shard_map/vmap(jit(_roll_dynamic))/concatenate | solution.py:135
  484.2 20.9 %gather_fusion.2 = f32[64,2,256,128]{3,1,2,0:T(2,128)} fusion(f32[64,2,512,128]{3,1,0,2:T(2,128)} %pad_maximum_fusion, s32[64]{0:T(128)S(1)} %or_bitcast_fusion), kind=kCustom, calls=%fused_computation.2 | custom fusion | bytes 33555456 | tf_op jit(solution)/shard_map/vmap(jit(_roll_dynamic))/gather | solution.py:135
  505.2 8.1 %copy.40 = f32[64,2,256,128]{3,2,1,0:T(8,128)S(1)} copy(f32[64,2,256,128]{3,1,2,0:T(2,128)} %gather_fusion.2) | data formatting | bytes 33554432 | tf_op jit(solution)/shard_map/vmap(jit(_roll_dynamic))/gather | solution.py:135
  513.2 6.3 fusion.108
  519.5 0.0 slice-start
  519.5 0.0 slice-start.1
  519.5 13.1 %fusion.3 = f32[2,128,128,64]{2,3,1,0:T(8,128)S(1)} fusion(f32[64,2,1,128,128]{4,3,2,1,0:T(8,128)} %get-tuple-element.8, s32[64]{0:T(128)S(1)} %get-tuple-element.5), kind=kOutput, calls=%fused_computation.9 | convolution fusion | flops 1610616832 | bytes 16777472 | tf_op jit(solution)/shard_map/bs,spyc->pbyc/dot_general | solution.py:143
  532.7 0.0 slice-done
  532.7 0.0 slice-done.1
  532.7 10.5 %fusion.6 = bf16[2,64,128,128]{3,1,2,0:T(8,128)(2,1)} fusion(f32[2,128,128,64]{2,3,1,0:T(8,128)S(1)} %fusion.3, f32[64,2,1,128,128]{4,3,2,1,0:T(8,128)S(1)} %bitcast.140, s32[64]{0:T(128)S(1)} %get-tuple-element.6), kind=kOutput, calls=%fused_computation.14 | convolution fusion | flops 1614811136 | bytes 20971776 | tf_op jit(solution)/shard_map/bs,spyc->pbyc/dot_general | solution.py:140
  543.2 4.9 copy.43
  548.0 7.0 convolution_bitcast_fusion
  555.1 0.0 reduce-scatter.2.cloned.1.call-update
  555.1 0.0 copy-start.1
  555.1 139.0 %reduce-scatter.2.cloned.1.call-done = f32[2048,512]{1,0:T(8,128)} async-done(((f32[8192,512]{1,0:T(8,128)}), f32[2048,512]{1,0:T(8,128)}) %reduce-scatter.2.cloned.1.call-update) | async-done | bytes 4194320 | tf_op jit(solution)/shard_map/reduce_scatter | solution.py:153
  694.0 2.5 convert_element_type.128
  696.5 1.5 copy.62
  698.0 0.0 copy-done.1
  (7 shorter events, 0.1 us)
Async XLA Ops:
  6.5 320.5 %copy-start = (s32[4,128]{1,0:T(4,128)S(1)}, s32[4,128]{1,0:T(4,128)}, u32[]{:S(2)}) copy-start(s32[4,128]{1,0:T(4,128)} %param.8) | copy-start | bytes 6148
  6.6 10.2 %copy-start.3 = (s32[64,1]{0,1:T(1,128)S(1)}, s32[64,1]{0,1:T(1,128)}, u32[]{:S(2)}) copy-start(s32[64,1]{0,1:T(1,128)} %param.6) | copy-start | bytes 772
  100.9 31.0 %copy-start.2 = (s32[64]{0:T(128)S(1)}, s32[64]{0:T(128)}, u32[]{:S(2)}) copy-start(s32[64]{0:T(128)} %param.7) | copy-start | bytes 772
  100.9 106.3 %all-to-all-start = ((bf16[1,64,256,128]{2,3,0,1:T(8,128)(2,1)}), bf16[1,64,256,128]{2,3,0,1:T(8,128)(2,1)}, u32[]{:S(2)}, u32[]{:S(2)}) async-start(bf16[1,64,256,128]{2,3,0,1:T(8,128)(2,1)} %convert_bitcast_fusion), calls=%async_computation | async-start | bytes 8388608 | tf_op jit(solution)/shard_map/all_to_all | solution.py:92
  317.6 101.5 %all-to-all-start.1 = ((bf16[1,64,256,128]{2,3,0,1:T(8,128)(2,1)}), bf16[1,64,256,128]{2,3,0,1:T(8,128)(2,1)}, u32[]{:S(2)}, u32[]{:S(2)}) async-start(bf16[1,64,256,128]{2,3,0,1:T(8,128)(2,1)} %reshape.355), calls=%async_computation.1 | async-start | bytes 8388608 | tf_op jit(solution)/shard_map/all_to_all | solution.py:124
  326.9 367.1 %reduce-scatter.2.cloned.1.call-start = ((), (), s32[]{:S(2)}) async-start(), calls=%async_computation.3 | async-start | bytes 20971520 | tf_op jit(solution)/shard_map/reduce_scatter | solution.py:153
  519.5 13.1 %slice-start = ((s8[8388608]{0:T(1024)(128)(4,1)}), s8[4194304]{0:T(1024)(128)(4,1)S(1)}, s32[]{:S(2)}) async-start(s8[8388608]{0:T(1024)(128)(4,1)} %bitcast.139), calls=%async_computation.4 | async-start | bytes 8388608
  519.5 13.1 %slice-start.1 = ((s8[8388608]{0:T(1024)(128)(4,1)}), s8[4194304]{0:T(1024)(128)(4,1)S(1)}, s32[]{:S(2)}) async-start(s8[8388608]{0:T(1024)(128)(4,1)} %bitcast.139), calls=%async_computation.5 | async-start | bytes 8388608
  555.1 142.9 %copy-start.1 = (s32[4,128]{1,0:T(4,128)S(1)}, s32[4,128]{1,0:T(4,128)}, u32[]{:S(2)}) copy-start(s32[4,128]{1,0:T(4,128)} %param.8) | copy-start | bytes 6148
Sparse Core Ops, SparseCore 0:
  555.2 138.7 reduce-scatter.1
where the time goes:
time: 712 us; the launch traced here: 705 us
  waiting for transfers between devices  305 us (43%)
  local copies, waits for them, and re-layouts  265 us (37%)
  matrix products  51.2 us (7%)
  other arithmetic  46 us (6%)
  starting transfers between devices  23.5 us (3%)
  between operations  13.8 us (2%)
    reduce_scatter x1, waiting for transfers between devices, body(): lax.psum_scatter(jnp.einsum('pyk,pkm->ym', strip_sum, own_map, preferred_...  139 us
    all_to_all x1, waiting for transfers between devices, body(): lax.all_to_all(back_rows, 'facet', split_axis=1, concat_axis=1, tiled=True)  91.4 us
    all_to_all x1, waiting for transfers between devices, body(): lax.all_to_all(payload, 'facet', split_axis=1, concat_axis=1, tiled=True)  75 us
    gather x1, local copies, waits for them, and re-layouts, body(): facet_strip[:, src_rows].transpose(1, 2, 0, 3, 4)  55.9 us
    gather x1, local copies, waits for them, and re-layouts, body(): grid_image[:, :, dest_rows]  54 us
    gather x2, local copies, waits for them, and re-layouts, body(): jnp.roll(term, amount, axis=1)  29 us
    reshape x2, local copies, waits for them, and re-layouts, body(): returned_terms = returned_terms.reshape(item_count, 2, XM, strip_width)  26.7 us
    concatenate x1, other arithmetic, body(): jnp.roll(term, amount, axis=1)  24.2 us
  transfers between devices with their start and end apart: 3, of which 3 were waited for; matrix products, arithmetic and copies ran while one was open for 3% of the time, Pallas kernels for 0%

commit v1 on v0

v1 whole, which is shorter than its diff:
```python
import math

import jax
import jax.numpy as jnp
import ml_dtypes
import numpy as np
from jax import lax
from jax.experimental import pallas as pl
from jax.experimental.pallas import tpu as pltpu
from jax.sharding import Mesh
from jax.sharding import PartitionSpec as P

XM = 128
LANES = 128
HALF = LANES // 2
BF16 = jnp.bfloat16
F32 = jnp.float32
FACET = ("z", "xl", "y")
NEAR = ("xl", "y")


def side_by_side(real_part, imag_part):
    return np.concatenate([real_part, imag_part], axis=1).astype(ml_dtypes.bfloat16)


def waves(length, sign_factor, scaling):
    positions = np.arange(length)
    angles = 2.0 * np.pi / length * ((positions[:, None] * positions[None, :]) % length)
    return np.cos(angles) * scaling, sign_factor * np.sin(angles) * scaling


def small_tables():
    taper = 0.3 + 0.7 * np.sin(np.pi * (np.arange(XM) + 0.5) / XM) ** 2
    fwd_re, fwd_im = waves(XM, -1.0, 1.0 / math.sqrt(XM))
    back_re, back_im = waves(XM, 1.0, 1.0 / math.sqrt(XM))
    forward = side_by_side(fwd_re * taper[None, :], fwd_im * taper[None, :])
    backward = side_by_side(back_re * taper[:, None], back_im * taper[:, None])
    return forward, backward


def grid_table(grid_len, facet_count):
    coarse = np.arange(0, grid_len, 16)[:, None] * np.arange(grid_len)[None, :] % grid_len
    fine = np.arange(16)[:, None] * np.arange(grid_len)[None, :] % grid_len
    scaling = 1.0 / math.sqrt(facet_count * XM)
    coarse = np.exp(-2j * np.pi * coarse / grid_len) * scaling
    fine = np.exp(-2j * np.pi * fine / grid_len)
    parts = [p.astype(np.float32) for p in (coarse.real, coarse.imag, fine.real, fine.imag)]
    c_re, c_im, f_re, f_im = lax.optimization_barrier(tuple(jnp.asarray(p) for p in parts))
    c_re, c_im = c_re[:, None, :], c_im[:, None, :]
    f_re, f_im = f_re[None, :, :], f_im[None, :, :]
    real_part = (c_re * f_re - c_im * f_im).reshape(grid_len, grid_len).astype(BF16)
    imag_part = (c_re * f_im + c_im * f_re).reshape(grid_len, grid_len).astype(BF16)
    return jnp.concatenate([real_part, imag_part], axis=1)


def finish_maps(columns, out_cols):
    frequency = jnp.arange(out_cols, dtype=jnp.int32)
    products = columns[:, :, None] * frequency[None, None, :] % out_cols
    angles = 2.0 * math.pi / out_cols * products.astype(F32)
    scaling = 1.0 / math.sqrt(2 * out_cols)
    real_part = jnp.cos(angles) * scaling
    imag_part = jnp.sin(angles) * scaling
    from_real = jnp.concatenate([real_part, imag_part], axis=2).astype(BF16)
    from_imag = jnp.concatenate([-imag_part, real_part], axis=2).astype(BF16)
    cols = columns.shape[0]
    shape = (cols, LANES // HALF, 1, HALF, 2 * out_cols)
    both = jnp.concatenate([from_real.reshape(shape), from_imag.reshape(shape)], axis=2)
    return both.transpose(1, 0, 2, 3, 4).reshape(LANES // HALF, cols, LANES, 2 * out_cols)


def low_half(shape):
    return lax.broadcasted_iota(jnp.int32, shape, len(shape) - 1) < HALF


def turn(block):
    swapped = pltpu.roll(block, HALF, 1)
    return jnp.where(low_half(block.shape), -swapped, swapped)


def pack(chunk, real_part, imag_part):
    if chunk == 0:
        return jnp.where(low_half(real_part.shape), real_part, pltpu.roll(imag_part, HALF, 1))
    return jnp.where(low_half(real_part.shape), pltpu.roll(real_part, HALF, 1), imag_part)


def stack_turned(blocks):
    tops = jnp.concatenate(blocks, axis=1)
    lows = jnp.concatenate([turn(b) for b in blocks], axis=1)
    return jnp.concatenate([tops, lows], axis=0).astype(BF16)


def contrib_kernel(chunk, place, starts, strip, table, out, held, source, made_rows, in_sems, out_sems):
    facet_len = strip.shape[1]
    parts = in_sems.shape[0]
    share = facet_len // parts
    tile = 256

    def fetch(p):
        rows = pl.ds(p * share, share)
        return pltpu.make_async_copy(strip.at[:, rows, :], held.at[:, rows, :], in_sems.at[p])

    for p in range(parts):
        fetch(p).start()

    def fill(i, _):
        rows = pl.ds(pl.multiple_of(i * tile, tile), tile)
        source[rows, :] = pack(chunk, held[0, rows, :].astype(F32), held[1, rows, :].astype(F32))
        return 0

    for p in range(parts):
        fetch(p).wait()
        lax.fori_loop(p * (share // tile), (p + 1) * (share // tile), fill, 0)
    source[pl.ds(facet_len, XM), :] = source[pl.ds(0, XM), :]
    planes, depth = out.shape[0], out.shape[1]

    def send(k):
        return pltpu.make_async_copy(made_rows.at[:, k], out.at[:, k], out_sems.at[k])

    def one_group(k, _):
        item = lax.rem(place[0] + k, depth) * planes
        for j in range(0, planes, 2):
            first = source[pl.ds(starts[item + j], XM), :]
            second = source[pl.ds(starts[item + j + 1], XM), :]
            made = jnp.dot(table[...], stack_turned([first, second]), preferred_element_type=F32)
            made_rows[j, k] = made[:, :LANES].astype(BF16)
            made_rows[j + 1, k] = made[:, LANES:].astype(BF16)
        send(k).start()
        return 0

    lax.fori_loop(0, depth, one_group, 0)
    for k in range(depth):
        send(k).wait()


def gather_kernel(chunk, place, offsets, arrived, *refs):
    *outs, held, total, sems = refs
    planes = arrived.shape[0]
    grid_len = total.shape[0] - XM
    base = chunk * grid_len

    def fetch(k):
        return pltpu.make_async_copy(arrived.at[:, k], held.at[:, k], sems.at[k])

    for k in range(len(outs)):
        fetch(k).start()
    for k, out in enumerate(outs):
        total[...] = jnp.zeros_like(total)
        fetch(k).wait()

        def one_facet(j, _, k=k):
            rows = pl.ds(offsets[place[0] * planes + j], XM)
            total[rows, :] = total[rows, :] + held[j, k].astype(F32)
            return 0

        lax.fori_loop(0, planes, one_facet, 0, unroll=2)
        total[pl.ds(0, XM), :] = total[pl.ds(0, XM), :] + total[pl.ds(grid_len, XM), :]
        out[pl.ds(base, grid_len), :] = total[pl.ds(0, grid_len), :].astype(BF16)
        if base > 0:
            out[pl.ds(0, base), :] = jnp.zeros((base, LANES), BF16)


def grid_kernel(chunk, weights, table, *refs):
    *parts, out = refs
    grid_len = weights.shape[1]
    rows = pl.ds(chunk * grid_len, grid_len)
    total = parts[0][rows, :].astype(F32)
    for part in parts[1:]:
        total = total + part[rows, :].astype(F32)
    assembled = total.astype(BF16).astype(F32)
    spectrum = jnp.dot(table[...], stack_turned([assembled]), preferred_element_type=F32)
    weight_re = weights[0].astype(F32)
    weight_im = weights[1].astype(F32)
    both_re = pack(chunk, weight_re, weight_re)
    both_im = pack(chunk, weight_im, weight_im)
    weighted = (both_re * spectrum + both_im * turn(spectrum)).astype(BF16).astype(F32)
    back = jnp.concatenate([weighted, -turn(weighted)], axis=0).astype(BF16)
    image = jnp.dot(table[...], back, preferred_element_type=F32)
    out[pl.ds(0, grid_len), :] = (image * 4.0).astype(BF16)
    if chunk == 0:
        out[pl.ds(grid_len, grid_len), :] = jnp.zeros((grid_len, LANES), BF16)


def spread_kernel(place, offsets, *refs):
    *images, out, wide, made_rows, sems = refs
    grid_len = wide.shape[0] - XM
    planes = out.shape[0]

    def send(k):
        return pltpu.make_async_copy(made_rows.at[:, k], out.at[:, k], sems.at[k])

    for k, image in enumerate(images):
        wide[pl.ds(0, grid_len), :] = image[pl.ds(0, grid_len), :].astype(F32)
        wide[pl.ds(grid_len, XM), :] = wide[pl.ds(0, XM), :]

        def one_facet(j, _, k=k):
            rows = pl.ds(offsets[place[0] * planes + j], XM)
            made_rows[j, k] = wide[rows, :].astype(BF16)
            return 0

        lax.fori_loop(0, planes, one_facet, 0, unroll=2)
        send(k).start()
    for k in range(len(images)):
        send(k).wait()


def accum_kernel(place, starts, returned, table, *refs):
    *outs, held, total, sems = refs
    planes, depth = returned.shape[0], returned.shape[1]
    own_rows = outs[0].shape[0]
    facet_len = own_rows * len(outs)

    def fetch(k):
        return pltpu.make_async_copy(returned.at[:, k], held.at[:, k], sems.at[k])

    for k in range(depth):
        fetch(k).start()
    total[...] = jnp.zeros_like(total)

    def one_group(k, _):
        fetch(k).wait()
        item = lax.rem(place[0] + depth - k, depth) * planes
        for j in range(0, planes, 2):
            blocks = [held[j, k].astype(F32), held[j + 1, k].astype(F32)]
            made = jnp.dot(table[...], stack_turned(blocks), preferred_element_type=F32)
            for n in range(2):
                rows = pl.ds(starts[item + j + n], XM)
                total[rows, :] = total[rows, :] + made[:, n * LANES : (n + 1) * LANES]
        return 0

    lax.fori_loop(0, depth, one_group, 0)
    total[pl.ds(0, XM), :] = total[pl.ds(0, XM), :] + total[pl.ds(facet_len, XM), :]
    tile = 256
    for k, out in enumerate(outs):
        first = jnp.bitwise_xor(place[1], k) * own_rows

        def drain(i, _, out=out, first=first):
            rows = pl.ds(pl.multiple_of(first + i * tile, tile), tile)
            out[pl.ds(pl.multiple_of(i * tile, tile), tile), :] = total[rows, :].astype(BF16)
            return 0

        lax.fori_loop(0, own_rows // tile, drain, 0)


def window(place, strips, maps):
    made = None
    for k, strip in enumerate(strips):
        term = jnp.dot(
            strip[...], maps[jnp.bitwise_xor(place[1], k)], preferred_element_type=F32
        )
        made = term if made is None else made + term
    return made


def half_kernel(place, maps, *strips_and_out):
    *strips, out = strips_and_out
    out[...] = window(place, strips, maps)


def finish_kernel(place, maps, made, *strips_and_out):
    *strips, out = strips_and_out
    out_cols = out.shape[2]
    both = made[...] + window(place, strips, maps)
    out[0] = both[:, :out_cols].astype(BF16)
    out[1] = both[:, out_cols:].astype(BF16)


SMEM = pl.BlockSpec(memory_space=pltpu.SMEM)
VMEM = pl.BlockSpec(memory_space=pltpu.VMEM)
HBM = pl.BlockSpec(memory_space=pltpu.HBM)


def call(kernel, name, outs, in_specs, scratch, micros, limit, where=VMEM):
    shapes = [jax.ShapeDtypeStruct(s, BF16) for s in outs]
    one = len(outs) == 1
    return pl.pallas_call(
        kernel,
        name=name,
        out_shape=shapes[0] if one else shapes,
        in_specs=in_specs,
        out_specs=where if one else [where] * len(outs),
        scratch_shapes=scratch,
        compiler_params=pltpu.CompilerParams(vmem_limit_bytes=limit << 20),
        cost_estimate=cost(micros),
    )


def cost(micros):
    return pl.CostEstimate(flops=0, bytes_accessed=int(micros * 3.5e6), transcendentals=0)


def bind(kernel, chunk):
    def bound(*refs):
        kernel(chunk, *refs)

    return bound


def shifted(value, step):
    size = lax.axis_size("z")
    return lax.ppermute(value, "z", [(i, (i + step) % size) for i in range(size)])


def swapped(value, flip):
    return lax.ppermute(value, "col", [(i, i ^ flip) for i in range(lax.axis_size("col"))])


def add(first, second):
    return (first.astype(F32) + second.astype(F32)).astype(BF16)


def body(prepared, sub_off, fac_off, win_col, vis_weights):
    depth = lax.axis_size("z")
    planes = lax.axis_size(NEAR)
    facet_count = fac_off.shape[0]
    strip = prepared[0]
    weights = vis_weights[0]
    facet_len = strip.shape[1]
    grid_len = weights.shape[1]
    col_count = lax.axis_size("col")
    own_rows = facet_len // col_count
    out_cols = LANES * col_count // 2
    place = jnp.stack([lax.axis_index("z"), lax.axis_index("col")]).astype(jnp.int32)
    starts = jnp.bitwise_and(sub_off[:, 0], facet_len - 1)
    offsets = jnp.bitwise_and(fac_off, grid_len - 1)
    forward_small, backward_small = small_tables()
    grid_forward = grid_table(grid_len, facet_count)
    blocks = (planes, depth, XM, LANES)
    flips = sorted(range(1, col_count), reverse=True)

    long_rows = pltpu.VMEM((facet_len + XM, LANES), F32)
    grid_rows = pltpu.VMEM((grid_len + XM, LANES), F32)
    all_blocks = pltpu.VMEM(blocks, BF16)
    sems = pltpu.SemaphoreType.DMA((depth,))

    def contrib(c, strip):
        return call(
            bind(contrib_kernel, c), f"contrib{c}", [blocks], [SMEM, SMEM, HBM, VMEM],
            [pltpu.VMEM(strip.shape, BF16), long_rows, all_blocks, pltpu.SemaphoreType.DMA((8,)), sems],
            6.5, 63, HBM,
        )(place, starts, strip, forward_small)

    def near(value):
        return lax.all_to_all(value, NEAR, 0, 0, tiled=True)

    def gather(c, arrived):
        return call(
            bind(gather_kernel, c), f"gather{c}", [(grid_len * (1 + c), LANES)] * depth, [SMEM, SMEM, HBM],
            [all_blocks, grid_rows, sems], 2, 8,
        )(place, offsets, arrived)

    def image_of(c, parts):
        return call(
            bind(grid_kernel, c), f"grid{c}", [(grid_len * (2 - c), LANES)], [VMEM] * (2 + len(parts)), [], 1.5, 12
        )(weights, grid_forward, *parts)

    def spread(c, images):
        return call(
            spread_kernel, f"spread{c}", [blocks], [SMEM, SMEM] + [VMEM] * depth,
            [grid_rows, all_blocks, sems], 2, 8, HBM,
        )(place, offsets, *images)

    def accum(c, returned):
        return call(
            accum_kernel, f"accum{c}", [(own_rows, LANES)] * col_count,
            [SMEM, SMEM, HBM, VMEM], [all_blocks, long_rows, sems], 6, 14,
        )(place, starts, returned, backward_small)

    def exchange(summed):
        moved = {k: swapped(summed[k], k) for k in flips}
        return [summed[0]] + [moved[k] for k in range(1, col_count)]

    far, near_side = depth // 2, (depth - 1) // 2

    def reduce_step(parts, state, i):
        up, down = state
        up = shifted(up, 1)
        if i < far - 1:
            up = add(up, parts[far - 1 - i])
        if i < near_side:
            down = shifted(down, -1)
            if i < near_side - 1:
                down = add(down, parts[far + 2 + i])
        return up, down

    def share_step(state, i):
        up, down = state
        up = up + [shifted(up[-1], 1)]
        if i < near_side:
            down = down + [shifted(down[-1], -1)]
        return up, down

    def shared(state):
        up, down = state
        return up + down[:0:-1]

    barrier = lax.optimization_barrier
    maps = finish_maps(win_col, out_cols)
    payload0 = contrib(0, strip)
    payload0, strip = barrier((payload0, strip))
    arrived0 = near(payload0)
    payload1 = contrib(1, strip)
    arrived0, payload1, maps, grid_forward = barrier((arrived0, payload1, maps, grid_forward))
    arrived1 = near(payload1)
    parts0 = gather(0, arrived0)
    reduced0 = parts0[far], parts0[far + 1]
    for i in range(far):
        reduced0 = reduce_step(parts0, reduced0, i)
    image0 = image_of(0, [parts0[0], *reduced0])
    parts1 = gather(1, arrived1)
    image0, parts1 = barrier((image0, parts1))
    up, down = add(image0, parts1[far]), add(image0, parts1[far + 1])
    ups, downs = [], []
    for i in range(far):
        up = shifted(up, 1)
        ups.append(up)
        if i < near_side:
            down = shifted(down, -1)
            downs.append(down)
        if i < far - 1:
            up = add(up, parts1[far - 1 - i])
        if i < near_side - 1:
            down = add(down, parts1[far + 2 + i])
    image1 = image_of(1, [parts1[0], up, down])
    images0 = [image0] + ups + downs[::-1]
    image1, images0 = barrier((image1, images0))
    returned0 = near(spread(0, images0))
    share1 = [image1], [image1]
    for i in range(far):
        share1 = share_step(share1, i)
    spread1 = spread(1, shared(share1))
    returned0, spread1 = barrier((returned0, spread1))
    returned1 = near(spread1)
    strips0 = exchange(accum(0, returned0))
    strips1 = exchange(accum(1, returned1))

    tile = min(512, own_rows)
    strip_spec = pl.BlockSpec((tile, LANES), lambda i: (i, 0))
    maps_spec = pl.BlockSpec(maps.shape[1:], lambda i: (0, 0, 0))
    wide_spec = pl.BlockSpec((tile, 2 * out_cols), lambda i: (i, 0))
    half = pl.pallas_call(
        half_kernel,
        name="half",
        grid=(own_rows // tile,),
        out_shape=jax.ShapeDtypeStruct((own_rows, 2 * out_cols), F32),
        in_specs=[SMEM, maps_spec] + [strip_spec] * col_count,
        out_specs=wide_spec,
        compiler_params=pltpu.CompilerParams(vmem_limit_bytes=16 << 20),
        cost_estimate=cost(4),
    )(place, maps[0], *strips0)
    result = pl.pallas_call(
        finish_kernel,
        name="finish",
        grid=(own_rows // tile,),
        out_shape=jax.ShapeDtypeStruct((2, own_rows, out_cols), BF16),
        in_specs=[SMEM, maps_spec, wide_spec] + [strip_spec] * col_count,
        out_specs=pl.BlockSpec((2, tile, out_cols), lambda i: (0, i, 0)),
        compiler_params=pltpu.CompilerParams(vmem_limit_bytes=16 << 20),
        cost_estimate=cost(4),
    )(place, maps[1], half, *strips1)
    return result[None]


def solution(mesh):
    facets, cols = mesh.devices.shape
    fine = Mesh(
        mesh.devices.reshape(facets // 8, 2, 4, cols), ("z", "xl", "y", "col")
    )
    in_specs = (
        P(FACET, None, None, "col"),
        P(None, "col"),
        P(),
        P(),
        P(FACET, None, None, "col"),
    )
    out_specs = P(FACET, None, "col", None)
    return jax.shard_map(body, mesh=fine, in_specs=in_specs, out_specs=out_specs, check_vma=False)
```

time: 712 us -> 228 us (0.32)
  local copies, waits for them, and re-layouts: 265 us -> 1.56 us
  waiting for transfers between devices: 305 us -> 90.1 us
  starting transfers between devices: 23.5 us -> 83.6 us
  matrix products: 51.2 us -> 0 us
  Pallas kernels: 0 us -> 44.9 us
  other arithmetic: 46 us -> 6.56 us
  between operations: 13.8 us -> 0.45 us
    all_to_all x2 -> x4, waiting for transfers between devices: 166 us -> 13.2 us  [near(): return lax.all_to_all(value, NEAR, 0, 0, tiled=True)]
    reduce_scatter x1 -> x0, waiting for transfers between devices: 139 us -> none  [body(): lax.psum_scatter(jnp.einsum('pyk,pkm->ym', strip_sum, own_map, preferred_...]
    gather x4 -> x0, local copies, waits for them, and re-layouts: 139 us -> none  [the longest x1 55.9 us: body(): facet_strip[:, src_rows].transpose(1, 2, 0, 3, 4)]
    ppermute x0 -> x27, waiting for transfers between devices: none -> 76.8 us  [the longest x21 47.8 us: shifted(): lax.ppermute(value, 'z', [(i, (i + step) % size) for i in range(size)])]
    ppermute x0 -> x27, starting transfers between devices: none -> 61.2 us  [the longest x6 31.9 us: swapped(): lax.ppermute(value, 'col', [(i, i ^ flip) for i in range(lax.axis_size('c...]
    reshape x9 -> x0, local copies, waits for them, and re-layouts: 51.8 us -> none  [the longest x2 26.7 us: body(): returned_terms = returned_terms.reshape(item_count, 2, XM, strip_width)]
    dot_general x8 -> x0, matrix products: 51.2 us -> none  [the longest x1 13.1 us: body(): jnp.einsum('bs,spyc->pbyc', upper_hits, frames[:, :, 1], precision=lax.Pr...]
    pallas_call x0 -> x12, Pallas kernels: none -> 44.9 us  [the longest x2 17.4 us: contrib(): call(bind(contrib_kernel, c), f'contrib{c}', [blocks], [SMEM, SMEM, HBM,...]
  transfers between devices with their start and end apart: 3 -> 31, of which waited for: 3 -> 15; matrix products, arithmetic and copies ran while one was open for 3% -> 2% of each run, Pallas kernels for 0% -> 12%
where the time goes in v1:
time: 228 us; the launch traced here: 227 us
  waiting for transfers between devices  90.1 us (40%)
  starting transfers between devices  83.6 us (37%)
  Pallas kernels  44.9 us (20%)
  other arithmetic  6.56 us (3%)
    ppermute x21, waiting for transfers between devices, shifted(): lax.ppermute(value, 'z', [(i, (i + step) % size) for i in range(size)])  47.8 us
    ppermute x6, starting transfers between devices, swapped(): lax.ppermute(value, 'col', [(i, i ^ flip) for i in range(lax.axis_size('c...  31.9 us
    ppermute x21, starting transfers between devices, shifted(): lax.ppermute(value, 'z', [(i, (i + step) % size) for i in range(size)])  29.3 us
    ppermute x6, waiting for transfers between devices, swapped(): lax.ppermute(value, 'col', [(i, i ^ flip) for i in range(lax.axis_size('c...  29.1 us
    all_to_all x4, starting transfers between devices, near(): return lax.all_to_all(value, NEAR, 0, 0, tiled=True)  22.3 us
    pallas_call x2, Pallas kernels, contrib(): call(bind(contrib_kernel, c), f'contrib{c}', [blocks], [SMEM, SMEM, HBM,...  17.4 us
    all_to_all x4, waiting for transfers between devices, near(): return lax.all_to_all(value, NEAR, 0, 0, tiled=True)  13.2 us
    pallas_call x2, Pallas kernels, accum(): call(accum_kernel, f'accum{c}', [(own_rows, LANES)] * col_count, [SMEM, S...  9.38 us
  transfers between devices with their start and end apart: 31, of which 15 were waited for; matrix products, arithmetic and copies ran while one was open for 2% of the time, Pallas kernels for 12%

profile of v1, /device:TPU:1, one launch (start us, length us, event | category | flops | bytes accessed | tf_op | source)
XLA Modules:
  0.0 227.1 jit_solution(7813484365363758208)
XLA Ops:
  0.0 1.2 and_bitcast_fusion.refs_1_.starts
  1.2 0.6 pad_add_fusion.refs_0_.place
  1.8 8.7 %contrib0.1 = bf16[8,8,128,128]{3,2,1,0:T(8,128)(2,1)} custom-call(s32[2]{0:T(128)} %pad_add_fusion.refs_0_.place, s32[64]{0:T(128)} %and_bitcast_fusion.refs_1_.starts, bf16[2,8192,128]{2,1,0:T(8,128)(2,1)} %bitcast.26, bf16[128,256]{1,0:T(8,128)(2,1)} %constant.49.clone.refs_3_), custom_call_target="tpu_custom_call" | custom-call | bytes 22750000 | tf_op jit(solution)/shard_map/contrib0/pallas_call | solution.py:336
  10.5 6.0 %all-to-all-start = ((bf16[8,8,128,128]{3,2,1,0:T(8,128)(2,1)}), bf16[8,8,128,128]{3,2,1,0:T(8,128)(2,1)}, u32[]{:S(2)}, u32[]{:S(2)}) async-start(bf16[8,8,128,128]{3,2,1,0:T(8,128)(2,1)} %contrib0.1), calls=%async_computation | async-start | bytes 4194304 | tf_op jit(solution)/shard_map/all_to_all | solution.py:343
  16.5 0.1 mul.142
  16.6 8.7 %contrib1.1 = bf16[8,8,128,128]{3,2,1,0:T(8,128)(2,1)} custom-call(s32[2]{0:T(128)} %pad_add_fusion.refs_0_.place, s32[64]{0:T(128)} %and_bitcast_fusion.refs_1_.starts, bf16[2,8192,128]{2,1,0:T(8,128)(2,1)} %bitcast.27, bf16[128,256]{1,0:T(8,128)(2,1)} %constant.49.clone.refs_3_), custom_call_target="tpu_custom_call" | custom-call | bytes 22750000 | tf_op jit(solution)/shard_map/contrib1/pallas_call | solution.py:336
  25.3 0.4 subtract_convert_fusion
  25.7 0.1 pad_maximum_fusion.refs_1_
  25.8 2.6 %fusion.9 = (bf16[4,2,1,64,256]{4,3,2,0,1:T(8,128)(2,1)S(1)}, bf16[4,2,1,64,256]{4,3,2,0,1:T(8,128)(2,1)S(1)}, bf16[4,2,1,64,256]{4,3,2,0,1:T(8,128)(2,1)S(1)}) fusion(s32[4,2,64]{2,0,1:T(4,128)S(1)} %copy.12), kind=kLoop, calls=%fused_computation.28 | loop fusion | flops 2621440 | bytes 788480 | tf_op jit(solution)/shard_map/concatenate | solution.py:63
  28.4 1.1 maximum_maximum_fusion
  29.5 13.2 %all-to-all-done.refs_2_ = bf16[8,8,128,128]{3,2,1,0:T(8,128)(2,1)} async-done(((bf16[8,8,128,128]{3,2,1,0:T(8,128)(2,1)}), bf16[8,8,128,128]{3,2,1,0:T(8,128)(2,1)}, u32[]{:S(2)}, u32[]{:S(2)}) %all-to-all-start) | async-done | bytes 2097184 | tf_op jit(solution)/shard_map/all_to_all | solution.py:343
  42.7 3.8 %all-to-all-start.1 = ((bf16[8,8,128,128]{3,2,1,0:T(8,128)(2,1)}), bf16[8,8,128,128]{3,2,1,0:T(8,128)(2,1)S(1)}, u32[]{:S(2)}, u32[]{:S(2)}) async-start(bf16[8,8,128,128]{3,2,1,0:T(8,128)(2,1)} %contrib1.1), calls=%async_computation.1 | async-start | bytes 4194304 | tf_op jit(solution)/shard_map/all_to_all | solution.py:343
  46.6 2.5 %gather0.1 = (bf16[512,128]{1,0:T(8,128)(2,1)S(1)}, bf16[512,128]{1,0:T(8,128)(2,1)S(1)}, bf16[512,128]{1,0:T(8,128)(2,1)S(1)}, bf16[512,128]{1,0:T(8,128)(2,1)S...) custom-call(s32[2]{0:T(128)S(1)} %copy-done.4, ...), custom_call_target="tpu_custom_call" | custom-call | bytes 7000000 | tf_op jit(solution)/shard_map/gather0/pallas_call | solution.py:346
  49.1 1.7 collective-permute-start
  50.8 4.0 %collective-permute-start.4 = (bf16[512,128]{1,0:T(8,128)(2,1)S(1)}, bf16[512,128]{1,0:T(8,128)(2,1)S(1)}, u32[]{:S(2)}, u32[]{:S(2)}) collective-permute-start(bf16[512,128]{1,0:T(8,128)(2,1)S(1)} %get-tuple-element.73), channel_id=1, source_target_pairs={{0,224},{32,0},{64,32},{96,64},{128,96},{160,128},{192,160},{224,1... | collective-permute-start | bytes 393224 | tf_op jit(solution)/shard_map/ppermute | solution.py:300
  54.8 3.0 %collective-permute-done = bf16[512,128]{1,0:T(8,128)(2,1)S(1)} collective-permute-done((bf16[512,128]{1,0:T(8,128)(2,1)S(1)}, bf16[512,128]{1,0:T(8,128)(2,1)S(1)}, u32[]{:S(2)}, u32[]{:S(2)}) %collective-permute-start) | collective-permute-done | bytes 131104 | tf_op jit(solution)/shard_map/ppermute | solution.py:300
  57.9 0.1 collective-permute-start.1
  58.0 2.7 %collective-permute-start.5 = (bf16[512,128]{1,0:T(8,128)(2,1)S(1)}, bf16[512,128]{1,0:T(8,128)(2,1)S(1)}, u32[]{:S(2)}, u32[]{:S(2)}) collective-permute-start(bf16[512,128]{1,0:T(8,128)(2,1)S(1)} %add_convert_fusion.7), channel_id=1, source_target_pairs={{0,224},{32,0},{64,32},{96,64},{128,96},{160,128},{192,160},{224,1... | collective-permute-start | bytes 393224 | tf_op jit(solution)/shard_map/ppermute | solution.py:300
  60.7 2.5 %collective-permute-done.1 = bf16[512,128]{1,0:T(8,128)(2,1)S(1)} collective-permute-done((bf16[512,128]{1,0:T(8,128)(2,1)S(1)}, bf16[512,128]{1,0:T(8,128)(2,1)S(1)}, u32[]{:S(2)}, u32[]{:S(2)}) %collective-permute-start.1) | collective-permute-done | bytes 131104 | tf_op jit(solution)/shard_map/ppermute | solution.py:300
  63.3 0.1 collective-permute-start.2
  63.4 2.7 %collective-permute-start.6 = (bf16[512,128]{1,0:T(8,128)(2,1)S(1)}, bf16[512,128]{1,0:T(8,128)(2,1)S(1)}, u32[]{:S(2)}, u32[]{:S(2)}) collective-permute-start(bf16[512,128]{1,0:T(8,128)(2,1)S(1)} %add_convert_fusion.6), channel_id=1, source_target_pairs={{0,224},{32,0},{64,32},{96,64},{128,96},{160,128},{192,160},{224,1... | collective-permute-start | bytes 393224 | tf_op jit(solution)/shard_map/ppermute | solution.py:300
  66.2 2.5 %collective-permute-done.2 = bf16[512,128]{1,0:T(8,128)(2,1)S(1)} collective-permute-done((bf16[512,128]{1,0:T(8,128)(2,1)S(1)}, bf16[512,128]{1,0:T(8,128)(2,1)S(1)}, u32[]{:S(2)}, u32[]{:S(2)}) %collective-permute-start.2) | collective-permute-done | bytes 131104 | tf_op jit(solution)/shard_map/ppermute | solution.py:300
  68.7 0.1 collective-permute-start.3
  68.8 5.0 %collective-permute-done.3.refs_3_ = bf16[512,128]{1,0:T(8,128)(2,1)S(1)} collective-permute-done((bf16[512,128]{1,0:T(8,128)(2,1)S(1)}, bf16[512,128]{1,0:T(8,128)(2,1)S(1)}, u32[]{:S(2)}, u32[]{:S(2)}) %collective-permute-start.3) | collective-permute-done | bytes 131104 | tf_op jit(solution)/shard_map/ppermute | solution.py:300
  73.9 1.4 grid0.1.refs_0_
  75.2 1.9 gather1.1
  77.1 0.1 fusion.1
  77.2 0.1 collective-permute-start.7
  77.3 3.3 %collective-permute-start.11 = (bf16[1024,128]{1,0:T(8,128)(2,1)S(1)}, bf16[1024,128]{1,0:T(8,128)(2,1)S(1)}, u32[]{:S(2)}, u32[]{:S(2)}) collective-permute-start(bf16[1024,128]{1,0:T(8,128)(2,1)S(1)} %get-tuple-element.115), channel_id=1, source_target_pairs={{0,224},{32,0},{64,32},{96,64},{128,96},{160,128},{192,160},{224,1... | collective-permute-start | bytes 786440 | tf_op jit(solution)/shard_map/ppermute | solution.py:300
  80.6 3.5 %collective-permute-done.7.refs_1_ = bf16[1024,128]{1,0:T(8,128)(2,1)S(1)} collective-permute-done((bf16[1024,128]{1,0:T(8,128)(2,1)S(1)}, bf16[1024,128]{1,0:T(8,128)(2,1)S(1)}, u32[]{:S(2)}, u32[]{:S(2)}) %collective-permute-start.7) | collective-permute-done | bytes 262176 | tf_op jit(solution)/shard_map/ppermute | solution.py:300
  84.2 0.1 collective-permute-start.8
  84.3 0.1 add_convert_fusion.2
  84.4 3.3 %collective-permute-start.12 = (bf16[1024,128]{1,0:T(8,128)(2,1)S(1)}, bf16[1024,128]{1,0:T(8,128)(2,1)S(1)}, u32[]{:S(2)}, u32[]{:S(2)}) collective-permute-start(bf16[1024,128]{1,0:T(8,128)(2,1)S(1)} %add_convert_fusion.2), channel_id=1, source_target_pairs={{0,224},{32,0},{64,32},{96,64},{128,96},{160,128},{192,160},{224,1... | collective-permute-start | bytes 786440 | tf_op jit(solution)/shard_map/ppermute | solution.py:300
  87.7 3.6 %collective-permute-done.8.refs_2_ = bf16[1024,128]{1,0:T(8,128)(2,1)S(1)} collective-permute-done((bf16[1024,128]{1,0:T(8,128)(2,1)S(1)}, bf16[1024,128]{1,0:T(8,128)(2,1)S(1)}, u32[]{:S(2)}, u32[]{:S(2)}) %collective-permute-start.8) | collective-permute-done | bytes 262176 | tf_op jit(solution)/shard_map/ppermute | solution.py:300
  91.4 0.1 collective-permute-start.9
  91.5 2.8 %collective-permute-start.13 = (bf16[1024,128]{1,0:T(8,128)(2,1)S(1)}, bf16[1024,128]{1,0:T(8,128)(2,1)S(1)}, u32[]{:S(2)}, u32[]{:S(2)}) collective-permute-start(bf16[1024,128]{1,0:T(8,128)(2,1)S(1)} %add_convert_fusion.1), channel_id=1, source_target_pairs={{0,224},{32,0},{64,32},{96,64},{128,96},{160,128},{192,160},{224,1... | collective-permute-start | bytes 786440 | tf_op jit(solution)/shard_map/ppermute | solution.py:300
  94.3 4.6 %collective-permute-done.9.refs_3_ = bf16[1024,128]{1,0:T(8,128)(2,1)S(1)} collective-permute-done((bf16[1024,128]{1,0:T(8,128)(2,1)S(1)}, bf16[1024,128]{1,0:T(8,128)(2,1)S(1)}, u32[]{:S(2)}, u32[]{:S(2)}) %collective-permute-start.9) | collective-permute-done | bytes 262176 | tf_op jit(solution)/shard_map/ppermute | solution.py:300
  99.0 0.1 collective-permute-start.10
  99.1 8.6 %collective-permute-done.10.refs_3_.refs_4_ = bf16[1024,128]{1,0:T(8,128)(2,1)S(1)} collective-permute-done((bf16[1024,128]{1,0:T(8,128)(2,1)S(1)}, bf16[1024,128]{1,0:T(8,128)(2,1)S(1)}, u32[]{:S(2)}, u32[]{:S(2)}) %collective-permute-start.10) | collective-permute-done | bytes 262176 | tf_op jit(solution)/shard_map/ppermute | solution.py:300
  107.7 1.4 grid1.1.refs_0_
  109.1 2.0 spread0.1
  111.1 7.1 %all-to-all-start.2 = ((bf16[8,8,128,128]{3,2,1,0:T(8,128)(2,1)}), bf16[8,8,128,128]{3,2,1,0:T(8,128)(2,1)S(1)}, u32[]{:S(2)}, u32[]{:S(2)}) async-start(bf16[8,8,128,128]{3,2,1,0:T(8,128)(2,1)} %spread0.1), calls=%async_computation.2 | async-start | bytes 4194304 | tf_op jit(solution)/shard_map/all_to_all | solution.py:343
  118.2 2.7 %collective-permute-start.18 = (bf16[512,128]{1,0:T(8,128)(2,1)S(1)}, bf16[512,128]{1,0:T(8,128)(2,1)S(1)}, u32[]{:S(2)}, u32[]{:S(2)}) collective-permute-start(bf16[512,128]{1,0:T(8,128)(2,1)S(1)} %grid1.1.refs_0_), channel_id=1, source_target_pairs={{0,224},{32,0},{64,32},{96,64},{128,96},{160,128},{192,160},{224,1... | collective-permute-start | bytes 393224 | tf_op jit(solution)/shard_map/ppermute | solution.py:300
  120.9 2.4 %collective-permute-done.14.refs_1_ = bf16[512,128]{1,0:T(8,128)(2,1)S(1)} collective-permute-done((bf16[512,128]{1,0:T(8,128)(2,1)S(1)}, bf16[512,128]{1,0:T(8,128)(2,1)S(1)}, u32[]{:S(2)}, u32[]{:S(2)}) %collective-permute-start.14) | collective-permute-done | bytes 131104 | tf_op jit(solution)/shard_map/ppermute | solution.py:300
  123.2 2.7 %collective-permute-start.19 = (bf16[512,128]{1,0:T(8,128)(2,1)S(1)}, bf16[512,128]{1,0:T(8,128)(2,1)S(1)}, u32[]{:S(2)}, u32[]{:S(2)}) collective-permute-start(bf16[512,128]{1,0:T(8,128)(2,1)S(1)} %collective-permute-done.18.refs_7_), channel_id=1, source_target_pairs={{0,224},{32,0},{64,32},{96,64},{128,96},{160,128},{192,160},{224,1... | collective-permute-start | bytes 393224 | tf_op jit(solution)/shard_map/ppermute | solution.py:300
  125.9 2.3 %collective-permute-done.15.refs_2_ = bf16[512,128]{1,0:T(8,128)(2,1)S(1)} collective-permute-done((bf16[512,128]{1,0:T(8,128)(2,1)S(1)}, bf16[512,128]{1,0:T(8,128)(2,1)S(1)}, u32[]{:S(2)}, u32[]{:S(2)}) %collective-permute-start.15) | collective-permute-done | bytes 131104 | tf_op jit(solution)/shard_map/ppermute | solution.py:300
  128.3 2.8 %collective-permute-start.20 = (bf16[512,128]{1,0:T(8,128)(2,1)S(1)}, bf16[512,128]{1,0:T(8,128)(2,1)S(1)}, u32[]{:S(2)}, u32[]{:S(2)}) collective-permute-start(bf16[512,128]{1,0:T(8,128)(2,1)S(1)} %collective-permute-done.19.refs_6_), channel_id=1, source_target_pairs={{0,224},{32,0},{64,32},{96,64},{128,96},{160,128},{192,160},{224,1... | collective-permute-start | bytes 393224 | tf_op jit(solution)/shard_map/ppermute | solution.py:300
  131.1 3.6 %collective-permute-done.16.refs_3_ = bf16[512,128]{1,0:T(8,128)(2,1)S(1)} collective-permute-done((bf16[512,128]{1,0:T(8,128)(2,1)S(1)}, bf16[512,128]{1,0:T(8,128)(2,1)S(1)}, u32[]{:S(2)}, u32[]{:S(2)}) %collective-permute-start.16) | collective-permute-done | bytes 131104 | tf_op jit(solution)/shard_map/ppermute | solution.py:300
  134.6 6.2 %collective-permute-done.17.refs_4_ = bf16[512,128]{1,0:T(8,128)(2,1)S(1)} collective-permute-done((bf16[512,128]{1,0:T(8,128)(2,1)S(1)}, bf16[512,128]{1,0:T(8,128)(2,1)S(1)}, u32[]{:S(2)}, u32[]{:S(2)}) %collective-permute-start.17) | collective-permute-done | bytes 131104 | tf_op jit(solution)/shard_map/ppermute | solution.py:300
  140.8 1.5 spread1.1
  142.3 1.3 copy-done
  143.7 5.4 %all-to-all-start.3 = ((bf16[8,8,128,128]{3,2,1,0:T(8,128)(2,1)}), bf16[8,8,128,128]{3,2,1,0:T(8,128)(2,1)}, u32[]{:S(2)}, u32[]{:S(2)}) async-start(bf16[8,8,128,128]{3,2,1,0:T(8,128)(2,1)} %copy-done), calls=%async_computation.3 | async-start | bytes 4194304 | tf_op jit(solution)/shard_map/all_to_all | solution.py:343
  149.1 4.9 %accum0.1 = (bf16[2048,128]{1,0:T(8,128)(2,1)S(1)}, bf16[2048,128]{1,0:T(8,128)(2,1)}, bf16[2048,128]{1,0:T(8,128)(2,1)}, bf16[2048,128]{1,0:T(8,128)(2,1)S(1)}) custom-call(s32[2]{0:T(128)S(1)} %copy-done.4, s32[64]{0:T(128)S(1)} %copy-done.5, bf16[8,8,128,128]{3,2,1,0:T(8,128)(2,1)S(1)} %all-to-all-done.2.returned, bf16[128,256]{1,0:T(8,128)(2,1)S(1)} %copy-done.3), custom_call_target="tpu_custom_call" | custom-call | bytes 21000000 | tf_op jit(solution)/shard_map/accum0/pallas_call | solution.py:363
  154.0 13.9 %collective-permute-start.21 = (bf16[2048,128]{1,0:T(8,128)(2,1)}, bf16[2048,128]{1,0:T(8,128)(2,1)S(1)}, u32[]{:S(2)}, u32[]{:S(2)}) collective-permute-start(bf16[2048,128]{1,0:T(8,128)(2,1)} %get-tuple-element.105), channel_id=1, source_target_pairs={{0,1},{1,0},{2,3},{3,2},{4,5},{5,4},{6,7},{7,6},{8,9},{9,8},{10,11... | collective-permute-start | bytes 1572872 | tf_op jit(solution)/shard_map/ppermute | solution.py:304
  167.9 2.5 %collective-permute-start.22 = (bf16[2048,128]{1,0:T(8,128)(2,1)}, bf16[2048,128]{1,0:T(8,128)(2,1)S(1)}, u32[]{:S(2)}, u32[]{:S(2)}) collective-permute-start(bf16[2048,128]{1,0:T(8,128)(2,1)} %get-tuple-element.106), channel_id=1, source_target_pairs={{0,2},{1,3},{2,0},{3,1},{4,6},{5,7},{6,4},{7,5},{8,10},{9,11},{10,... | collective-permute-start | bytes 1572872 | tf_op jit(solution)/shard_map/ppermute | solution.py:304
  170.3 0.8 collective-permute-start.23
  171.1 4.5 %accum1.1 = (bf16[2048,128]{1,0:T(8,128)(2,1)S(1)}, bf16[2048,128]{1,0:T(8,128)(2,1)S(1)}, bf16[2048,128]{1,0:T(8,128)(2,1)S(1)}, bf16[2048,128]{1,0:T(8,128)(2,1)S(1)}) custom-call(s32[2]{0:T(128)S(1)} %copy-done.4, s32[64]{0:T(128)S(1)} %copy-done.5, bf16[8,8,128,128]{3,2,1,0:T(8,128)(2,1)} %all-to-all-done.3.returned, bf16[128,256]{1,0:T(8,128)(2,1)S(1)} %copy-done.3), custom_call_target="tpu_custom_call" | custom-call | bytes 21000000 | tf_op jit(solution)/shard_map/accum1/pallas_call | solution.py:363
  175.6 11.6 %collective-permute-start.24 = (bf16[2048,128]{1,0:T(8,128)(2,1)S(1)}, bf16[2048,128]{1,0:T(8,128)(2,1)S(1)}, u32[]{:S(2)}, u32[]{:S(2)}) collective-permute-start(bf16[2048,128]{1,0:T(8,128)(2,1)S(1)} %get-tuple-element.110), channel_id=1, source_target_pairs={{0,1},{1,0},{2,3},{3,2},{4,5},{5,4},{6,7},{7,6},{8,9},{9,8},{10,11... | collective-permute-start | bytes 1572872 | tf_op jit(solution)/shard_map/ppermute | solution.py:304
  187.1 3.2 %collective-permute-start.25 = (bf16[2048,128]{1,0:T(8,128)(2,1)S(1)}, bf16[2048,128]{1,0:T(8,128)(2,1)S(1)}, u32[]{:S(2)}, u32[]{:S(2)}) collective-permute-start(bf16[2048,128]{1,0:T(8,128)(2,1)S(1)} %get-tuple-element.111), channel_id=1, source_target_pairs={{0,2},{1,3},{2,0},{3,1},{4,6},{5,7},{6,4},{7,5},{8,10},{9,11},{10,... | collective-permute-start | bytes 1572872 | tf_op jit(solution)/shard_map/ppermute | solution.py:304
  190.3 0.1 collective-permute-start.26
  190.4 16.1 %collective-permute-done.23.strips_and_out_3_ = bf16[2048,128]{1,0:T(8,128)(2,1)S(1)} collective-permute-done((bf16[2048,128]{1,0:T(8,128)(2,1)S(1)}, bf16[2048,128]{1,0:T(8,128)(2,1)S(1)}, u32[]{:S(2)}, u32[]{:S(2)}) %collective-permute-start.23) | collective-permute-done | bytes 524320 | tf_op jit(solution)/shard_map/ppermute | solution.py:304
  206.5 3.3 %half.1.made = f32[2048,512]{1,0:T(8,128)S(1)} custom-call(s32[2]{0:T(128)S(1)} %copy-done.4, bf16[4,128,512]{2,1,0:T(8,128)(2,1)S(1)} %get-tuple-element.113.maps, bf16[2048,128]{1,0:T(8,128)(2,1)S(1)} %get-tuple-element.104.strips_and_out_0_, bf16[2048,128]{1,0:T(8,128)(2,1)S(1)} %collective-permute-done.21.strips_and_out_1_, ...), custom_call_target="tpu_custom_call" | custom-call | bytes 14000000 | tf_op jit(solution)/shard_map/half/pallas_call | solution.py:440
  209.9 13.0 %collective-permute-done.26.strips_and_out_3_ = bf16[2048,128]{1,0:T(8,128)(2,1)S(1)} collective-permute-done((bf16[2048,128]{1,0:T(8,128)(2,1)S(1)}, bf16[2048,128]{1,0:T(8,128)(2,1)S(1)}, u32[]{:S(2)}, u32[]{:S(2)}) %collective-permute-start.26) | collective-permute-done | bytes 524320 | tf_op jit(solution)/shard_map/ppermute | solution.py:304
  222.9 4.2 %finish.1 = bf16[2,2048,256]{2,1,0:T(8,128)(2,1)} custom-call(s32[2]{0:T(128)S(1)} %copy-done.4, bf16[4,128,512]{2,1,0:T(8,128)(2,1)S(1)} %get-tuple-element.114.maps, f32[2048,512]{1,0:T(8,128)S(1)} %half.1.made, bf16[2048,128]{1,0:T(8,128)(2,1)S(1)} %get-tuple-element.109.strips_and_out_0_, ...), custom_call_target="tpu_custom_call" | custom-call | bytes 14000000 | tf_op jit(solution)/shard_map/finish/pallas_call | solution.py:450
  (57 shorter events, 0.7 us)
Async XLA Ops:
  10.5 6.0 %copy-start.11 = (s32[4,128]{1,0:T(4,128)S(1)}, s32[4,128]{1,0:T(4,128)}, u32[]{:S(2)}) copy-start(s32[4,128]{1,0:T(4,128)} %param.14) | copy-start | bytes 6148
  10.5 32.2 %all-to-all-start = ((bf16[8,8,128,128]{3,2,1,0:T(8,128)(2,1)}), bf16[8,8,128,128]{3,2,1,0:T(8,128)(2,1)}, u32[]{:S(2)}, u32[]{:S(2)}) async-start(bf16[8,8,128,128]{3,2,1,0:T(8,128)(2,1)} %contrib0.1), calls=%async_computation | async-start | bytes 4194304 | tf_op jit(solution)/shard_map/all_to_all | solution.py:343
  16.5 8.8 %copy-start.7 = (f32[32,512]{1,0:T(8,128)S(1)}, f32[32,512]{1,0:T(8,128)}, u32[]{:S(2)}) copy-start(f32[32,512]{1,0:T(8,128)} %constant.46.clone) | copy-start | bytes 196612
  16.5 8.8 %copy-start.8 = (f32[32,512]{1,0:T(8,128)S(1)}, f32[32,512]{1,0:T(8,128)}, u32[]{:S(2)}) copy-start(f32[32,512]{1,0:T(8,128)} %constant.45.clone) | copy-start | bytes 196612
  16.5 8.8 %copy-start.9 = (f32[16,512]{1,0:T(8,128)S(1)}, f32[16,512]{1,0:T(8,128)}, u32[]{:S(2)}) copy-start(f32[16,512]{1,0:T(8,128)} %constant.48.clone) | copy-start | bytes 98308
  16.5 8.8 %copy-start.10 = (f32[16,512]{1,0:T(8,128)S(1)}, f32[16,512]{1,0:T(8,128)}, u32[]{:S(2)}) copy-start(f32[16,512]{1,0:T(8,128)} %constant.47.clone) | copy-start | bytes 98308
  42.7 3.9 %copy-start.12 = (s32[64]{0:T(128)S(1)}, s32[64]{0:T(128)}, u32[]{:S(2)}) copy-start(s32[64]{0:T(128)} %param.13) | copy-start | bytes 772
  42.7 3.9 %copy-start.4 = (s32[2]{0:T(128)S(1)}, s32[2]{0:T(128)}, u32[]{:S(2)}) copy-start(s32[2]{0:T(128)} %pad_add_fusion.refs_0_.place) | copy-start | bytes 28
  42.7 32.5 %all-to-all-start.1 = ((bf16[8,8,128,128]{3,2,1,0:T(8,128)(2,1)}), bf16[8,8,128,128]{3,2,1,0:T(8,128)(2,1)S(1)}, u32[]{:S(2)}, u32[]{:S(2)}) async-start(bf16[8,8,128,128]{3,2,1,0:T(8,128)(2,1)} %contrib1.1), calls=%async_computation.1 | async-start | bytes 4194304 | tf_op jit(solution)/shard_map/all_to_all | solution.py:343
  46.5 27.3 %copy-start.1 = (bf16[1,2,512,128]{3,2,1,0:T(8,128)(2,1)S(1)}, bf16[1,2,512,128]{3,2,1,0:T(8,128)(2,1)}, u32[]{:S(2)}) copy-start(bf16[1,2,512,128]{3,2,1,0:T(8,128)(2,1)} %param.15) | copy-start | bytes 786436
  49.1 8.8 %collective-permute-start = (bf16[512,128]{1,0:T(8,128)(2,1)S(1)}, bf16[512,128]{1,0:T(8,128)(2,1)S(1)}, u32[]{:S(2)}, u32[]{:S(2)}) collective-permute-start(bf16[512,128]{1,0:T(8,128)(2,1)S(1)} %get-tuple-element.69), channel_id=1, source_target_pairs={{0,32},{32,64},{64,96},{96,128},{128,160},{160,192},{192,224},{224... | collective-permute-start | bytes 393224 | tf_op jit(solution)/shard_map/ppermute | solution.py:300
  50.8 7.2 %collective-permute-start.4 = (bf16[512,128]{1,0:T(8,128)(2,1)S(1)}, bf16[512,128]{1,0:T(8,128)(2,1)S(1)}, u32[]{:S(2)}, u32[]{:S(2)}) collective-permute-start(bf16[512,128]{1,0:T(8,128)(2,1)S(1)} %get-tuple-element.73), channel_id=1, source_target_pairs={{0,224},{32,0},{64,32},{96,64},{128,96},{160,128},{192,160},{224,1... | collective-permute-start | bytes 393224 | tf_op jit(solution)/shard_map/ppermute | solution.py:300
  57.9 5.4 %collective-permute-start.1 = (bf16[512,128]{1,0:T(8,128)(2,1)S(1)}, bf16[512,128]{1,0:T(8,128)(2,1)S(1)}, u32[]{:S(2)}, u32[]{:S(2)}) collective-permute-start(bf16[512,128]{1,0:T(8,128)(2,1)S(1)} %add_convert_fusion.10), channel_id=1, source_target_pairs={{0,32},{32,64},{64,96},{96,128},{128,160},{160,192},{192,224},{224... | collective-permute-start | bytes 393224 | tf_op jit(solution)/shard_map/ppermute | solution.py:300
  58.0 5.4 %collective-permute-start.5 = (bf16[512,128]{1,0:T(8,128)(2,1)S(1)}, bf16[512,128]{1,0:T(8,128)(2,1)S(1)}, u32[]{:S(2)}, u32[]{:S(2)}) collective-permute-start(bf16[512,128]{1,0:T(8,128)(2,1)S(1)} %add_convert_fusion.7), channel_id=1, source_target_pairs={{0,224},{32,0},{64,32},{96,64},{128,96},{160,128},{192,160},{224,1... | collective-permute-start | bytes 393224 | tf_op jit(solution)/shard_map/ppermute | solution.py:300
  63.3 5.4 %collective-permute-start.2 = (bf16[512,128]{1,0:T(8,128)(2,1)S(1)}, bf16[512,128]{1,0:T(8,128)(2,1)S(1)}, u32[]{:S(2)}, u32[]{:S(2)}) collective-permute-start(bf16[512,128]{1,0:T(8,128)(2,1)S(1)} %add_convert_fusion.9), channel_id=1, source_target_pairs={{0,32},{32,64},{64,96},{96,128},{128,160},{160,192},{192,224},{224... | collective-permute-start | bytes 393224 | tf_op jit(solution)/shard_map/ppermute | solution.py:300
  63.4 5.4 %collective-permute-start.6 = (bf16[512,128]{1,0:T(8,128)(2,1)S(1)}, bf16[512,128]{1,0:T(8,128)(2,1)S(1)}, u32[]{:S(2)}, u32[]{:S(2)}) collective-permute-start(bf16[512,128]{1,0:T(8,128)(2,1)S(1)} %add_convert_fusion.6), channel_id=1, source_target_pairs={{0,224},{32,0},{64,32},{96,64},{128,96},{160,128},{192,160},{224,1... | collective-permute-start | bytes 393224 | tf_op jit(solution)/shard_map/ppermute | solution.py:300
  68.7 5.1 %collective-permute-start.3 = (bf16[512,128]{1,0:T(8,128)(2,1)S(1)}, bf16[512,128]{1,0:T(8,128)(2,1)S(1)}, u32[]{:S(2)}, u32[]{:S(2)}) collective-permute-start(bf16[512,128]{1,0:T(8,128)(2,1)S(1)} %add_convert_fusion.8), channel_id=1, source_target_pairs={{0,32},{32,64},{64,96},{96,128},{128,160},{160,192},{192,224},{224... | collective-permute-start | bytes 393224 | tf_op jit(solution)/shard_map/ppermute | solution.py:300
  77.2 30.5 %copy-start.2 = (bf16[1,2,512,128]{3,2,1,0:T(8,128)(2,1)S(1)}, bf16[1,2,512,128]{3,2,1,0:T(8,128)(2,1)}, u32[]{:S(2)}) copy-start(bf16[1,2,512,128]{3,2,1,0:T(8,128)(2,1)} %param.15) | copy-start | bytes 786436
  77.2 6.9 %collective-permute-start.7 = (bf16[1024,128]{1,0:T(8,128)(2,1)S(1)}, bf16[1024,128]{1,0:T(8,128)(2,1)S(1)}, u32[]{:S(2)}, u32[]{:S(2)}) collective-permute-start(bf16[1024,128]{1,0:T(8,128)(2,1)S(1)} %get-tuple-element.116), channel_id=1, source_target_pairs={{0,32},{32,64},{64,96},{96,128},{128,160},{160,192},{192,224},{224... | collective-permute-start | bytes 786440 | tf_op jit(solution)/shard_map/ppermute | solution.py:300
  77.3 7.0 %collective-permute-start.11 = (bf16[1024,128]{1,0:T(8,128)(2,1)S(1)}, bf16[1024,128]{1,0:T(8,128)(2,1)S(1)}, u32[]{:S(2)}, u32[]{:S(2)}) collective-permute-start(bf16[1024,128]{1,0:T(8,128)(2,1)S(1)} %get-tuple-element.115), channel_id=1, source_target_pairs={{0,224},{32,0},{64,32},{96,64},{128,96},{160,128},{192,160},{224,1... | collective-permute-start | bytes 786440 | tf_op jit(solution)/shard_map/ppermute | solution.py:300
  84.2 7.1 %collective-permute-start.8 = (bf16[1024,128]{1,0:T(8,128)(2,1)S(1)}, bf16[1024,128]{1,0:T(8,128)(2,1)S(1)}, u32[]{:S(2)}, u32[]{:S(2)}) collective-permute-start(bf16[1024,128]{1,0:T(8,128)(2,1)S(1)} %add_convert_fusion.5), channel_id=1, source_target_pairs={{0,32},{32,64},{64,96},{96,128},{128,160},{160,192},{192,224},{224... | collective-permute-start | bytes 786440 | tf_op jit(solution)/shard_map/ppermute | solution.py:300
  84.4 7.1 %collective-permute-start.12 = (bf16[1024,128]{1,0:T(8,128)(2,1)S(1)}, bf16[1024,128]{1,0:T(8,128)(2,1)S(1)}, u32[]{:S(2)}, u32[]{:S(2)}) collective-permute-start(bf16[1024,128]{1,0:T(8,128)(2,1)S(1)} %add_convert_fusion.2), channel_id=1, source_target_pairs={{0,224},{32,0},{64,32},{96,64},{128,96},{160,128},{192,160},{224,1... | collective-permute-start | bytes 786440 | tf_op jit(solution)/shard_map/ppermute | solution.py:300
  91.4 7.6 %collective-permute-start.9 = (bf16[1024,128]{1,0:T(8,128)(2,1)S(1)}, bf16[1024,128]{1,0:T(8,128)(2,1)S(1)}, u32[]{:S(2)}, u32[]{:S(2)}) collective-permute-start(bf16[1024,128]{1,0:T(8,128)(2,1)S(1)} %add_convert_fusion.4), channel_id=1, source_target_pairs={{0,32},{32,64},{64,96},{96,128},{128,160},{160,192},{192,224},{224... | collective-permute-start | bytes 786440 | tf_op jit(solution)/shard_map/ppermute | solution.py:300
  91.5 7.6 %collective-permute-start.13 = (bf16[1024,128]{1,0:T(8,128)(2,1)S(1)}, bf16[1024,128]{1,0:T(8,128)(2,1)S(1)}, u32[]{:S(2)}, u32[]{:S(2)}) collective-permute-start(bf16[1024,128]{1,0:T(8,128)(2,1)S(1)} %add_convert_fusion.1), channel_id=1, source_target_pairs={{0,224},{32,0},{64,32},{96,64},{128,96},{160,128},{192,160},{224,1... | collective-permute-start | bytes 786440 | tf_op jit(solution)/shard_map/ppermute | solution.py:300
  99.0 8.7 %collective-permute-start.10 = (bf16[1024,128]{1,0:T(8,128)(2,1)S(1)}, bf16[1024,128]{1,0:T(8,128)(2,1)S(1)}, u32[]{:S(2)}, u32[]{:S(2)}) collective-permute-start(bf16[1024,128]{1,0:T(8,128)(2,1)S(1)} %add_convert_fusion.3), channel_id=1, source_target_pairs={{0,32},{32,64},{64,96},{96,128},{128,160},{160,192},{192,224},{224... | collective-permute-start | bytes 786440 | tf_op jit(solution)/shard_map/ppermute | solution.py:300
  111.1 32.6 %all-to-all-start.2 = ((bf16[8,8,128,128]{3,2,1,0:T(8,128)(2,1)}), bf16[8,8,128,128]{3,2,1,0:T(8,128)(2,1)S(1)}, u32[]{:S(2)}, u32[]{:S(2)}) async-start(bf16[8,8,128,128]{3,2,1,0:T(8,128)(2,1)} %spread0.1), calls=%async_computation.2 | async-start | bytes 4194304 | tf_op jit(solution)/shard_map/all_to_all | solution.py:343
  118.2 5.0 %collective-permute-start.14 = (bf16[512,128]{1,0:T(8,128)(2,1)S(1)}, bf16[512,128]{1,0:T(8,128)(2,1)S(1)}, u32[]{:S(2)}, u32[]{:S(2)}) collective-permute-start(bf16[512,128]{1,0:T(8,128)(2,1)S(1)} %grid1.1.refs_0_), channel_id=1, source_target_pairs={{0,32},{32,64},{64,96},{96,128},{128,160},{160,192},{192,224},{224... | collective-permute-start | bytes 393224 | tf_op jit(solution)/shard_map/ppermute | solution.py:300
  118.2 5.0 %collective-permute-start.18 = (bf16[512,128]{1,0:T(8,128)(2,1)S(1)}, bf16[512,128]{1,0:T(8,128)(2,1)S(1)}, u32[]{:S(2)}, u32[]{:S(2)}) collective-permute-start(bf16[512,128]{1,0:T(8,128)(2,1)S(1)} %grid1.1.refs_0_), channel_id=1, source_target_pairs={{0,224},{32,0},{64,32},{96,64},{128,96},{160,128},{192,160},{224,1... | collective-permute-start | bytes 393224 | tf_op jit(solution)/shard_map/ppermute | solution.py:300
  123.2 5.0 %collective-permute-start.15 = (bf16[512,128]{1,0:T(8,128)(2,1)S(1)}, bf16[512,128]{1,0:T(8,128)(2,1)S(1)}, u32[]{:S(2)}, u32[]{:S(2)}) collective-permute-start(bf16[512,128]{1,0:T(8,128)(2,1)S(1)} %collective-permute-done.14.refs_1_), channel_id=1, source_target_pairs={{0,32},{32,64},{64,96},{96,128},{128,160},{160,192},{192,224},{224... | collective-permute-start | bytes 393224 | tf_op jit(solution)/shard_map/ppermute | solution.py:300
  123.2 5.0 %collective-permute-start.19 = (bf16[512,128]{1,0:T(8,128)(2,1)S(1)}, bf16[512,128]{1,0:T(8,128)(2,1)S(1)}, u32[]{:S(2)}, u32[]{:S(2)}) collective-permute-start(bf16[512,128]{1,0:T(8,128)(2,1)S(1)} %collective-permute-done.18.refs_7_), channel_id=1, source_target_pairs={{0,224},{32,0},{64,32},{96,64},{128,96},{160,128},{192,160},{224,1... | collective-permute-start | bytes 393224 | tf_op jit(solution)/shard_map/ppermute | solution.py:300
  128.3 6.4 %collective-permute-start.16 = (bf16[512,128]{1,0:T(8,128)(2,1)S(1)}, bf16[512,128]{1,0:T(8,128)(2,1)S(1)}, u32[]{:S(2)}, u32[]{:S(2)}) collective-permute-start(bf16[512,128]{1,0:T(8,128)(2,1)S(1)} %collective-permute-done.15.refs_2_), channel_id=1, source_target_pairs={{0,32},{32,64},{64,96},{96,128},{128,160},{160,192},{192,224},{224... | collective-permute-start | bytes 393224 | tf_op jit(solution)/shard_map/ppermute | solution.py:300
  128.3 6.4 %collective-permute-start.20 = (bf16[512,128]{1,0:T(8,128)(2,1)S(1)}, bf16[512,128]{1,0:T(8,128)(2,1)S(1)}, u32[]{:S(2)}, u32[]{:S(2)}) collective-permute-start(bf16[512,128]{1,0:T(8,128)(2,1)S(1)} %collective-permute-done.19.refs_6_), channel_id=1, source_target_pairs={{0,224},{32,0},{64,32},{96,64},{128,96},{160,128},{192,160},{224,1... | collective-permute-start | bytes 393224 | tf_op jit(solution)/shard_map/ppermute | solution.py:300
  134.6 6.2 %collective-permute-start.17 = (bf16[512,128]{1,0:T(8,128)(2,1)S(1)}, bf16[512,128]{1,0:T(8,128)(2,1)S(1)}, u32[]{:S(2)}, u32[]{:S(2)}) collective-permute-start(bf16[512,128]{1,0:T(8,128)(2,1)S(1)} %collective-permute-done.16.refs_3_), channel_id=1, source_target_pairs={{0,32},{32,64},{64,96},{96,128},{128,160},{160,192},{192,224},{224... | collective-permute-start | bytes 393224 | tf_op jit(solution)/shard_map/ppermute | solution.py:300
  142.3 1.4 copy-start
  143.7 5.4 %copy-start.3 = (bf16[128,256]{1,0:T(8,128)(2,1)S(1)}, bf16[128,256]{1,0:T(8,128)(2,1)}, u32[]{:S(2)}) copy-start(bf16[128,256]{1,0:T(8,128)(2,1)} %constant.50.clone.table) | copy-start | bytes 196612
  143.7 5.4 %copy-start.5 = (s32[64]{0:T(128)S(1)}, s32[64]{0:T(128)}, u32[]{:S(2)}) copy-start(s32[64]{0:T(128)} %and_bitcast_fusion.refs_1_.starts) | copy-start | bytes 772
  143.7 27.4 %all-to-all-start.3 = ((bf16[8,8,128,128]{3,2,1,0:T(8,128)(2,1)}), bf16[8,8,128,128]{3,2,1,0:T(8,128)(2,1)}, u32[]{:S(2)}, u32[]{:S(2)}) async-start(bf16[8,8,128,128]{3,2,1,0:T(8,128)(2,1)} %copy-done), calls=%async_computation.3 | async-start | bytes 4194304 | tf_op jit(solution)/shard_map/all_to_all | solution.py:343
  154.0 36.3 %collective-permute-start.21 = (bf16[2048,128]{1,0:T(8,128)(2,1)}, bf16[2048,128]{1,0:T(8,128)(2,1)S(1)}, u32[]{:S(2)}, u32[]{:S(2)}) collective-permute-start(bf16[2048,128]{1,0:T(8,128)(2,1)} %get-tuple-element.105), channel_id=1, source_target_pairs={{0,1},{1,0},{2,3},{3,2},{4,5},{5,4},{6,7},{7,6},{8,9},{9,8},{10,11... | collective-permute-start | bytes 1572872 | tf_op jit(solution)/shard_map/ppermute | solution.py:304
  167.9 22.6 %collective-permute-start.22 = (bf16[2048,128]{1,0:T(8,128)(2,1)}, bf16[2048,128]{1,0:T(8,128)(2,1)S(1)}, u32[]{:S(2)}, u32[]{:S(2)}) collective-permute-start(bf16[2048,128]{1,0:T(8,128)(2,1)} %get-tuple-element.106), channel_id=1, source_target_pairs={{0,2},{1,3},{2,0},{3,1},{4,6},{5,7},{6,4},{7,5},{8,10},{9,11},{10,... | collective-permute-start | bytes 1572872 | tf_op jit(solution)/shard_map/ppermute | solution.py:304
  170.3 36.2 %collective-permute-start.23 = (bf16[2048,128]{1,0:T(8,128)(2,1)S(1)}, bf16[2048,128]{1,0:T(8,128)(2,1)S(1)}, u32[]{:S(2)}, u32[]{:S(2)}) collective-permute-start(bf16[2048,128]{1,0:T(8,128)(2,1)S(1)} %get-tuple-element.107), channel_id=1, source_target_pairs={{0,3},{1,2},{2,1},{3,0},{4,7},{5,6},{6,5},{7,4},{8,11},{9,10},{10,... | collective-permute-start | bytes 1572872 | tf_op jit(solution)/shard_map/ppermute | solution.py:304
  171.1 19.3 %copy-start.6 = (bf16[4,2,2,64,512]{4,3,2,0,1:T(8,128)(2,1)S(1)}, bf16[4,2,2,64,512]{4,3,2,0,1:T(8,128)(2,1)}, u32[]{:S(2)}) copy-start(bf16[4,2,2,64,512]{4,3,2,0,1:T(8,128)(2,1)} %maximum_maximum_fusion) | copy-start | bytes 3145732
  175.6 34.3 %collective-permute-start.24 = (bf16[2048,128]{1,0:T(8,128)(2,1)S(1)}, bf16[2048,128]{1,0:T(8,128)(2,1)S(1)}, u32[]{:S(2)}, u32[]{:S(2)}) collective-permute-start(bf16[2048,128]{1,0:T(8,128)(2,1)S(1)} %get-tuple-element.110), channel_id=1, source_target_pairs={{0,1},{1,0},{2,3},{3,2},{4,5},{5,4},{6,7},{7,6},{8,9},{9,8},{10,11... | collective-permute-start | bytes 1572872 | tf_op jit(solution)/shard_map/ppermute | solution.py:304
  187.1 22.8 %collective-permute-start.25 = (bf16[2048,128]{1,0:T(8,128)(2,1)S(1)}, bf16[2048,128]{1,0:T(8,128)(2,1)S(1)}, u32[]{:S(2)}, u32[]{:S(2)}) collective-permute-start(bf16[2048,128]{1,0:T(8,128)(2,1)S(1)} %get-tuple-element.111), channel_id=1, source_target_pairs={{0,2},{1,3},{2,0},{3,1},{4,6},{5,7},{6,4},{7,5},{8,10},{9,11},{10,... | collective-permute-start | bytes 1572872 | tf_op jit(solution)/shard_map/ppermute | solution.py:304
  190.3 32.6 %collective-permute-start.26 = (bf16[2048,128]{1,0:T(8,128)(2,1)S(1)}, bf16[2048,128]{1,0:T(8,128)(2,1)S(1)}, u32[]{:S(2)}, u32[]{:S(2)}) collective-permute-start(bf16[2048,128]{1,0:T(8,128)(2,1)S(1)} %get-tuple-element.112), channel_id=1, source_target_pairs={{0,3},{1,2},{2,1},{3,0},{4,7},{5,6},{6,5},{7,4},{8,11},{9,10},{10,... | collective-permute-start | bytes 1572872 | tf_op jit(solution)/shard_map/ppermute | solution.py:304

commit v2 on v1

--- a/solution.py
+++ b/solution.py
@@ -15,8 +15,9 @@
 HALF = LANES // 2
 BF16 = jnp.bfloat16
 F32 = jnp.float32
-FACET = ("z", "xl", "y")
-NEAR = ("xl", "y")
+FACET = ("zq", "zp", "xl", "y")
+NEAR = (("zp", "xl", "y"), ("xl", "y"))
+FAR = (("zq",), ("zq", "zp"))
 
 
 def side_by_side(real_part, imag_part):
@@ -89,7 +90,11 @@
     return jnp.concatenate([tops, lows], axis=0).astype(BF16)
 
 
-def contrib_kernel(chunk, place, starts, strip, table, out, held, source, made_rows, in_sems, out_sems):
+def window_rows(first_rows, item, length):
+    return pl.ds(jnp.bitwise_and(first_rows[item], length - 1), XM)
+
+
+def contrib_kernel(chunk, starts, strip, table, out, held, source, made_rows, in_sems, out_sems):
     facet_len = strip.shape[1]
     parts = in_sems.shape[0]
     share = facet_len // parts
@@ -117,10 +122,9 @@
         return pltpu.make_async_copy(made_rows.at[:, k], out.at[:, k], out_sems.at[k])
 
     def one_group(k, _):
-        item = lax.rem(place[0] + k, depth) * planes
         for j in range(0, planes, 2):
-            first = source[pl.ds(starts[item + j], XM), :]
-            second = source[pl.ds(starts[item + j + 1], XM), :]
+            first = source[window_rows(starts, k * planes + j, facet_len), :]
+            second = source[window_rows(starts, k * planes + j + 1, facet_len), :]
             made = jnp.dot(table[...], stack_turned([first, second]), preferred_element_type=F32)
             made_rows[j, k] = made[:, :LANES].astype(BF16)
             made_rows[j + 1, k] = made[:, LANES:].astype(BF16)
@@ -134,26 +138,27 @@
 
 def gather_kernel(chunk, place, offsets, arrived, *refs):
     *outs, held, total, sems = refs
-    planes = arrived.shape[0]
+    planes, depth = arrived.shape[0], arrived.shape[1]
     grid_len = total.shape[0] - XM
-    base = chunk * grid_len
-
-    def fetch(k):
-        return pltpu.make_async_copy(arrived.at[:, k], held.at[:, k], sems.at[k])
-
-    for k in range(len(outs)):
-        fetch(k).start()
-    for k, out in enumerate(outs):
+    owners = [lax.rem(place[chunk] + k * (1 if chunk == 0 else place[3]), depth) for k in range(depth)]
+
+    def fetch(owner):
+        return pltpu.make_async_copy(arrived.at[:, owner], held.at[:, owner], sems.at[owner])
+
+    for owner in owners:
+        fetch(owner).start()
+    for owner, out in zip(owners, outs):
         total[...] = jnp.zeros_like(total)
-        fetch(k).wait()
-
-        def one_facet(j, _, k=k):
-            rows = pl.ds(offsets[place[0] * planes + j], XM)
-            total[rows, :] = total[rows, :] + held[j, k].astype(F32)
+        fetch(owner).wait()
+
+        def one_facet(j, _, owner=owner):
+            rows = window_rows(offsets, place[chunk] * planes + j, grid_len)
+            total[rows, :] = total[rows, :] + held[j, owner].astype(F32)
             return 0
 
         lax.fori_loop(0, planes, one_facet, 0, unroll=2)
         total[pl.ds(0, XM), :] = total[pl.ds(0, XM), :] + total[pl.ds(grid_len, XM), :]
+        base = out.shape[0] - grid_len
         out[pl.ds(base, grid_len), :] = total[pl.ds(0, grid_len), :].astype(BF16)
         if base > 0:
             out[pl.ds(0, base), :] = jnp.zeros((base, LANES), BF16)
@@ -162,10 +167,9 @@
 def grid_kernel(chunk, weights, table, *refs):
     *parts, out = refs
     grid_len = weights.shape[1]
-    rows = pl.ds(chunk * grid_len, grid_len)
-    total = parts[0][rows, :].astype(F32)
-    for part in parts[1:]:
-        total = total + part[rows, :].astype(F32)
+    total = 0.0
+    for part in parts:
+        total = total + part[pl.ds(part.shape[0] - grid_len, grid_len), :].astype(F32)
     assembled = total.astype(BF16).astype(F32)
     spectrum = jnp.dot(table[...], stack_turned([assembled]), preferred_element_type=F32)
     weight_re = weights[0].astype(F32)
@@ -175,9 +179,7 @@
     weighted = (both_re * spectrum + both_im * turn(spectrum)).astype(BF16).astype(F32)
     back = jnp.concatenate([weighted, -turn(weighted)], axis=0).astype(BF16)
     image = jnp.dot(table[...], back, preferred_element_type=F32)
-    out[pl.ds(0, grid_len), :] = (image * 4.0).astype(BF16)
-    if chunk == 0:
-        out[pl.ds(grid_len, grid_len), :] = jnp.zeros((grid_len, LANES), BF16)
+    out[...] = (image * 4.0).astype(BF16)
 
 
 def spread_kernel(place, offsets, *refs):
@@ -193,7 +195,7 @@
         wide[pl.ds(grid_len, XM), :] = wide[pl.ds(0, XM), :]
 
         def one_facet(j, _, k=k):
-            rows = pl.ds(offsets[place[0] * planes + j], XM)
+            rows = window_rows(offsets, place[1] * planes + j, grid_len)
             made_rows[j, k] = wide[rows, :].astype(BF16)
             return 0
 
@@ -218,12 +220,12 @@
 
     def one_group(k, _):
         fetch(k).wait()
-        item = lax.rem(place[0] + depth - k, depth) * planes
+        item = lax.rem(place[1] + k * (depth - place[3]), depth) * planes
         for j in range(0, planes, 2):
             blocks = [held[j, k].astype(F32), held[j + 1, k].astype(F32)]
             made = jnp.dot(table[...], stack_turned(blocks), preferred_element_type=F32)
             for n in range(2):
-                rows = pl.ds(starts[item + j + n], XM)
+                rows = window_rows(starts, item + j + n, facet_len)
                 total[rows, :] = total[rows, :] + made[:, n * LANES : (n + 1) * LANES]
         return 0
 
@@ -231,7 +233,7 @@
     total[pl.ds(0, XM), :] = total[pl.ds(0, XM), :] + total[pl.ds(facet_len, XM), :]
     tile = 256
     for k, out in enumerate(outs):
-        first = jnp.bitwise_xor(place[1], k) * own_rows
+        first = jnp.bitwise_xor(place[2], k) * own_rows
 
         def drain(i, _, out=out, first=first):
             rows = pl.ds(pl.multiple_of(first + i * tile, tile), tile)
@@ -241,25 +243,24 @@
         lax.fori_loop(0, own_rows // tile, drain, 0)
 
 
-def window(place, strips, maps):
+def window(place, terms, maps):
     made = None
-    for k, strip in enumerate(strips):
-        term = jnp.dot(
-            strip[...], maps[jnp.bitwise_xor(place[1], k)], preferred_element_type=F32
-        )
+    for chunk, k, strip in terms:
+        table = maps[chunk, jnp.bitwise_xor(place[2], k)]
+        term = jnp.dot(strip[...], table, preferred_element_type=F32)
         made = term if made is None else made + term
     return made
 
 
-def half_kernel(place, maps, *strips_and_out):
+def half_kernel(keys, place, maps, *strips_and_out):
     *strips, out = strips_and_out
-    out[...] = window(place, strips, maps)
-
-
-def finish_kernel(place, maps, made, *strips_and_out):
+    out[...] = window(place, [(*key, s) for key, s in zip(keys, strips)], maps)
+
+
+def finish_kernel(keys, place, maps, made, *strips_and_out):
     *strips, out = strips_and_out
     out_cols = out.shape[2]
-    both = made[...] + window(place, strips, maps)
+    both = made[...] + window(place, [(*key, s) for key, s in zip(keys, strips)], maps)
     out[0] = both[:, :out_cols].astype(BF16)
     out[1] = both[:, out_cols:].astype(BF16)
 
@@ -296,8 +297,18 @@
 
 
 def shifted(value, step):
-    size = lax.axis_size("z")
-    return lax.ppermute(value, "z", [(i, (i + step) % size) for i in range(size)])
+    size = lax.axis_size("zq")
+    return lax.ppermute(value, "zq", [(i, (i + step) % size) for i in range(size)])
+
+
+def turned(value, step):
+    size, cols = lax.axis_size(FAR[1]), lax.axis_size("col")
+    perm = [
+        (i * cols + c, (i + (step if c % 2 == 0 else -step)) % size * cols + c)
+        for i in range(size)
+        for c in range(cols)
+    ]
+    return lax.ppermute(value, (*FAR[1], "col"), perm)
 
 
 def swapped(value, flip):
@@ -309,8 +320,6 @@
 
 
 def body(prepared, sub_off, fac_off, win_col, vis_weights):
-    depth = lax.axis_size("z")
-    planes = lax.axis_size(NEAR)
     facet_count = fac_off.shape[0]
     strip = prepared[0]
     weights = vis_weights[0]
@@ -319,151 +328,143 @@
     col_count = lax.axis_size("col")
     own_rows = facet_len // col_count
     out_cols = LANES * col_count // 2
-    place = jnp.stack([lax.axis_index("z"), lax.axis_index("col")]).astype(jnp.int32)
-    starts = jnp.bitwise_and(sub_off[:, 0], facet_len - 1)
-    offsets = jnp.bitwise_and(fac_off, grid_len - 1)
+    place = [lax.axis_index(FAR[0]), lax.axis_index(FAR[1]), lax.axis_index("col")]
+    size = lax.axis_size(FAR[1])
+    place.append(jnp.where(place[2] % 2 == 0, 1, size - 1))
+    place = jnp.stack(place).astype(jnp.int32)
+    starts = sub_off.reshape(-1)
     forward_small, backward_small = small_tables()
     grid_forward = grid_table(grid_len, facet_count)
-    blocks = (planes, depth, XM, LANES)
     flips = sorted(range(1, col_count), reverse=True)
-
     long_rows = pltpu.VMEM((facet_len + XM, LANES), F32)
     grid_rows = pltpu.VMEM((grid_len + XM, LANES), F32)
-    all_blocks = pltpu.VMEM(blocks, BF16)
-    sems = pltpu.SemaphoreType.DMA((depth,))
+    planes = [lax.axis_size(axes) for axes in NEAR]
+    depths = [lax.axis_size(axes) for axes in FAR]
+    blocks = [(p, d, XM, LANES) for p, d in zip(planes, depths)]
+    held = [pltpu.VMEM(b, BF16) for b in blocks]
+    sems = [pltpu.SemaphoreType.DMA((d,)) for d in depths]
 
     def contrib(c, strip):
         return call(
-            bind(contrib_kernel, c), f"contrib{c}", [blocks], [SMEM, SMEM, HBM, VMEM],
-            [pltpu.VMEM(strip.shape, BF16), long_rows, all_blocks, pltpu.SemaphoreType.DMA((8,)), sems],
-            6.5, 63, HBM,
-        )(place, starts, strip, forward_small)
-
-    def near(value):
-        return lax.all_to_all(value, NEAR, 0, 0, tiled=True)
-
-    def gather(c, arrived):
+            bind(contrib_kernel, c), f"contrib{c}", [blocks[c]], [SMEM, HBM, VMEM],
+            [pltpu.VMEM(strip.shape, BF16), long_rows, held[c], pltpu.SemaphoreType.DMA((8,)), sems[c]],
+            8, 63, HBM,
+        )(starts, strip, forward_small)
+
+    def near(c, value):
+        return lax.all_to_all(value, NEAR[c], 0, 0, tiled=True)
+
+    def gather(c, arrived, doubled):
+        outs = [(grid_len * (1 + (k in doubled)), LANES) for k in range(depths[c])]
         return call(
-            bind(gather_kernel, c), f"gather{c}", [(grid_len * (1 + c), LANES)] * depth, [SMEM, SMEM, HBM],
-            [all_blocks, grid_rows, sems], 2, 8,
-        )(place, offsets, arrived)
+            bind(gather_kernel, c), f"gather{c}", outs,
+            [SMEM, SMEM, HBM], [held[c], grid_rows, sems[c]], 2, 8,
+        )(place, fac_off, arrived)
 
     def image_of(c, parts):
         return call(
-            bind(grid_kernel, c), f"grid{c}", [(grid_len * (2 - c), LANES)], [VMEM] * (2 + len(parts)), [], 1.5, 12
+            bind(grid_kernel, c), f"grid{c}", [(grid_len, LANES)], [VMEM] * (2 + len(parts)),
+            [], 1.5, 12,
         )(weights, grid_forward, *parts)
 
     def spread(c, images):
         return call(
-            spread_kernel, f"spread{c}", [blocks], [SMEM, SMEM] + [VMEM] * depth,
-            [grid_rows, all_blocks, sems], 2, 8, HBM,
-        )(place, offsets, *images)
+            spread_kernel, f"spread{c}", [blocks[1]], [SMEM, SMEM] + [VMEM] * depths[1],
+            [grid_rows, held[1], sems[1]], 2, 8, HBM,
+        )(place, fac_off, *images)
 
     def accum(c, returned):
         return call(
             accum_kernel, f"accum{c}", [(own_rows, LANES)] * col_count,
-            [SMEM, SMEM, HBM, VMEM], [all_blocks, long_rows, sems], 6, 14,
+            [SMEM, SMEM, HBM, VMEM], [held[1], long_rows, sems[1]], 5, 14,
         )(place, starts, returned, backward_small)
 
     def exchange(summed):
         moved = {k: swapped(summed[k], k) for k in flips}
         return [summed[0]] + [moved[k] for k in range(1, col_count)]
-
-    far, near_side = depth // 2, (depth - 1) // 2
-
-    def reduce_step(parts, state, i):
-        up, down = state
-        up = shifted(up, 1)
-        if i < far - 1:
-            up = add(up, parts[far - 1 - i])
-        if i < near_side:
-            down = shifted(down, -1)
-            if i < near_side - 1:
-                down = add(down, parts[far + 2 + i])
-        return up, down
-
-    def share_step(state, i):
-        up, down = state
-        up = up + [shifted(up[-1], 1)]
-        if i < near_side:
-            down = down + [shifted(down[-1], -1)]
-        return up, down
-
-    def shared(state):
-        up, down = state
-        return up + down[:0:-1]
 
     barrier = lax.optimization_barrier
     maps = finish_maps(win_col, out_cols)
     payload0 = contrib(0, strip)
     payload0, strip = barrier((payload0, strip))
-    arrived0 = near(payload0)
+    arrived0 = near(0, payload0)
     payload1 = contrib(1, strip)
     arrived0, payload1, maps, grid_forward = barrier((arrived0, payload1, maps, grid_forward))
-    arrived1 = near(payload1)
-    parts0 = gather(0, arrived0)
-    reduced0 = parts0[far], parts0[far + 1]
+    arrived1 = near(1, payload1)
+
+    steps = sorted(range(1, depths[0]), key=lambda k: -min(k, depths[0] - k))
+    parts0 = gather(0, arrived0, ())
+    image0 = image_of(0, [parts0[0]] + [shifted(parts0[k], k) for k in steps])
+
+    far, near_side = depths[1] // 2, (depths[1] - 1) // 2
+    doubled = [*range(2, far), *range(far + 2, depths[1] - 1)]
+    parts1 = gather(1, arrived1, doubled)
+    ups, downs = [turned(image0, 1)], [turned(image0, -1)]
+    up = jnp.concatenate([ups[0], parts1[far]])
+    down = jnp.concatenate([downs[0], parts1[far + 1]])
+    for i in range(far - 1):
+        up = turned(up, 1)
+        ups.append(up)
+        if i < far - 2:
+            up = add(up, parts1[far - 1 - i])
+    for i in range(near_side - 1):
+        down = turned(down, -1)
+        downs.append(down)
+        if i < near_side - 2:
+            down = add(down, parts1[far + 2 + i])
+    up = turned(add(up[grid_len:], parts1[1]), 1)
+    down = turned(add(down[grid_len:], parts1[depths[1] - 1]), -1)
+    images0 = [image0] + ups + downs[::-1]
+    image1 = image_of(1, [parts1[0], up, down])
+    images0[0], image1 = barrier((image0, image1))
+    returned0 = near(1, spread(0, images0))
+
+    ups, downs = [image1], [image1]
     for i in range(far):
-        reduced0 = reduce_step(parts0, reduced0, i)
-    image0 = image_of(0, [parts0[0], *reduced0])
-    parts1 = gather(1, arrived1)
-    image0, parts1 = barrier((image0, parts1))
-    up, down = add(image0, parts1[far]), add(image0, parts1[far + 1])
-    ups, downs = [], []
-    for i in range(far):
-        up = shifted(up, 1)
-        ups.append(up)
+        ups.append(turned(ups[-1], 1))
         if i < near_side:
-            down = shifted(down, -1)
-            downs.append(down)
-        if i < far - 1:
-            up = add(up, parts1[far - 1 - i])
-        if i < near_side - 1:
-            down = add(down, parts1[far + 2 + i])
-    image1 = image_of(1, [parts1[0], up, down])
-    images0 = [image0] + ups + downs[::-1]
-    image1, images0 = barrier((image1, images0))
-    returned0 = near(spread(0, images0))
-    share1 = [image1], [image1]
-    for i in range(far):
-        share1 = share_step(share1, i)
-    spread1 = spread(1, shared(share1))
+            downs.append(turned(downs[-1], -1))
+    spread1 = spread(1, ups + downs[:0:-1])
     returned0, spread1 = barrier((returned0, spread1))
-    returned1 = near(spread1)
-    strips0 = exchange(accum(0, returned0))
+    returned1 = near(1, spread1)
+    accum0 = accum(0, returned0)
+    strips0 = exchange(accum0)
     strips1 = exchange(accum(1, returned1))
 
     tile = min(512, own_rows)
     strip_spec = pl.BlockSpec((tile, LANES), lambda i: (i, 0))
-    maps_spec = pl.BlockSpec(maps.shape[1:], lambda i: (0, 0, 0))
+    maps_spec = pl.BlockSpec(maps.shape, lambda i: (0, 0, 0, 0))
     wide_spec = pl.BlockSpec((tile, 2 * out_cols), lambda i: (i, 0))
+    late = [(1, k) for k in range(2, col_count)]
+    early = [(0, k) for k in range(col_count)] + [(1, 0), (1, 1)]
+    strips = (strips0, strips1)
     half = pl.pallas_call(
-        half_kernel,
+        bind(half_kernel, early),
         name="half",
         grid=(own_rows // tile,),
         out_shape=jax.ShapeDtypeStruct((own_rows, 2 * out_cols), F32),
-        in_specs=[SMEM, maps_spec] + [strip_spec] * col_count,
+        in_specs=[SMEM, maps_spec] + [strip_spec] * len(early),
         out_specs=wide_spec,
         compiler_params=pltpu.CompilerParams(vmem_limit_bytes=16 << 20),
         cost_estimate=cost(4),
-    )(place, maps[0], *strips0)
+    )(place, maps, *[strips[c][k] for c, k in early])
     result = pl.pallas_call(
-        finish_kernel,
+        bind(finish_kernel, late),
         name="finish",
         grid=(own_rows // tile,),
         out_shape=jax.ShapeDtypeStruct((2, own_rows, out_cols), BF16),
-        in_specs=[SMEM, maps_spec, wide_spec] + [strip_spec] * col_count,
+        in_specs=[SMEM, maps_spec, wide_spec] + [strip_spec] * len(late),
         out_specs=pl.BlockSpec((2, tile, out_cols), lambda i: (0, i, 0)),
         compiler_params=pltpu.CompilerParams(vmem_limit_bytes=16 << 20),
         cost_estimate=cost(4),
-    )(place, maps[1], half, *strips1)
+    )(place, maps, half, *[strips[c][k] for c, k in late])
     return result[None]
 
 
 def solution(mesh):
     facets, cols = mesh.devices.shape
     fine = Mesh(
-        mesh.devices.reshape(facets // 8, 2, 4, cols), ("z", "xl", "y", "col")
+        mesh.devices.reshape(facets // 16, 2, 2, 4, cols), ("zq", "zp", "xl", "y", "col")
     )
     in_specs = (
         P(FACET, None, None, "col"),

time: 228 us -> 224 us (0.982)
  waiting for transfers between devices: 90.1 us -> 82.7 us
  starting transfers between devices: 83.6 us -> 88.2 us
  other arithmetic: 6.56 us -> 3.53 us
    ppermute x21 -> x19, waiting for transfers between devices: 47.8 us -> 36.5 us  [the longest x16 27.5 us: turned(): return lax.ppermute(value, (*FAR[1], 'col'), perm)]
    ppermute x21 -> x19, starting transfers between devices: 29.3 us -> 38.2 us  [the longest x16 28.5 us: turned(): return lax.ppermute(value, (*FAR[1], 'col'), perm)]
    all_to_all x4, waiting for transfers between devices: 13.2 us -> 18.7 us  [near(): return lax.all_to_all(value, NEAR[c], 0, 0, tiled=True)]
    ppermute x6, starting transfers between devices: 31.9 us -> 29.2 us  [swapped(): lax.ppermute(value, 'col', [(i, i ^ flip) for i in range(lax.axis_size('c...]
  transfers between devices with their start and end apart: 31 -> 29, of which waited for: 15 -> 17; matrix products, arithmetic and copies ran while one was open for 2% -> 2% of each run, Pallas kernels for 12% -> 14%
where the time goes in v2:
time: 224 us; the launch traced here: 223 us
  starting transfers between devices  88.2 us (39%)
  waiting for transfers between devices  82.7 us (37%)
  Pallas kernels  44.7 us (20%)
  local copies, waits for them, and re-layouts  3.58 us (2%)
  other arithmetic  3.53 us (2%)
    ppermute x6, starting transfers between devices, swapped(): lax.ppermute(value, 'col', [(i, i ^ flip) for i in range(lax.axis_size('c...  29.2 us
    ppermute x16, starting transfers between devices, turned(): return lax.ppermute(value, (*FAR[1], 'col'), perm)  28.5 us
    ppermute x16, waiting for transfers between devices, turned(): return lax.ppermute(value, (*FAR[1], 'col'), perm)  27.5 us
    ppermute x6, waiting for transfers between devices, swapped(): lax.ppermute(value, 'col', [(i, i ^ flip) for i in range(lax.axis_size('c...  27.4 us
    all_to_all x4, starting transfers between devices, near(): return lax.all_to_all(value, NEAR[c], 0, 0, tiled=True)  20.8 us
    all_to_all x4, waiting for transfers between devices, near(): return lax.all_to_all(value, NEAR[c], 0, 0, tiled=True)  18.7 us
    pallas_call x2, Pallas kernels, contrib(): call(bind(contrib_kernel, c), f'contrib{c}', [blocks[c]], [SMEM, HBM, VME...  16.6 us
    ppermute x3, starting transfers between devices, shifted(): lax.ppermute(value, 'zq', [(i, (i + step) % size) for i in range(size)])  9.68 us
  transfers between devices with their start and end apart: 29, of which 17 were waited for; matrix products, arithmetic and copies ran while one was open for 2% of the time, Pallas kernels for 14%

profile of v2, /device:TPU:1, one launch (start us, length us, event | category | flops | bytes accessed | tf_op | source)
XLA Modules:
  0.0 223.0 jit_solution(1276503691027981593)
XLA Ops:
  0.0 7.9 %contrib0.1 = bf16[16,4,128,128]{3,2,1,0:T(8,128)(2,1)} custom-call(s32[64]{0:T(128)} %bitcast.25, bf16[2,8192,128]{2,1,0:T(8,128)(2,1)} %bitcast.29, bf16[128,256]{1,0:T(8,128)(2,1)} %constant.65.clone.refs_2_), custom_call_target="tpu_custom_call" | custom-call | bytes 28000000 | tf_op jit(solution)/shard_map/contrib0/pallas_call | solution.py:348
  7.9 7.5 %all-to-all-start = ((bf16[16,4,128,128]{3,2,1,0:T(8,128)(2,1)}), bf16[16,4,128,128]{3,2,1,0:T(8,128)(2,1)}, u32[]{:S(2)}, u32[]{:S(2)}) async-start(bf16[16,4,128,128]{3,2,1,0:T(8,128)(2,1)} %contrib0.1), calls=%async_computation | async-start | bytes 4194304 | tf_op jit(solution)/shard_map/all_to_all | solution.py:355
  15.4 0.1 mul.146
  15.5 8.7 %contrib1.1 = bf16[8,8,128,128]{3,2,1,0:T(8,128)(2,1)} custom-call(s32[64]{0:T(128)} %bitcast.26, bf16[2,8192,128]{2,1,0:T(8,128)(2,1)} %bitcast.30, bf16[128,256]{1,0:T(8,128)(2,1)} %constant.65.clone.refs_2_), custom_call_target="tpu_custom_call" | custom-call | bytes 28000000 | tf_op jit(solution)/shard_map/contrib1/pallas_call | solution.py:348
  24.2 0.4 subtract_convert_fusion
  24.6 0.1 pad_maximum_fusion.refs_1_
  24.7 2.6 %fusion.7 = (bf16[4,2,1,64,256]{4,3,2,0,1:T(8,128)(2,1)S(1)}, bf16[4,2,1,64,256]{4,3,2,0,1:T(8,128)(2,1)S(1)}, bf16[4,2,1,64,256]{4,3,2,0,1:T(8,128)(2,1)S(1)}) fusion(s32[4,2,64]{2,0,1:T(4,128)S(1)} %copy.12), kind=kLoop, calls=%fused_computation.20 | loop fusion | flops 2621440 | bytes 788480 | tf_op jit(solution)/shard_map/concatenate | solution.py:64
  27.3 0.1 maximum_maximum_fusion
  27.4 15.0 %all-to-all-done.refs_2_ = bf16[16,4,128,128]{3,2,1,0:T(8,128)(2,1)} async-done(((bf16[16,4,128,128]{3,2,1,0:T(8,128)(2,1)}), bf16[16,4,128,128]{3,2,1,0:T(8,128)(2,1)}, u32[]{:S(2)}, u32[]{:S(2)}) %all-to-all-start) | async-done | bytes 2097184 | tf_op jit(solution)/shard_map/all_to_all | solution.py:355
  42.4 4.5 %all-to-all-start.1 = ((bf16[8,8,128,128]{3,2,1,0:T(8,128)(2,1)}), bf16[8,8,128,128]{3,2,1,0:T(8,128)(2,1)}, u32[]{:S(2)}, u32[]{:S(2)}) async-start(bf16[8,8,128,128]{3,2,1,0:T(8,128)(2,1)} %contrib1.1), calls=%async_computation.1 | async-start | bytes 4194304 | tf_op jit(solution)/shard_map/all_to_all | solution.py:355
  47.0 0.1 pad_add_fusion.refs_0_.place
  47.1 2.4 %gather0.1 = (bf16[512,128]{1,0:T(8,128)(2,1)S(1)}, bf16[512,128]{1,0:T(8,128)(2,1)S(1)}, bf16[512,128]{1,0:T(8,128)(2,1)S(1)}, bf16[512,128]{1,0:T(8,128)(2,1)S(1)}) custom-call(s32[4]{0:T(128)S(1)} %pad_add_fusion.refs_0_.place, s32[64]{0:T(128)S(1)} %copy-done.6, bf16[16,4,128,128]{3,2,1,0:T(8,128)(2,1)} %all-to-all-done.refs_2_), custom_call_target="tpu_custom_call" | custom-call | bytes 7000000 | tf_op jit(solution)/shard_map/gather0/pallas_call | solution.py:359
  49.5 6.1 %collective-permute-start = (bf16[512,128]{1,0:T(8,128)(2,1)S(1)}, bf16[512,128]{1,0:T(8,128)(2,1)S(1)}, u32[]{:S(2)}, u32[]{:S(2)}) collective-permute-start(bf16[512,128]{1,0:T(8,128)(2,1)S(1)} %get-tuple-element.49), channel_id=1, source_target_pairs={{0,128},{64,192},{128,0},{192,64},{1,129},{65,193},{129,1},{193,65... | collective-permute-start | bytes 393224 | tf_op jit(solution)/shard_map/ppermute | solution.py:301
  55.6 1.2 collective-permute-start.1
  56.8 2.4 %collective-permute-start.2 = (bf16[512,128]{1,0:T(8,128)(2,1)S(1)}, bf16[512,128]{1,0:T(8,128)(2,1)S(1)}, u32[]{:S(2)}, u32[]{:S(2)}) collective-permute-start(bf16[512,128]{1,0:T(8,128)(2,1)S(1)} %get-tuple-element.51), channel_id=1, source_target_pairs={{0,192},{64,0},{128,64},{192,128},{1,193},{65,1},{129,65},{193,129... | collective-permute-start | bytes 393224 | tf_op jit(solution)/shard_map/ppermute | solution.py:301
  59.2 6.2 %collective-permute-done.1.refs_4_ = bf16[512,128]{1,0:T(8,128)(2,1)S(1)} collective-permute-done((bf16[512,128]{1,0:T(8,128)(2,1)S(1)}, bf16[512,128]{1,0:T(8,128)(2,1)S(1)}, u32[]{:S(2)}, u32[]{:S(2)}) %collective-permute-start.1) | collective-permute-done | bytes 131104 | tf_op jit(solution)/shard_map/ppermute | solution.py:301
  65.3 2.9 %collective-permute-done.2.refs_5_ = bf16[512,128]{1,0:T(8,128)(2,1)S(1)} collective-permute-done((bf16[512,128]{1,0:T(8,128)(2,1)S(1)}, bf16[512,128]{1,0:T(8,128)(2,1)S(1)}, u32[]{:S(2)}, u32[]{:S(2)}) %collective-permute-start.2) | collective-permute-done | bytes 131104 | tf_op jit(solution)/shard_map/ppermute | solution.py:301
  68.2 1.4 grid0.1.refs_0_
  69.6 0.1 collective-permute-start.3
  69.7 3.4 %all-to-all-done.1.refs_2_ = bf16[8,8,128,128]{3,2,1,0:T(8,128)(2,1)} async-done(((bf16[8,8,128,128]{3,2,1,0:T(8,128)(2,1)}), bf16[8,8,128,128]{3,2,1,0:T(8,128)(2,1)}, u32[]{:S(2)}, u32[]{:S(2)}) %all-to-all-start.1) | async-done | bytes 2097184 | tf_op jit(solution)/shard_map/all_to_all | solution.py:355
  73.1 2.6 %gather1.1 = (bf16[512,128]{1,0:T(8,128)(2,1)S(1)}, bf16[512,128]{1,0:T(8,128)(2,1)S(1)}, bf16[1024,128]{1,0:T(8,128)(2,1)S(1)}, bf16[1024,128]{1,0:T(8,128)(2,1...) custom-call(s32[4]{0:T(128)S(1)} %pad_add_fusion.refs_0_.place, ...), custom_call_target="tpu_custom_call" | custom-call | bytes 7000000 | tf_op jit(solution)/shard_map/gather1/pallas_call | solution.py:359
  75.7 5.3 %collective-permute-start.4 = (bf16[1024,128]{1,0:T(8,128)(2,1)S(1)}, bf16[1024,128]{1,0:T(8,128)(2,1)S(1)}, u32[]{:S(2)}, u32[]{:S(2)}) collective-permute-start(bf16[1024,128]{1,0:T(8,128)(2,1)S(1)} %pad_maximum_fusion.1), channel_id=1, source_target_pairs={{0,32},{1,225},{2,34},{3,227},{32,64},{33,1},{34,66},{35,3},{64,96... | collective-permute-start | bytes 786440 | tf_op jit(solution)/shard_map/ppermute | solution.py:311
  81.0 6.0 %collective-permute-done.8.refs_7_ = bf16[512,128]{1,0:T(8,128)(2,1)S(1)} collective-permute-done((bf16[512,128]{1,0:T(8,128)(2,1)S(1)}, bf16[512,128]{1,0:T(8,128)(2,1)S(1)}, u32[]{:S(2)}, u32[]{:S(2)}) %collective-permute-start.8) | collective-permute-done | bytes 131104 | tf_op jit(solution)/shard_map/ppermute | solution.py:311
  87.0 0.1 collective-permute-start.9
  87.1 0.1 add_convert_fusion.3
  87.2 2.7 %collective-permute-start.5 = (bf16[1024,128]{1,0:T(8,128)(2,1)S(1)}, bf16[1024,128]{1,0:T(8,128)(2,1)S(1)}, u32[]{:S(2)}, u32[]{:S(2)}) collective-permute-start(bf16[1024,128]{1,0:T(8,128)(2,1)S(1)} %add_convert_fusion.3), channel_id=1, source_target_pairs={{0,32},{1,225},{2,34},{3,227},{32,64},{33,1},{34,66},{35,3},{64,96... | collective-permute-start | bytes 786440 | tf_op jit(solution)/shard_map/ppermute | solution.py:311
  89.9 3.6 %collective-permute-done.9.refs_6_ = bf16[1024,128]{1,0:T(8,128)(2,1)S(1)} collective-permute-done((bf16[1024,128]{1,0:T(8,128)(2,1)S(1)}, bf16[1024,128]{1,0:T(8,128)(2,1)S(1)}, u32[]{:S(2)}, u32[]{:S(2)}) %collective-permute-start.9) | collective-permute-done | bytes 262176 | tf_op jit(solution)/shard_map/ppermute | solution.py:311
  93.6 0.1 collective-permute-start.10
  93.7 2.4 %collective-permute-done.5.refs_3_ = bf16[1024,128]{1,0:T(8,128)(2,1)S(1)} collective-permute-done((bf16[1024,128]{1,0:T(8,128)(2,1)S(1)}, bf16[1024,128]{1,0:T(8,128)(2,1)S(1)}, u32[]{:S(2)}, u32[]{:S(2)}) %collective-permute-start.5) | collective-permute-done | bytes 262176 | tf_op jit(solution)/shard_map/ppermute | solution.py:311
  96.1 3.6 %collective-permute-start.6 = (bf16[1024,128]{1,0:T(8,128)(2,1)S(1)}, bf16[1024,128]{1,0:T(8,128)(2,1)S(1)}, u32[]{:S(2)}, u32[]{:S(2)}) collective-permute-start(bf16[1024,128]{1,0:T(8,128)(2,1)S(1)} %add_convert_fusion.2), channel_id=1, source_target_pairs={{0,32},{1,225},{2,34},{3,227},{32,64},{33,1},{34,66},{35,3},{64,96... | collective-permute-start | bytes 786440 | tf_op jit(solution)/shard_map/ppermute | solution.py:311
  99.8 0.4 collective-permute-done.10.refs_5_
  100.2 0.1 collective-permute-start.11
  100.3 5.0 %collective-permute-done.6.refs_4_ = bf16[1024,128]{1,0:T(8,128)(2,1)S(1)} collective-permute-done((bf16[1024,128]{1,0:T(8,128)(2,1)S(1)}, bf16[1024,128]{1,0:T(8,128)(2,1)S(1)}, u32[]{:S(2)}, u32[]{:S(2)}) %collective-permute-start.6) | collective-permute-done | bytes 262176 | tf_op jit(solution)/shard_map/ppermute | solution.py:311
  105.3 3.5 %collective-permute-start.7 = (bf16[512,128]{1,0:T(8,128)(2,1)S(1)}, bf16[512,128]{1,0:T(8,128)(2,1)S(1)}, u32[]{:S(2)}, u32[]{:S(2)}) collective-permute-start(bf16[512,128]{1,0:T(8,128)(2,1)S(1)} %add_convert_fusion.5), channel_id=1, source_target_pairs={{0,32},{1,225},{2,34},{3,227},{32,64},{33,1},{34,66},{35,3},{64,96... | collective-permute-start | bytes 393224 | tf_op jit(solution)/shard_map/ppermute | solution.py:311
  108.8 1.9 collective-permute-done.7.refs_3_
  110.7 1.4 grid1.1.refs_0_
  112.1 1.5 spread0.1
  113.6 1.3 copy-done
  114.9 3.6 %all-to-all-start.2 = ((bf16[8,8,128,128]{3,2,1,0:T(8,128)(2,1)}), bf16[8,8,128,128]{3,2,1,0:T(8,128)(2,1)S(1)}, u32[]{:S(2)}, u32[]{:S(2)}) async-start(bf16[8,8,128,128]{3,2,1,0:T(8,128)(2,1)} %copy-done), calls=%async_computation.2 | async-start | bytes 4194304 | tf_op jit(solution)/shard_map/all_to_all | solution.py:355
  118.6 3.2 %collective-permute-start.12 = (bf16[512,128]{1,0:T(8,128)(2,1)S(1)}, bf16[512,128]{1,0:T(8,128)(2,1)S(1)}, u32[]{:S(2)}, u32[]{:S(2)}) collective-permute-start(bf16[512,128]{1,0:T(8,128)(2,1)S(1)} %grid1.1.refs_0_), channel_id=1, source_target_pairs={{0,32},{1,225},{2,34},{3,227},{32,64},{33,1},{34,66},{35,3},{64,96... | collective-permute-start | bytes 393224 | tf_op jit(solution)/shard_map/ppermute | solution.py:311
  121.7 1.9 collective-permute-done.12.refs_1_
  123.7 3.1 %collective-permute-start.13 = (bf16[512,128]{1,0:T(8,128)(2,1)S(1)}, bf16[512,128]{1,0:T(8,128)(2,1)S(1)}, u32[]{:S(2)}, u32[]{:S(2)}) collective-permute-start(bf16[512,128]{1,0:T(8,128)(2,1)S(1)} %collective-permute-done.12.refs_1_), channel_id=1, source_target_pairs={{0,32},{1,225},{2,34},{3,227},{32,64},{33,1},{34,66},{35,3},{64,96... | collective-permute-start | bytes 393224 | tf_op jit(solution)/shard_map/ppermute | solution.py:311
  126.7 2.4 %collective-permute-done.13.refs_2_ = bf16[512,128]{1,0:T(8,128)(2,1)S(1)} collective-permute-done((bf16[512,128]{1,0:T(8,128)(2,1)S(1)}, bf16[512,128]{1,0:T(8,128)(2,1)S(1)}, u32[]{:S(2)}, u32[]{:S(2)}) %collective-permute-start.13) | collective-permute-done | bytes 131104 | tf_op jit(solution)/shard_map/ppermute | solution.py:311
  129.1 3.4 %collective-permute-start.14 = (bf16[512,128]{1,0:T(8,128)(2,1)S(1)}, bf16[512,128]{1,0:T(8,128)(2,1)S(1)}, u32[]{:S(2)}, u32[]{:S(2)}) collective-permute-start(bf16[512,128]{1,0:T(8,128)(2,1)S(1)} %collective-permute-done.13.refs_2_), channel_id=1, source_target_pairs={{0,32},{1,225},{2,34},{3,227},{32,64},{33,1},{34,66},{35,3},{64,96... | collective-permute-start | bytes 393224 | tf_op jit(solution)/shard_map/ppermute | solution.py:311
  132.5 1.9 collective-permute-done.14.refs_3_
  134.5 3.4 %collective-permute-start.15 = (bf16[512,128]{1,0:T(8,128)(2,1)S(1)}, bf16[512,128]{1,0:T(8,128)(2,1)S(1)}, u32[]{:S(2)}, u32[]{:S(2)}) collective-permute-start(bf16[512,128]{1,0:T(8,128)(2,1)S(1)} %collective-permute-done.14.refs_3_), channel_id=1, source_target_pairs={{0,32},{1,225},{2,34},{3,227},{32,64},{33,1},{34,66},{35,3},{64,96... | collective-permute-start | bytes 393224 | tf_op jit(solution)/shard_map/ppermute | solution.py:311
  137.8 1.9 collective-permute-done.15.refs_4_
  139.8 1.5 spread1.1
  141.3 1.3 copy-done.1
  142.6 5.2 %all-to-all-start.3 = ((bf16[8,8,128,128]{3,2,1,0:T(8,128)(2,1)}), bf16[8,8,128,128]{3,2,1,0:T(8,128)(2,1)}, u32[]{:S(2)}, u32[]{:S(2)}) async-start(bf16[8,8,128,128]{3,2,1,0:T(8,128)(2,1)} %copy-done.1), calls=%async_computation.3 | async-start | bytes 4194304 | tf_op jit(solution)/shard_map/all_to_all | solution.py:355
  147.8 5.1 %accum0.1 = (bf16[2048,128]{1,0:T(8,128)(2,1)S(1)}, bf16[2048,128]{1,0:T(8,128)(2,1)}, bf16[2048,128]{1,0:T(8,128)(2,1)}, bf16[2048,128]{1,0:T(8,128)(2,1)}) custom-call(s32[4]{0:T(128)S(1)} %pad_add_fusion.refs_0_.place, s32[64]{0:T(128)S(1)} %bitcast.27, bf16[8,8,128,128]{3,2,1,0:T(8,128)(2,1)S(1)} %all-to-all-done.2.returned, bf16[128,256]{1,0:T(8,128)(2,1)S(1)} %copy-done.5), custom_call_target="tpu_custom_call" | custom-call | bytes 17500000 | tf_op jit(solution)/shard_map/accum0/pallas_call | solution.py:377
  153.0 0.8 copy-done.3
  153.8 9.8 %collective-permute-start.19 = (bf16[2048,128]{1,0:T(8,128)(2,1)}, bf16[2048,128]{1,0:T(8,128)(2,1)S(1)}, u32[]{:S(2)}, u32[]{:S(2)}) collective-permute-start(bf16[2048,128]{1,0:T(8,128)(2,1)} %get-tuple-element.65), channel_id=1, source_target_pairs={{0,1},{1,0},{2,3},{3,2},{4,5},{5,4},{6,7},{7,6},{8,9},{9,8},{10,11... | collective-permute-start | bytes 1572872 | tf_op jit(solution)/shard_map/ppermute | solution.py:315
  163.6 2.5 %collective-permute-start.20 = (bf16[2048,128]{1,0:T(8,128)(2,1)}, bf16[2048,128]{1,0:T(8,128)(2,1)S(1)}, u32[]{:S(2)}, u32[]{:S(2)}) collective-permute-start(bf16[2048,128]{1,0:T(8,128)(2,1)} %get-tuple-element.66), channel_id=1, source_target_pairs={{0,2},{1,3},{2,0},{3,1},{4,6},{5,7},{6,4},{7,5},{8,10},{9,11},{10,... | collective-permute-start | bytes 1572872 | tf_op jit(solution)/shard_map/ppermute | solution.py:315
  166.0 0.7 collective-permute-start.21
  166.7 0.3 all-to-all-done.3.returned
  167.0 4.5 %accum1.1 = (bf16[2048,128]{1,0:T(8,128)(2,1)S(1)}, bf16[2048,128]{1,0:T(8,128)(2,1)S(1)}, bf16[2048,128]{1,0:T(8,128)(2,1)S(1)}, bf16[2048,128]{1,0:T(8,128)(2,1)S(1)}) custom-call(s32[4]{0:T(128)S(1)} %pad_add_fusion.refs_0_.place, s32[64]{0:T(128)S(1)} %bitcast.28, bf16[8,8,128,128]{3,2,1,0:T(8,128)(2,1)} %all-to-all-done.3.returned, ...), custom_call_target="tpu_custom_call" | custom-call | bytes 17500000 | tf_op jit(solution)/shard_map/accum1/pallas_call | solution.py:377
  171.5 13.0 %collective-permute-start.22 = (bf16[2048,128]{1,0:T(8,128)(2,1)S(1)}, bf16[2048,128]{1,0:T(8,128)(2,1)S(1)}, u32[]{:S(2)}, u32[]{:S(2)}) collective-permute-start(bf16[2048,128]{1,0:T(8,128)(2,1)S(1)} %get-tuple-element.70), channel_id=1, source_target_pairs={{0,1},{1,0},{2,3},{3,2},{4,5},{5,4},{6,7},{7,6},{8,9},{9,8},{10,11... | collective-permute-start | bytes 1572872 | tf_op jit(solution)/shard_map/ppermute | solution.py:315
  184.5 3.2 %collective-permute-start.23 = (bf16[2048,128]{1,0:T(8,128)(2,1)S(1)}, bf16[2048,128]{1,0:T(8,128)(2,1)S(1)}, u32[]{:S(2)}, u32[]{:S(2)}) collective-permute-start(bf16[2048,128]{1,0:T(8,128)(2,1)S(1)} %get-tuple-element.71), channel_id=1, source_target_pairs={{0,2},{1,3},{2,0},{3,1},{4,6},{5,7},{6,4},{7,5},{8,10},{9,11},{10,... | collective-permute-start | bytes 1572872 | tf_op jit(solution)/shard_map/ppermute | solution.py:315
  187.7 0.1 collective-permute-start.24
  187.8 16.5 %collective-permute-done.21.refs_5_ = bf16[2048,128]{1,0:T(8,128)(2,1)S(1)} collective-permute-done((bf16[2048,128]{1,0:T(8,128)(2,1)}, bf16[2048,128]{1,0:T(8,128)(2,1)S(1)}, u32[]{:S(2)}, u32[]{:S(2)}) %collective-permute-start.21) | collective-permute-done | bytes 524320 | tf_op jit(solution)/shard_map/ppermute | solution.py:315
  204.3 4.4 %half.1.refs_2_ = f32[2048,512]{1,0:T(8,128)S(1)} custom-call(s32[4]{0:T(128)S(1)} %pad_add_fusion.refs_0_.place, bf16[2,4,128,512]{3,2,1,0:T(8,128)(2,1)S(1)} %bitcast.21, bf16[2048,128]{1,0:T(8,128)(2,1)S(1)} %copy-done.4, bf16[2048,128]{1,0:T(8,128)(2,1)S(1)} %collective-permute-done.19.refs_3_, bf16[2048,128]{1,0:T(8,128)(2,1)S(1)} %collective-permute-done.20.refs_4_, ...), custom_call_target="tpu_custom_call" | custom-call | bytes 14000000 | tf_op jit(solution)/shard_map/half/pallas_call | solution.py:441
  208.7 10.9 %collective-permute-done.24.refs_4_ = bf16[2048,128]{1,0:T(8,128)(2,1)S(1)} collective-permute-done((bf16[2048,128]{1,0:T(8,128)(2,1)S(1)}, bf16[2048,128]{1,0:T(8,128)(2,1)S(1)}, u32[]{:S(2)}, u32[]{:S(2)}) %collective-permute-start.24) | collective-permute-done | bytes 524320 | tf_op jit(solution)/shard_map/ppermute | solution.py:315
  219.6 3.4 %finish.1 = bf16[2,2048,256]{2,1,0:T(8,128)(2,1)} custom-call(s32[4]{0:T(128)S(1)} %pad_add_fusion.refs_0_.place, bf16[2,4,128,512]{3,2,1,0:T(8,128)(2,1)S(1)} %bitcast.22, f32[2048,512]{1,0:T(8,128)S(1)} %half.1.refs_2_, bf16[2048,128]{1,0:T(8,128)(2,1)S(1)} %collective-permute-done.23.refs_3_, bf16[2048,128]{1,0:T(8,128)(2,1)S(1)} %collective-permute-done.24.refs_4_), custom_call_target="tpu_custom_call" | custom-call | bytes 14000000 | tf_op jit(solution)/shard_map/finish/pallas_call | solution.py:451
  (46 shorter events, 0.4 us)
Async XLA Ops:
  7.9 7.5 %copy-start.12 = (s32[4,128]{1,0:T(4,128)S(1)}, s32[4,128]{1,0:T(4,128)}, u32[]{:S(2)}) copy-start(s32[4,128]{1,0:T(4,128)} %param.14) | copy-start | bytes 6148
  7.9 34.5 %all-to-all-start = ((bf16[16,4,128,128]{3,2,1,0:T(8,128)(2,1)}), bf16[16,4,128,128]{3,2,1,0:T(8,128)(2,1)}, u32[]{:S(2)}, u32[]{:S(2)}) async-start(bf16[16,4,128,128]{3,2,1,0:T(8,128)(2,1)} %contrib0.1), calls=%async_computation | async-start | bytes 4194304 | tf_op jit(solution)/shard_map/all_to_all | solution.py:355
  15.5 8.7 %copy-start.8 = (f32[32,512]{1,0:T(8,128)S(1)}, f32[32,512]{1,0:T(8,128)}, u32[]{:S(2)}) copy-start(f32[32,512]{1,0:T(8,128)} %constant.62.clone) | copy-start | bytes 196612
  15.5 8.7 %copy-start.9 = (f32[32,512]{1,0:T(8,128)S(1)}, f32[32,512]{1,0:T(8,128)}, u32[]{:S(2)}) copy-start(f32[32,512]{1,0:T(8,128)} %constant.61.clone) | copy-start | bytes 196612
  15.5 8.8 %copy-start.10 = (f32[16,512]{1,0:T(8,128)S(1)}, f32[16,512]{1,0:T(8,128)}, u32[]{:S(2)}) copy-start(f32[16,512]{1,0:T(8,128)} %constant.64.clone) | copy-start | bytes 98308
  15.5 8.8 %copy-start.11 = (f32[16,512]{1,0:T(8,128)S(1)}, f32[16,512]{1,0:T(8,128)}, u32[]{:S(2)}) copy-start(f32[16,512]{1,0:T(8,128)} %constant.63.clone) | copy-start | bytes 98308
  42.4 4.6 %copy-start.6 = (s32[64]{0:T(128)S(1)}, s32[64]{0:T(128)}, u32[]{:S(2)}) copy-start(s32[64]{0:T(128)} %offsets.3) | copy-start | bytes 772
  42.4 30.6 %all-to-all-start.1 = ((bf16[8,8,128,128]{3,2,1,0:T(8,128)(2,1)}), bf16[8,8,128,128]{3,2,1,0:T(8,128)(2,1)}, u32[]{:S(2)}, u32[]{:S(2)}) async-start(bf16[8,8,128,128]{3,2,1,0:T(8,128)(2,1)} %contrib1.1), calls=%async_computation.1 | async-start | bytes 4194304 | tf_op jit(solution)/shard_map/all_to_all | solution.py:355
  47.0 21.3 %copy-start.2 = (bf16[1,2,512,128]{3,2,1,0:T(8,128)(2,1)S(1)}, bf16[1,2,512,128]{3,2,1,0:T(8,128)(2,1)}, u32[]{:S(2)}) copy-start(bf16[1,2,512,128]{3,2,1,0:T(8,128)(2,1)} %param.15) | copy-start | bytes 786436
  49.5 9.7 %collective-permute-start = (bf16[512,128]{1,0:T(8,128)(2,1)S(1)}, bf16[512,128]{1,0:T(8,128)(2,1)S(1)}, u32[]{:S(2)}, u32[]{:S(2)}) collective-permute-start(bf16[512,128]{1,0:T(8,128)(2,1)S(1)} %get-tuple-element.49), channel_id=1, source_target_pairs={{0,128},{64,192},{128,0},{192,64},{1,129},{65,193},{129,1},{193,65... | collective-permute-start | bytes 393224 | tf_op jit(solution)/shard_map/ppermute | solution.py:301
  55.6 9.7 %collective-permute-start.1 = (bf16[512,128]{1,0:T(8,128)(2,1)S(1)}, bf16[512,128]{1,0:T(8,128)(2,1)S(1)}, u32[]{:S(2)}, u32[]{:S(2)}) collective-permute-start(bf16[512,128]{1,0:T(8,128)(2,1)S(1)} %get-tuple-element.50), channel_id=1, source_target_pairs={{0,64},{64,128},{128,192},{192,0},{1,65},{65,129},{129,193},{193,1... | collective-permute-start | bytes 393224 | tf_op jit(solution)/shard_map/ppermute | solution.py:301
  56.8 11.4 %collective-permute-start.2 = (bf16[512,128]{1,0:T(8,128)(2,1)S(1)}, bf16[512,128]{1,0:T(8,128)(2,1)S(1)}, u32[]{:S(2)}, u32[]{:S(2)}) collective-permute-start(bf16[512,128]{1,0:T(8,128)(2,1)S(1)} %get-tuple-element.51), channel_id=1, source_target_pairs={{0,192},{64,0},{128,64},{192,128},{1,193},{65,1},{129,65},{193,129... | collective-permute-start | bytes 393224 | tf_op jit(solution)/shard_map/ppermute | solution.py:301
  69.6 6.1 %collective-permute-start.3 = (bf16[512,128]{1,0:T(8,128)(2,1)S(1)}, bf16[512,128]{1,0:T(8,128)(2,1)S(1)}, u32[]{:S(2)}, u32[]{:S(2)}) collective-permute-start(bf16[512,128]{1,0:T(8,128)(2,1)S(1)} %grid0.1.refs_0_), channel_id=1, source_target_pairs={{0,32},{1,225},{2,34},{3,227},{32,64},{33,1},{34,66},{35,3},{64,96... | collective-permute-start | bytes 393224 | tf_op jit(solution)/shard_map/ppermute | solution.py:311
  75.7 11.4 %collective-permute-start.4 = (bf16[1024,128]{1,0:T(8,128)(2,1)S(1)}, bf16[1024,128]{1,0:T(8,128)(2,1)S(1)}, u32[]{:S(2)}, u32[]{:S(2)}) collective-permute-start(bf16[1024,128]{1,0:T(8,128)(2,1)S(1)} %pad_maximum_fusion.1), channel_id=1, source_target_pairs={{0,32},{1,225},{2,34},{3,227},{32,64},{33,1},{34,66},{35,3},{64,96... | collective-permute-start | bytes 786440 | tf_op jit(solution)/shard_map/ppermute | solution.py:311
  81.0 6.0 %collective-permute-start.8 = (bf16[512,128]{1,0:T(8,128)(2,1)S(1)}, bf16[512,128]{1,0:T(8,128)(2,1)S(1)}, u32[]{:S(2)}, u32[]{:S(2)}) collective-permute-start(bf16[512,128]{1,0:T(8,128)(2,1)S(1)} %grid0.1.refs_0_), channel_id=1, source_target_pairs={{0,224},{1,33},{2,226},{3,35},{32,0},{33,65},{34,2},{35,67},{64,32... | collective-permute-start | bytes 393224 | tf_op jit(solution)/shard_map/ppermute | solution.py:311
  87.0 6.5 %collective-permute-start.9 = (bf16[1024,128]{1,0:T(8,128)(2,1)S(1)}, bf16[1024,128]{1,0:T(8,128)(2,1)S(1)}, u32[]{:S(2)}, u32[]{:S(2)}) collective-permute-start(bf16[1024,128]{1,0:T(8,128)(2,1)S(1)} %pad_maximum_fusion.2), channel_id=1, source_target_pairs={{0,224},{1,33},{2,226},{3,35},{32,0},{33,65},{34,2},{35,67},{64,32... | collective-permute-start | bytes 786440 | tf_op jit(solution)/shard_map/ppermute | solution.py:311
  87.2 8.8 %collective-permute-start.5 = (bf16[1024,128]{1,0:T(8,128)(2,1)S(1)}, bf16[1024,128]{1,0:T(8,128)(2,1)S(1)}, u32[]{:S(2)}, u32[]{:S(2)}) collective-permute-start(bf16[1024,128]{1,0:T(8,128)(2,1)S(1)} %add_convert_fusion.3), channel_id=1, source_target_pairs={{0,32},{1,225},{2,34},{3,227},{32,64},{33,1},{34,66},{35,3},{64,96... | collective-permute-start | bytes 786440 | tf_op jit(solution)/shard_map/ppermute | solution.py:311
  93.6 6.5 %collective-permute-start.10 = (bf16[1024,128]{1,0:T(8,128)(2,1)S(1)}, bf16[1024,128]{1,0:T(8,128)(2,1)S(1)}, u32[]{:S(2)}, u32[]{:S(2)}) collective-permute-start(bf16[1024,128]{1,0:T(8,128)(2,1)S(1)} %add_convert_fusion.1), channel_id=1, source_target_pairs={{0,224},{1,33},{2,226},{3,35},{32,0},{33,65},{34,2},{35,67},{64,32... | collective-permute-start | bytes 786440 | tf_op jit(solution)/shard_map/ppermute | solution.py:311
  96.1 9.1 %collective-permute-start.6 = (bf16[1024,128]{1,0:T(8,128)(2,1)S(1)}, bf16[1024,128]{1,0:T(8,128)(2,1)S(1)}, u32[]{:S(2)}, u32[]{:S(2)}) collective-permute-start(bf16[1024,128]{1,0:T(8,128)(2,1)S(1)} %add_convert_fusion.2), channel_id=1, source_target_pairs={{0,32},{1,225},{2,34},{3,227},{32,64},{33,1},{34,66},{35,3},{64,96... | collective-permute-start | bytes 786440 | tf_op jit(solution)/shard_map/ppermute | solution.py:311
  100.2 8.6 %collective-permute-start.11 = (bf16[512,128]{1,0:T(8,128)(2,1)S(1)}, bf16[512,128]{1,0:T(8,128)(2,1)S(1)}, u32[]{:S(2)}, u32[]{:S(2)}) collective-permute-start(bf16[512,128]{1,0:T(8,128)(2,1)S(1)} %add_convert_fusion.4), channel_id=1, source_target_pairs={{0,224},{1,33},{2,226},{3,35},{32,0},{33,65},{34,2},{35,67},{64,32... | collective-permute-start | bytes 393224 | tf_op jit(solution)/shard_map/ppermute | solution.py:311
  105.3 5.4 %collective-permute-start.7 = (bf16[512,128]{1,0:T(8,128)(2,1)S(1)}, bf16[512,128]{1,0:T(8,128)(2,1)S(1)}, u32[]{:S(2)}, u32[]{:S(2)}) collective-permute-start(bf16[512,128]{1,0:T(8,128)(2,1)S(1)} %add_convert_fusion.5), channel_id=1, source_target_pairs={{0,32},{1,225},{2,34},{3,227},{32,64},{33,1},{34,66},{35,3},{64,96... | collective-permute-start | bytes 393224 | tf_op jit(solution)/shard_map/ppermute | solution.py:311
  113.6 1.3 copy-start
  114.9 27.7 %all-to-all-start.2 = ((bf16[8,8,128,128]{3,2,1,0:T(8,128)(2,1)}), bf16[8,8,128,128]{3,2,1,0:T(8,128)(2,1)S(1)}, u32[]{:S(2)}, u32[]{:S(2)}) async-start(bf16[8,8,128,128]{3,2,1,0:T(8,128)(2,1)} %copy-done), calls=%async_computation.2 | async-start | bytes 4194304 | tf_op jit(solution)/shard_map/all_to_all | solution.py:355
  118.6 5.1 %collective-permute-start.12 = (bf16[512,128]{1,0:T(8,128)(2,1)S(1)}, bf16[512,128]{1,0:T(8,128)(2,1)S(1)}, u32[]{:S(2)}, u32[]{:S(2)}) collective-permute-start(bf16[512,128]{1,0:T(8,128)(2,1)S(1)} %grid1.1.refs_0_), channel_id=1, source_target_pairs={{0,32},{1,225},{2,34},{3,227},{32,64},{33,1},{34,66},{35,3},{64,96... | collective-permute-start | bytes 393224 | tf_op jit(solution)/shard_map/ppermute | solution.py:311
  121.7 5.0 %collective-permute-start.16 = (bf16[512,128]{1,0:T(8,128)(2,1)S(1)}, bf16[512,128]{1,0:T(8,128)(2,1)S(1)}, u32[]{:S(2)}, u32[]{:S(2)}) collective-permute-start(bf16[512,128]{1,0:T(8,128)(2,1)S(1)} %grid1.1.refs_0_), channel_id=1, source_target_pairs={{0,224},{1,33},{2,226},{3,35},{32,0},{33,65},{34,2},{35,67},{64,32... | collective-permute-start | bytes 393224 | tf_op jit(solution)/shard_map/ppermute | solution.py:311
  123.7 5.4 %collective-permute-start.13 = (bf16[512,128]{1,0:T(8,128)(2,1)S(1)}, bf16[512,128]{1,0:T(8,128)(2,1)S(1)}, u32[]{:S(2)}, u32[]{:S(2)}) collective-permute-start(bf16[512,128]{1,0:T(8,128)(2,1)S(1)} %collective-permute-done.12.refs_1_), channel_id=1, source_target_pairs={{0,32},{1,225},{2,34},{3,227},{32,64},{33,1},{34,66},{35,3},{64,96... | collective-permute-start | bytes 393224 | tf_op jit(solution)/shard_map/ppermute | solution.py:311
  126.7 5.8 %collective-permute-start.17 = (bf16[512,128]{1,0:T(8,128)(2,1)S(1)}, bf16[512,128]{1,0:T(8,128)(2,1)S(1)}, u32[]{:S(2)}, u32[]{:S(2)}) collective-permute-start(bf16[512,128]{1,0:T(8,128)(2,1)S(1)} %collective-permute-done.16.refs_7_), channel_id=1, source_target_pairs={{0,224},{1,33},{2,226},{3,35},{32,0},{33,65},{34,2},{35,67},{64,32... | collective-permute-start | bytes 393224 | tf_op jit(solution)/shard_map/ppermute | solution.py:311
  129.1 5.4 %collective-permute-start.14 = (bf16[512,128]{1,0:T(8,128)(2,1)S(1)}, bf16[512,128]{1,0:T(8,128)(2,1)S(1)}, u32[]{:S(2)}, u32[]{:S(2)}) collective-permute-start(bf16[512,128]{1,0:T(8,128)(2,1)S(1)} %collective-permute-done.13.refs_2_), channel_id=1, source_target_pairs={{0,32},{1,225},{2,34},{3,227},{32,64},{33,1},{34,66},{35,3},{64,96... | collective-permute-start | bytes 393224 | tf_op jit(solution)/shard_map/ppermute | solution.py:311
  132.5 5.3 %collective-permute-start.18 = (bf16[512,128]{1,0:T(8,128)(2,1)S(1)}, bf16[512,128]{1,0:T(8,128)(2,1)S(1)}, u32[]{:S(2)}, u32[]{:S(2)}) collective-permute-start(bf16[512,128]{1,0:T(8,128)(2,1)S(1)} %collective-permute-done.17.refs_6_), channel_id=1, source_target_pairs={{0,224},{1,33},{2,226},{3,35},{32,0},{33,65},{34,2},{35,67},{64,32... | collective-permute-start | bytes 393224 | tf_op jit(solution)/shard_map/ppermute | solution.py:311
  134.5 5.3 %collective-permute-start.15 = (bf16[512,128]{1,0:T(8,128)(2,1)S(1)}, bf16[512,128]{1,0:T(8,128)(2,1)S(1)}, u32[]{:S(2)}, u32[]{:S(2)}) collective-permute-start(bf16[512,128]{1,0:T(8,128)(2,1)S(1)} %collective-permute-done.14.refs_3_), channel_id=1, source_target_pairs={{0,32},{1,225},{2,34},{3,227},{32,64},{33,1},{34,66},{35,3},{64,96... | collective-permute-start | bytes 393224 | tf_op jit(solution)/shard_map/ppermute | solution.py:311
  141.3 1.3 copy-start.1
  142.6 5.2 %copy-start.5 = (bf16[128,256]{1,0:T(8,128)(2,1)S(1)}, bf16[128,256]{1,0:T(8,128)(2,1)}, u32[]{:S(2)}) copy-start(bf16[128,256]{1,0:T(8,128)(2,1)} %constant.66.clone.table) | copy-start | bytes 196612
  142.6 5.2 %copy-start.7 = (s32[64,1]{0,1:T(1,128)S(1)}, s32[64,1]{0,1:T(1,128)}, u32[]{:S(2)}) copy-start(s32[64,1]{0,1:T(1,128)} %param.12) | copy-start | bytes 772
  142.6 24.4 %all-to-all-start.3 = ((bf16[8,8,128,128]{3,2,1,0:T(8,128)(2,1)}), bf16[8,8,128,128]{3,2,1,0:T(8,128)(2,1)}, u32[]{:S(2)}, u32[]{:S(2)}) async-start(bf16[8,8,128,128]{3,2,1,0:T(8,128)(2,1)} %copy-done.1), calls=%async_computation.3 | async-start | bytes 4194304 | tf_op jit(solution)/shard_map/all_to_all | solution.py:355
  152.9 0.8 copy-start.3
  153.8 50.5 %copy-start.4 = (bf16[2048,128]{1,0:T(8,128)(2,1)S(1)}, bf16[2048,128]{1,0:T(8,128)(2,1)}, u32[]{:S(2)}) copy-start(bf16[2048,128]{1,0:T(8,128)(2,1)} %copy-done.3) | copy-start | bytes 1572868
  153.8 33.9 %collective-permute-start.19 = (bf16[2048,128]{1,0:T(8,128)(2,1)}, bf16[2048,128]{1,0:T(8,128)(2,1)S(1)}, u32[]{:S(2)}, u32[]{:S(2)}) collective-permute-start(bf16[2048,128]{1,0:T(8,128)(2,1)} %get-tuple-element.65), channel_id=1, source_target_pairs={{0,1},{1,0},{2,3},{3,2},{4,5},{5,4},{6,7},{7,6},{8,9},{9,8},{10,11... | collective-permute-start | bytes 1572872 | tf_op jit(solution)/shard_map/ppermute | solution.py:315
  163.6 24.2 %collective-permute-start.20 = (bf16[2048,128]{1,0:T(8,128)(2,1)}, bf16[2048,128]{1,0:T(8,128)(2,1)S(1)}, u32[]{:S(2)}, u32[]{:S(2)}) collective-permute-start(bf16[2048,128]{1,0:T(8,128)(2,1)} %get-tuple-element.66), channel_id=1, source_target_pairs={{0,2},{1,3},{2,0},{3,1},{4,6},{5,7},{6,4},{7,5},{8,10},{9,11},{10,... | collective-permute-start | bytes 1572872 | tf_op jit(solution)/shard_map/ppermute | solution.py:315
  166.0 38.3 %collective-permute-start.21 = (bf16[2048,128]{1,0:T(8,128)(2,1)}, bf16[2048,128]{1,0:T(8,128)(2,1)S(1)}, u32[]{:S(2)}, u32[]{:S(2)}) collective-permute-start(bf16[2048,128]{1,0:T(8,128)(2,1)} %get-tuple-element.67), channel_id=1, source_target_pairs={{0,3},{1,2},{2,1},{3,0},{4,7},{5,6},{6,5},{7,4},{8,11},{9,10},{10,... | collective-permute-start | bytes 1572872 | tf_op jit(solution)/shard_map/ppermute | solution.py:315
  171.5 32.8 %collective-permute-start.22 = (bf16[2048,128]{1,0:T(8,128)(2,1)S(1)}, bf16[2048,128]{1,0:T(8,128)(2,1)S(1)}, u32[]{:S(2)}, u32[]{:S(2)}) collective-permute-start(bf16[2048,128]{1,0:T(8,128)(2,1)S(1)} %get-tuple-element.70), channel_id=1, source_target_pairs={{0,1},{1,0},{2,3},{3,2},{4,5},{5,4},{6,7},{7,6},{8,9},{9,8},{10,11... | collective-permute-start | bytes 1572872 | tf_op jit(solution)/shard_map/ppermute | solution.py:315
  184.5 24.3 %collective-permute-start.23 = (bf16[2048,128]{1,0:T(8,128)(2,1)S(1)}, bf16[2048,128]{1,0:T(8,128)(2,1)S(1)}, u32[]{:S(2)}, u32[]{:S(2)}) collective-permute-start(bf16[2048,128]{1,0:T(8,128)(2,1)S(1)} %get-tuple-element.71), channel_id=1, source_target_pairs={{0,2},{1,3},{2,0},{3,1},{4,6},{5,7},{6,4},{7,5},{8,10},{9,11},{10,... | collective-permute-start | bytes 1572872 | tf_op jit(solution)/shard_map/ppermute | solution.py:315
  187.7 31.9 %collective-permute-start.24 = (bf16[2048,128]{1,0:T(8,128)(2,1)S(1)}, bf16[2048,128]{1,0:T(8,128)(2,1)S(1)}, u32[]{:S(2)}, u32[]{:S(2)}) collective-permute-start(bf16[2048,128]{1,0:T(8,128)(2,1)S(1)} %get-tuple-element.72), channel_id=1, source_target_pairs={{0,3},{1,2},{2,1},{3,0},{4,7},{5,6},{6,5},{7,4},{8,11},{9,10},{10,... | collective-permute-start | bytes 1572872 | tf_op jit(solution)/shard_map/ppermute | solution.py:315

commit v3 on v2

--- a/solution.py
+++ b/solution.py
@@ -131,7 +131,7 @@
         send(k).start()
         return 0
 
-    lax.fori_loop(0, depth, one_group, 0)
+    lax.fori_loop(0, depth, one_group, 0, unroll=2)
     for k in range(depth):
         send(k).wait()
 
@@ -156,7 +156,7 @@
             total[rows, :] = total[rows, :] + held[j, owner].astype(F32)
             return 0
 
-        lax.fori_loop(0, planes, one_facet, 0, unroll=2)
+        lax.fori_loop(0, planes, one_facet, 0, unroll=8)
         total[pl.ds(0, XM), :] = total[pl.ds(0, XM), :] + total[pl.ds(grid_len, XM), :]
         base = out.shape[0] - grid_len
         out[pl.ds(base, grid_len), :] = total[pl.ds(0, grid_len), :].astype(BF16)
@@ -199,7 +199,7 @@
             made_rows[j, k] = wide[rows, :].astype(BF16)
             return 0
 
-        lax.fori_loop(0, planes, one_facet, 0, unroll=2)
+        lax.fori_loop(0, planes, one_facet, 0, unroll=8)
         send(k).start()
     for k in range(len(images)):
         send(k).wait()
@@ -221,15 +221,17 @@
     def one_group(k, _):
         fetch(k).wait()
         item = lax.rem(place[1] + k * (depth - place[3]), depth) * planes
+        terms = []
         for j in range(0, planes, 2):
             blocks = [held[j, k].astype(F32), held[j + 1, k].astype(F32)]
             made = jnp.dot(table[...], stack_turned(blocks), preferred_element_type=F32)
-            for n in range(2):
-                rows = window_rows(starts, item + j + n, facet_len)
-                total[rows, :] = total[rows, :] + made[:, n * LANES : (n + 1) * LANES]
+            terms += [made[:, :LANES], made[:, LANES:]]
+        for j, term in enumerate(terms):
+            rows = window_rows(starts, item + j, facet_len)
+            total[rows, :] = total[rows, :] + term
         return 0
 
-    lax.fori_loop(0, depth, one_group, 0)
+    lax.fori_loop(0, depth, one_group, 0, unroll=2)
     total[pl.ds(0, XM), :] = total[pl.ds(0, XM), :] + total[pl.ds(facet_len, XM), :]
     tile = 256
     for k, out in enumerate(outs):
@@ -271,7 +273,8 @@
 
 
 def call(kernel, name, outs, in_specs, scratch, micros, limit, where=VMEM):
-    shapes = [jax.ShapeDtypeStruct(s, BF16) for s in outs]
+    made = jax.ShapeDtypeStruct if where is VMEM else pltpu.HBM
+    shapes = [made(s, BF16) for s in outs]
     one = len(outs) == 1
     return pl.pallas_call(
         kernel,

time: 224 us -> 222 us (level)
  local copies, waits for them, and re-layouts: 3.58 us -> 0.94 us
    unnamed x26 -> x22, local copies, waits for them, and re-layouts: 3.49 us -> 0.86 us
  transfers between devices with their start and end apart: 29 -> 29, of which waited for: 17 -> 17; matrix products, arithmetic and copies ran while one was open for 2% -> 2% of each run, Pallas kernels for 14% -> 13%
where the time goes in v3:
time: 222 us; the launch traced here: 221 us
  starting transfers between devices  89.4 us (40%)
  waiting for transfers between devices  82.8 us (37%)
  Pallas kernels  44 us (20%)
  other arithmetic  3.53 us (2%)
    ppermute x6, starting transfers between devices, swapped(): lax.ppermute(value, 'col', [(i, i ^ flip) for i in range(lax.axis_size('c...  29.4 us
    ppermute x16, starting transfers between devices, turned(): return lax.ppermute(value, (*FAR[1], 'col'), perm)  28.5 us
    ppermute x6, waiting for transfers between devices, swapped(): lax.ppermute(value, 'col', [(i, i ^ flip) for i in range(lax.axis_size('c...  27.9 us
    ppermute x16, waiting for transfers between devices, turned(): return lax.ppermute(value, (*FAR[1], 'col'), perm)  26.4 us
    all_to_all x4, starting transfers between devices, near(): return lax.all_to_all(value, NEAR[c], 0, 0, tiled=True)  21.7 us
    all_to_all x4, waiting for transfers between devices, near(): return lax.all_to_all(value, NEAR[c], 0, 0, tiled=True)  19.5 us
    pallas_call x2, Pallas kernels, contrib(): call(bind(contrib_kernel, c), f'contrib{c}', [blocks[c]], [SMEM, HBM, VME...  15.2 us
    ppermute x3, starting transfers between devices, shifted(): lax.ppermute(value, 'zq', [(i, (i + step) % size) for i in range(size)])  9.72 us
  transfers between devices with their start and end apart: 29, of which 17 were waited for; matrix products, arithmetic and copies ran while one was open for 2% of the time, Pallas kernels for 13%

profile of v3, /device:TPU:1, one launch (start us, length us, event | category | flops | bytes accessed | tf_op | source)
XLA Modules:
  0.0 221.0 jit_solution(2022239978917970685)
XLA Ops:
  0.0 7.3 %contrib0.1 = bf16[16,4,128,128]{3,2,1,0:T(8,128)(2,1)} custom-call(s32[64]{0:T(128)} %bitcast.25, bf16[2,8192,128]{2,1,0:T(8,128)(2,1)} %bitcast.29, bf16[128,256]{1,0:T(8,128)(2,1)} %constant.65.clone.refs_2_), custom_call_target="tpu_custom_call" | custom-call | bytes 28000000 | tf_op jit(solution)/shard_map/contrib0/pallas_call | solution.py:351
  7.4 7.5 %all-to-all-start = ((bf16[16,4,128,128]{3,2,1,0:T(8,128)(2,1)}), bf16[16,4,128,128]{3,2,1,0:T(8,128)(2,1)}, u32[]{:S(2)}, u32[]{:S(2)}) async-start(bf16[16,4,128,128]{3,2,1,0:T(8,128)(2,1)} %contrib0.1), calls=%async_computation | async-start | bytes 4194304 | tf_op jit(solution)/shard_map/all_to_all | solution.py:358
  14.9 0.1 mul.146
  15.0 7.9 %contrib1.1 = bf16[8,8,128,128]{3,2,1,0:T(8,128)(2,1)} custom-call(s32[64]{0:T(128)} %bitcast.26, bf16[2,8192,128]{2,1,0:T(8,128)(2,1)} %bitcast.30, bf16[128,256]{1,0:T(8,128)(2,1)} %constant.65.clone.refs_2_), custom_call_target="tpu_custom_call" | custom-call | bytes 28000000 | tf_op jit(solution)/shard_map/contrib1/pallas_call | solution.py:351
  22.9 0.4 subtract_convert_fusion
  23.2 0.1 pad_maximum_fusion.refs_1_
  23.4 2.6 %fusion.7 = (bf16[4,2,1,64,256]{4,3,2,0,1:T(8,128)(2,1)S(1)}, bf16[4,2,1,64,256]{4,3,2,0,1:T(8,128)(2,1)S(1)}, bf16[4,2,1,64,256]{4,3,2,0,1:T(8,128)(2,1)S(1)}) fusion(s32[4,2,64]{2,0,1:T(4,128)S(1)} %copy.12), kind=kLoop, calls=%fused_computation.20 | loop fusion | flops 2621440 | bytes 788480 | tf_op jit(solution)/shard_map/concatenate | solution.py:64
  25.9 0.1 maximum_maximum_fusion
  26.0 15.9 %all-to-all-done.refs_2_ = bf16[16,4,128,128]{3,2,1,0:T(8,128)(2,1)} async-done(((bf16[16,4,128,128]{3,2,1,0:T(8,128)(2,1)}), bf16[16,4,128,128]{3,2,1,0:T(8,128)(2,1)}, u32[]{:S(2)}, u32[]{:S(2)}) %all-to-all-start) | async-done | bytes 2097184 | tf_op jit(solution)/shard_map/all_to_all | solution.py:358
  41.9 4.5 %all-to-all-start.1 = ((bf16[8,8,128,128]{3,2,1,0:T(8,128)(2,1)}), bf16[8,8,128,128]{3,2,1,0:T(8,128)(2,1)}, u32[]{:S(2)}, u32[]{:S(2)}) async-start(bf16[8,8,128,128]{3,2,1,0:T(8,128)(2,1)} %contrib1.1), calls=%async_computation.1 | async-start | bytes 4194304 | tf_op jit(solution)/shard_map/all_to_all | solution.py:358
  46.5 0.1 pad_add_fusion.refs_0_.place
  46.5 2.3 %gather0.1 = (bf16[512,128]{1,0:T(8,128)(2,1)S(1)}, bf16[512,128]{1,0:T(8,128)(2,1)S(1)}, bf16[512,128]{1,0:T(8,128)(2,1)S(1)}, bf16[512,128]{1,0:T(8,128)(2,1)S(1)}) custom-call(s32[4]{0:T(128)S(1)} %pad_add_fusion.refs_0_.place, s32[64]{0:T(128)S(1)} %copy-done.4, bf16[16,4,128,128]{3,2,1,0:T(8,128)(2,1)} %all-to-all-done.refs_2_), custom_call_target="tpu_custom_call" | custom-call | bytes 7000000 | tf_op jit(solution)/shard_map/gather0/pallas_call | solution.py:362
  48.8 6.1 %collective-permute-start = (bf16[512,128]{1,0:T(8,128)(2,1)S(1)}, bf16[512,128]{1,0:T(8,128)(2,1)S(1)}, u32[]{:S(2)}, u32[]{:S(2)}) collective-permute-start(bf16[512,128]{1,0:T(8,128)(2,1)S(1)} %get-tuple-element.49), channel_id=1, source_target_pairs={{0,128},{64,192},{128,0},{192,64},{1,129},{65,193},{129,1},{193,65... | collective-permute-start | bytes 393224 | tf_op jit(solution)/shard_map/ppermute | solution.py:304
  55.0 1.1 collective-permute-start.1
  56.1 2.4 %collective-permute-start.2 = (bf16[512,128]{1,0:T(8,128)(2,1)S(1)}, bf16[512,128]{1,0:T(8,128)(2,1)S(1)}, u32[]{:S(2)}, u32[]{:S(2)}) collective-permute-start(bf16[512,128]{1,0:T(8,128)(2,1)S(1)} %get-tuple-element.51), channel_id=1, source_target_pairs={{0,192},{64,0},{128,64},{192,128},{1,193},{65,1},{129,65},{193,129... | collective-permute-start | bytes 393224 | tf_op jit(solution)/shard_map/ppermute | solution.py:304
  58.5 6.2 %collective-permute-done.1.refs_4_ = bf16[512,128]{1,0:T(8,128)(2,1)S(1)} collective-permute-done((bf16[512,128]{1,0:T(8,128)(2,1)S(1)}, bf16[512,128]{1,0:T(8,128)(2,1)S(1)}, u32[]{:S(2)}, u32[]{:S(2)}) %collective-permute-start.1) | collective-permute-done | bytes 131104 | tf_op jit(solution)/shard_map/ppermute | solution.py:304
  64.7 2.8 %collective-permute-done.2.refs_5_ = bf16[512,128]{1,0:T(8,128)(2,1)S(1)} collective-permute-done((bf16[512,128]{1,0:T(8,128)(2,1)S(1)}, bf16[512,128]{1,0:T(8,128)(2,1)S(1)}, u32[]{:S(2)}, u32[]{:S(2)}) %collective-permute-start.2) | collective-permute-done | bytes 131104 | tf_op jit(solution)/shard_map/ppermute | solution.py:304
  67.5 1.4 grid0.1.refs_0_
  68.9 0.1 collective-permute-start.3
  69.0 3.6 %all-to-all-done.1.refs_2_ = bf16[8,8,128,128]{3,2,1,0:T(8,128)(2,1)} async-done(((bf16[8,8,128,128]{3,2,1,0:T(8,128)(2,1)}), bf16[8,8,128,128]{3,2,1,0:T(8,128)(2,1)}, u32[]{:S(2)}, u32[]{:S(2)}) %all-to-all-start.1) | async-done | bytes 2097184 | tf_op jit(solution)/shard_map/all_to_all | solution.py:358
  72.6 2.3 %gather1.1 = (bf16[512,128]{1,0:T(8,128)(2,1)S(1)}, bf16[512,128]{1,0:T(8,128)(2,1)S(1)}, bf16[1024,128]{1,0:T(8,128)(2,1)S(1)}, bf16[1024,128]{1,0:T(8,128)(2,1...) custom-call(s32[4]{0:T(128)S(1)} %pad_add_fusion.refs_0_.place, ...), custom_call_target="tpu_custom_call" | custom-call | bytes 7000000 | tf_op jit(solution)/shard_map/gather1/pallas_call | solution.py:362
  74.9 5.4 %collective-permute-start.4 = (bf16[1024,128]{1,0:T(8,128)(2,1)S(1)}, bf16[1024,128]{1,0:T(8,128)(2,1)S(1)}, u32[]{:S(2)}, u32[]{:S(2)}) collective-permute-start(bf16[1024,128]{1,0:T(8,128)(2,1)S(1)} %pad_maximum_fusion.1), channel_id=1, source_target_pairs={{0,32},{1,225},{2,34},{3,227},{32,64},{33,1},{34,66},{35,3},{64,96... | collective-permute-start | bytes 786440 | tf_op jit(solution)/shard_map/ppermute | solution.py:314
  80.3 6.0 %collective-permute-done.8.refs_7_ = bf16[512,128]{1,0:T(8,128)(2,1)S(1)} collective-permute-done((bf16[512,128]{1,0:T(8,128)(2,1)S(1)}, bf16[512,128]{1,0:T(8,128)(2,1)S(1)}, u32[]{:S(2)}, u32[]{:S(2)}) %collective-permute-start.8) | collective-permute-done | bytes 131104 | tf_op jit(solution)/shard_map/ppermute | solution.py:314
  86.3 0.1 collective-permute-start.9
  86.4 0.1 add_convert_fusion.3
  86.5 2.7 %collective-permute-start.5 = (bf16[1024,128]{1,0:T(8,128)(2,1)S(1)}, bf16[1024,128]{1,0:T(8,128)(2,1)S(1)}, u32[]{:S(2)}, u32[]{:S(2)}) collective-permute-start(bf16[1024,128]{1,0:T(8,128)(2,1)S(1)} %add_convert_fusion.3), channel_id=1, source_target_pairs={{0,32},{1,225},{2,34},{3,227},{32,64},{33,1},{34,66},{35,3},{64,96... | collective-permute-start | bytes 786440 | tf_op jit(solution)/shard_map/ppermute | solution.py:314
  89.2 3.6 %collective-permute-done.9.refs_6_ = bf16[1024,128]{1,0:T(8,128)(2,1)S(1)} collective-permute-done((bf16[1024,128]{1,0:T(8,128)(2,1)S(1)}, bf16[1024,128]{1,0:T(8,128)(2,1)S(1)}, u32[]{:S(2)}, u32[]{:S(2)}) %collective-permute-start.9) | collective-permute-done | bytes 262176 | tf_op jit(solution)/shard_map/ppermute | solution.py:314
  92.8 0.1 add_convert_fusion.1
  92.9 0.3 collective-permute-start.10
  93.2 2.2 collective-permute-done.5.refs_3_
  95.4 0.1 add_convert_fusion.2
  95.4 3.4 %collective-permute-start.6 = (bf16[1024,128]{1,0:T(8,128)(2,1)S(1)}, bf16[1024,128]{1,0:T(8,128)(2,1)S(1)}, u32[]{:S(2)}, u32[]{:S(2)}) collective-permute-start(bf16[1024,128]{1,0:T(8,128)(2,1)S(1)} %add_convert_fusion.2), channel_id=1, source_target_pairs={{0,32},{1,225},{2,34},{3,227},{32,64},{33,1},{34,66},{35,3},{64,96... | collective-permute-start | bytes 786440 | tf_op jit(solution)/shard_map/ppermute | solution.py:314
  98.9 0.7 collective-permute-done.10.refs_5_
  99.6 0.1 collective-permute-start.11
  99.7 4.2 %collective-permute-done.6.refs_4_ = bf16[1024,128]{1,0:T(8,128)(2,1)S(1)} collective-permute-done((bf16[1024,128]{1,0:T(8,128)(2,1)S(1)}, bf16[1024,128]{1,0:T(8,128)(2,1)S(1)}, u32[]{:S(2)}, u32[]{:S(2)}) %collective-permute-start.6) | collective-permute-done | bytes 262176 | tf_op jit(solution)/shard_map/ppermute | solution.py:314
  104.0 3.5 %collective-permute-start.7 = (bf16[512,128]{1,0:T(8,128)(2,1)S(1)}, bf16[512,128]{1,0:T(8,128)(2,1)S(1)}, u32[]{:S(2)}, u32[]{:S(2)}) collective-permute-start(bf16[512,128]{1,0:T(8,128)(2,1)S(1)} %add_convert_fusion.5), channel_id=1, source_target_pairs={{0,32},{1,225},{2,34},{3,227},{32,64},{33,1},{34,66},{35,3},{64,96... | collective-permute-start | bytes 393224 | tf_op jit(solution)/shard_map/ppermute | solution.py:314
  107.5 1.9 collective-permute-done.7.refs_3_
  109.4 1.4 grid1.1.refs_0_
  110.8 2.0 spread0.1
  112.8 3.6 %all-to-all-start.2 = ((bf16[8,8,128,128]{3,2,1,0:T(8,128)(2,1)}), bf16[8,8,128,128]{3,2,1,0:T(8,128)(2,1)S(1)}, u32[]{:S(2)}, u32[]{:S(2)}) async-start(bf16[8,8,128,128]{3,2,1,0:T(8,128)(2,1)} %spread0.1), calls=%async_computation.2 | async-start | bytes 4194304 | tf_op jit(solution)/shard_map/all_to_all | solution.py:358
  116.4 3.2 %collective-permute-start.12 = (bf16[512,128]{1,0:T(8,128)(2,1)S(1)}, bf16[512,128]{1,0:T(8,128)(2,1)S(1)}, u32[]{:S(2)}, u32[]{:S(2)}) collective-permute-start(bf16[512,128]{1,0:T(8,128)(2,1)S(1)} %grid1.1.refs_0_), channel_id=1, source_target_pairs={{0,32},{1,225},{2,34},{3,227},{32,64},{33,1},{34,66},{35,3},{64,96... | collective-permute-start | bytes 393224 | tf_op jit(solution)/shard_map/ppermute | solution.py:314
  119.6 1.9 collective-permute-done.12.refs_1_
  121.5 3.1 %collective-permute-start.13 = (bf16[512,128]{1,0:T(8,128)(2,1)S(1)}, bf16[512,128]{1,0:T(8,128)(2,1)S(1)}, u32[]{:S(2)}, u32[]{:S(2)}) collective-permute-start(bf16[512,128]{1,0:T(8,128)(2,1)S(1)} %collective-permute-done.12.refs_1_), channel_id=1, source_target_pairs={{0,32},{1,225},{2,34},{3,227},{32,64},{33,1},{34,66},{35,3},{64,96... | collective-permute-start | bytes 393224 | tf_op jit(solution)/shard_map/ppermute | solution.py:314
  124.6 1.9 collective-permute-done.13.refs_2_
  126.6 3.4 %collective-permute-start.14 = (bf16[512,128]{1,0:T(8,128)(2,1)S(1)}, bf16[512,128]{1,0:T(8,128)(2,1)S(1)}, u32[]{:S(2)}, u32[]{:S(2)}) collective-permute-start(bf16[512,128]{1,0:T(8,128)(2,1)S(1)} %collective-permute-done.13.refs_2_), channel_id=1, source_target_pairs={{0,32},{1,225},{2,34},{3,227},{32,64},{33,1},{34,66},{35,3},{64,96... | collective-permute-start | bytes 393224 | tf_op jit(solution)/shard_map/ppermute | solution.py:314
  129.9 1.9 collective-permute-done.14.refs_3_
  131.9 3.4 %collective-permute-start.15 = (bf16[512,128]{1,0:T(8,128)(2,1)S(1)}, bf16[512,128]{1,0:T(8,128)(2,1)S(1)}, u32[]{:S(2)}, u32[]{:S(2)}) collective-permute-start(bf16[512,128]{1,0:T(8,128)(2,1)S(1)} %collective-permute-done.14.refs_3_), channel_id=1, source_target_pairs={{0,32},{1,225},{2,34},{3,227},{32,64},{33,1},{34,66},{35,3},{64,96... | collective-permute-start | bytes 393224 | tf_op jit(solution)/shard_map/ppermute | solution.py:314
  135.3 0.7 collective-permute-done.18.refs_5_
  135.9 1.3 collective-permute-done.15.refs_4_
  137.2 2.0 spread1.1
  139.3 6.1 %all-to-all-start.3 = ((bf16[8,8,128,128]{3,2,1,0:T(8,128)(2,1)}), bf16[8,8,128,128]{3,2,1,0:T(8,128)(2,1)}, u32[]{:S(2)}, u32[]{:S(2)}) async-start(bf16[8,8,128,128]{3,2,1,0:T(8,128)(2,1)} %spread1.1), calls=%async_computation.3 | async-start | bytes 4194304 | tf_op jit(solution)/shard_map/all_to_all | solution.py:358
  145.5 5.1 %accum0.1 = (bf16[2048,128]{1,0:T(8,128)(2,1)S(1)}, bf16[2048,128]{1,0:T(8,128)(2,1)}, bf16[2048,128]{1,0:T(8,128)(2,1)}, bf16[2048,128]{1,0:T(8,128)(2,1)}) custom-call(s32[4]{0:T(128)S(1)} %pad_add_fusion.refs_0_.place, s32[64]{0:T(128)S(1)} %bitcast.27, bf16[8,8,128,128]{3,2,1,0:T(8,128)(2,1)S(1)} %all-to-all-done.2.returned, bf16[128,256]{1,0:T(8,128)(2,1)S(1)} %copy-done.3), custom_call_target="tpu_custom_call" | custom-call | bytes 17500000 | tf_op jit(solution)/shard_map/accum0/pallas_call | solution.py:380
  150.6 0.8 copy-done.1
  151.4 10.5 %collective-permute-start.19 = (bf16[2048,128]{1,0:T(8,128)(2,1)}, bf16[2048,128]{1,0:T(8,128)(2,1)S(1)}, u32[]{:S(2)}, u32[]{:S(2)}) collective-permute-start(bf16[2048,128]{1,0:T(8,128)(2,1)} %get-tuple-element.65), channel_id=1, source_target_pairs={{0,1},{1,0},{2,3},{3,2},{4,5},{5,4},{6,7},{7,6},{8,9},{9,8},{10,11... | collective-permute-start | bytes 1572872 | tf_op jit(solution)/shard_map/ppermute | solution.py:318
  161.9 2.5 %collective-permute-start.20 = (bf16[2048,128]{1,0:T(8,128)(2,1)}, bf16[2048,128]{1,0:T(8,128)(2,1)S(1)}, u32[]{:S(2)}, u32[]{:S(2)}) collective-permute-start(bf16[2048,128]{1,0:T(8,128)(2,1)} %get-tuple-element.66), channel_id=1, source_target_pairs={{0,2},{1,3},{2,0},{3,1},{4,6},{5,7},{6,4},{7,5},{8,10},{9,11},{10,... | collective-permute-start | bytes 1572872 | tf_op jit(solution)/shard_map/ppermute | solution.py:318
  164.3 0.7 collective-permute-start.21
  165.0 4.4 %accum1.1 = (bf16[2048,128]{1,0:T(8,128)(2,1)S(1)}, bf16[2048,128]{1,0:T(8,128)(2,1)S(1)}, bf16[2048,128]{1,0:T(8,128)(2,1)S(1)}, bf16[2048,128]{1,0:T(8,128)(2,1)S(1)}) custom-call(s32[4]{0:T(128)S(1)} %pad_add_fusion.refs_0_.place, s32[64]{0:T(128)S(1)} %bitcast.28, bf16[8,8,128,128]{3,2,1,0:T(8,128)(2,1)} %all-to-all-done.3.returned, ...), custom_call_target="tpu_custom_call" | custom-call | bytes 17500000 | tf_op jit(solution)/shard_map/accum1/pallas_call | solution.py:380
  169.5 12.5 %collective-permute-start.22 = (bf16[2048,128]{1,0:T(8,128)(2,1)S(1)}, bf16[2048,128]{1,0:T(8,128)(2,1)S(1)}, u32[]{:S(2)}, u32[]{:S(2)}) collective-permute-start(bf16[2048,128]{1,0:T(8,128)(2,1)S(1)} %get-tuple-element.70), channel_id=1, source_target_pairs={{0,1},{1,0},{2,3},{3,2},{4,5},{5,4},{6,7},{7,6},{8,9},{9,8},{10,11... | collective-permute-start | bytes 1572872 | tf_op jit(solution)/shard_map/ppermute | solution.py:318
  182.0 3.2 %collective-permute-start.23 = (bf16[2048,128]{1,0:T(8,128)(2,1)S(1)}, bf16[2048,128]{1,0:T(8,128)(2,1)S(1)}, u32[]{:S(2)}, u32[]{:S(2)}) collective-permute-start(bf16[2048,128]{1,0:T(8,128)(2,1)S(1)} %get-tuple-element.71), channel_id=1, source_target_pairs={{0,2},{1,3},{2,0},{3,1},{4,6},{5,7},{6,4},{7,5},{8,10},{9,11},{10,... | collective-permute-start | bytes 1572872 | tf_op jit(solution)/shard_map/ppermute | solution.py:318
  185.2 0.1 collective-permute-start.24
  185.3 16.7 %collective-permute-done.21.refs_5_ = bf16[2048,128]{1,0:T(8,128)(2,1)S(1)} collective-permute-done((bf16[2048,128]{1,0:T(8,128)(2,1)}, bf16[2048,128]{1,0:T(8,128)(2,1)S(1)}, u32[]{:S(2)}, u32[]{:S(2)}) %collective-permute-start.21) | collective-permute-done | bytes 524320 | tf_op jit(solution)/shard_map/ppermute | solution.py:318
  202.0 4.4 %half.1.refs_2_ = f32[2048,512]{1,0:T(8,128)S(1)} custom-call(s32[4]{0:T(128)S(1)} %pad_add_fusion.refs_0_.place, bf16[2,4,128,512]{3,2,1,0:T(8,128)(2,1)S(1)} %bitcast.21, bf16[2048,128]{1,0:T(8,128)(2,1)S(1)} %copy-done.2, bf16[2048,128]{1,0:T(8,128)(2,1)S(1)} %collective-permute-done.19.refs_3_, bf16[2048,128]{1,0:T(8,128)(2,1)S(1)} %collective-permute-done.20.refs_4_, ...), custom_call_target="tpu_custom_call" | custom-call | bytes 14000000 | tf_op jit(solution)/shard_map/half/pallas_call | solution.py:444
  206.4 11.2 %collective-permute-done.24.refs_4_ = bf16[2048,128]{1,0:T(8,128)(2,1)S(1)} collective-permute-done((bf16[2048,128]{1,0:T(8,128)(2,1)S(1)}, bf16[2048,128]{1,0:T(8,128)(2,1)S(1)}, u32[]{:S(2)}, u32[]{:S(2)}) %collective-permute-start.24) | collective-permute-done | bytes 524320 | tf_op jit(solution)/shard_map/ppermute | solution.py:318
  217.6 3.4 %finish.1 = bf16[2,2048,256]{2,1,0:T(8,128)(2,1)} custom-call(s32[4]{0:T(128)S(1)} %pad_add_fusion.refs_0_.place, bf16[2,4,128,512]{3,2,1,0:T(8,128)(2,1)S(1)} %bitcast.22, f32[2048,512]{1,0:T(8,128)S(1)} %half.1.refs_2_, bf16[2048,128]{1,0:T(8,128)(2,1)S(1)} %collective-permute-done.23.refs_3_, bf16[2048,128]{1,0:T(8,128)(2,1)S(1)} %collective-permute-done.24.refs_4_), custom_call_target="tpu_custom_call" | custom-call | bytes 14000000 | tf_op jit(solution)/shard_map/finish/pallas_call | solution.py:454
  (42 shorter events, 0.2 us)
Async XLA Ops:
  7.4 7.5 %copy-start.10 = (s32[4,128]{1,0:T(4,128)S(1)}, s32[4,128]{1,0:T(4,128)}, u32[]{:S(2)}) copy-start(s32[4,128]{1,0:T(4,128)} %param.14) | copy-start | bytes 6148
  7.4 34.5 %all-to-all-start = ((bf16[16,4,128,128]{3,2,1,0:T(8,128)(2,1)}), bf16[16,4,128,128]{3,2,1,0:T(8,128)(2,1)}, u32[]{:S(2)}, u32[]{:S(2)}) async-start(bf16[16,4,128,128]{3,2,1,0:T(8,128)(2,1)} %contrib0.1), calls=%async_computation | async-start | bytes 4194304 | tf_op jit(solution)/shard_map/all_to_all | solution.py:358
  14.9 7.9 %copy-start.6 = (f32[32,512]{1,0:T(8,128)S(1)}, f32[32,512]{1,0:T(8,128)}, u32[]{:S(2)}) copy-start(f32[32,512]{1,0:T(8,128)} %constant.62.clone) | copy-start | bytes 196612
  14.9 7.9 %copy-start.7 = (f32[32,512]{1,0:T(8,128)S(1)}, f32[32,512]{1,0:T(8,128)}, u32[]{:S(2)}) copy-start(f32[32,512]{1,0:T(8,128)} %constant.61.clone) | copy-start | bytes 196612
  14.9 7.9 %copy-start.8 = (f32[16,512]{1,0:T(8,128)S(1)}, f32[16,512]{1,0:T(8,128)}, u32[]{:S(2)}) copy-start(f32[16,512]{1,0:T(8,128)} %constant.64.clone) | copy-start | bytes 98308
  14.9 7.9 %copy-start.9 = (f32[16,512]{1,0:T(8,128)S(1)}, f32[16,512]{1,0:T(8,128)}, u32[]{:S(2)}) copy-start(f32[16,512]{1,0:T(8,128)} %constant.63.clone) | copy-start | bytes 98308
  41.9 4.6 %copy-start.4 = (s32[64]{0:T(128)S(1)}, s32[64]{0:T(128)}, u32[]{:S(2)}) copy-start(s32[64]{0:T(128)} %offsets.3) | copy-start | bytes 772
  41.9 30.6 %all-to-all-start.1 = ((bf16[8,8,128,128]{3,2,1,0:T(8,128)(2,1)}), bf16[8,8,128,128]{3,2,1,0:T(8,128)(2,1)}, u32[]{:S(2)}, u32[]{:S(2)}) async-start(bf16[8,8,128,128]{3,2,1,0:T(8,128)(2,1)} %contrib1.1), calls=%async_computation.1 | async-start | bytes 4194304 | tf_op jit(solution)/shard_map/all_to_all | solution.py:358
  46.4 21.1 %copy-start = (bf16[1,2,512,128]{3,2,1,0:T(8,128)(2,1)S(1)}, bf16[1,2,512,128]{3,2,1,0:T(8,128)(2,1)}, u32[]{:S(2)}) copy-start(bf16[1,2,512,128]{3,2,1,0:T(8,128)(2,1)} %param.15) | copy-start | bytes 786436
  48.8 9.7 %collective-permute-start = (bf16[512,128]{1,0:T(8,128)(2,1)S(1)}, bf16[512,128]{1,0:T(8,128)(2,1)S(1)}, u32[]{:S(2)}, u32[]{:S(2)}) collective-permute-start(bf16[512,128]{1,0:T(8,128)(2,1)S(1)} %get-tuple-element.49), channel_id=1, source_target_pairs={{0,128},{64,192},{128,0},{192,64},{1,129},{65,193},{129,1},{193,65... | collective-permute-start | bytes 393224 | tf_op jit(solution)/shard_map/ppermute | solution.py:304
  55.0 9.8 %collective-permute-start.1 = (bf16[512,128]{1,0:T(8,128)(2,1)S(1)}, bf16[512,128]{1,0:T(8,128)(2,1)S(1)}, u32[]{:S(2)}, u32[]{:S(2)}) collective-permute-start(bf16[512,128]{1,0:T(8,128)(2,1)S(1)} %get-tuple-element.50), channel_id=1, source_target_pairs={{0,64},{64,128},{128,192},{192,0},{1,65},{65,129},{129,193},{193,1... | collective-permute-start | bytes 393224 | tf_op jit(solution)/shard_map/ppermute | solution.py:304
  56.1 11.4 %collective-permute-start.2 = (bf16[512,128]{1,0:T(8,128)(2,1)S(1)}, bf16[512,128]{1,0:T(8,128)(2,1)S(1)}, u32[]{:S(2)}, u32[]{:S(2)}) collective-permute-start(bf16[512,128]{1,0:T(8,128)(2,1)S(1)} %get-tuple-element.51), channel_id=1, source_target_pairs={{0,192},{64,0},{128,64},{192,128},{1,193},{65,1},{129,65},{193,129... | collective-permute-start | bytes 393224 | tf_op jit(solution)/shard_map/ppermute | solution.py:304
  68.9 6.0 %collective-permute-start.3 = (bf16[512,128]{1,0:T(8,128)(2,1)S(1)}, bf16[512,128]{1,0:T(8,128)(2,1)S(1)}, u32[]{:S(2)}, u32[]{:S(2)}) collective-permute-start(bf16[512,128]{1,0:T(8,128)(2,1)S(1)} %grid0.1.refs_0_), channel_id=1, source_target_pairs={{0,32},{1,225},{2,34},{3,227},{32,64},{33,1},{34,66},{35,3},{64,96... | collective-permute-start | bytes 393224 | tf_op jit(solution)/shard_map/ppermute | solution.py:314
  74.9 11.5 %collective-permute-start.4 = (bf16[1024,128]{1,0:T(8,128)(2,1)S(1)}, bf16[1024,128]{1,0:T(8,128)(2,1)S(1)}, u32[]{:S(2)}, u32[]{:S(2)}) collective-permute-start(bf16[1024,128]{1,0:T(8,128)(2,1)S(1)} %pad_maximum_fusion.1), channel_id=1, source_target_pairs={{0,32},{1,225},{2,34},{3,227},{32,64},{33,1},{34,66},{35,3},{64,96... | collective-permute-start | bytes 786440 | tf_op jit(solution)/shard_map/ppermute | solution.py:314
  80.3 6.0 %collective-permute-start.8 = (bf16[512,128]{1,0:T(8,128)(2,1)S(1)}, bf16[512,128]{1,0:T(8,128)(2,1)S(1)}, u32[]{:S(2)}, u32[]{:S(2)}) collective-permute-start(bf16[512,128]{1,0:T(8,128)(2,1)S(1)} %grid0.1.refs_0_), channel_id=1, source_target_pairs={{0,224},{1,33},{2,226},{3,35},{32,0},{33,65},{34,2},{35,67},{64,32... | collective-permute-start | bytes 393224 | tf_op jit(solution)/shard_map/ppermute | solution.py:314
  86.3 6.5 %collective-permute-start.9 = (bf16[1024,128]{1,0:T(8,128)(2,1)S(1)}, bf16[1024,128]{1,0:T(8,128)(2,1)S(1)}, u32[]{:S(2)}, u32[]{:S(2)}) collective-permute-start(bf16[1024,128]{1,0:T(8,128)(2,1)S(1)} %pad_maximum_fusion.2), channel_id=1, source_target_pairs={{0,224},{1,33},{2,226},{3,35},{32,0},{33,65},{34,2},{35,67},{64,32... | collective-permute-start | bytes 786440 | tf_op jit(solution)/shard_map/ppermute | solution.py:314
  86.5 8.9 %collective-permute-start.5 = (bf16[1024,128]{1,0:T(8,128)(2,1)S(1)}, bf16[1024,128]{1,0:T(8,128)(2,1)S(1)}, u32[]{:S(2)}, u32[]{:S(2)}) collective-permute-start(bf16[1024,128]{1,0:T(8,128)(2,1)S(1)} %add_convert_fusion.3), channel_id=1, source_target_pairs={{0,32},{1,225},{2,34},{3,227},{32,64},{33,1},{34,66},{35,3},{64,96... | collective-permute-start | bytes 786440 | tf_op jit(solution)/shard_map/ppermute | solution.py:314
  92.9 6.7 %collective-permute-start.10 = (bf16[1024,128]{1,0:T(8,128)(2,1)S(1)}, bf16[1024,128]{1,0:T(8,128)(2,1)S(1)}, u32[]{:S(2)}, u32[]{:S(2)}) collective-permute-start(bf16[1024,128]{1,0:T(8,128)(2,1)S(1)} %add_convert_fusion.1), channel_id=1, source_target_pairs={{0,224},{1,33},{2,226},{3,35},{32,0},{33,65},{34,2},{35,67},{64,32... | collective-permute-start | bytes 786440 | tf_op jit(solution)/shard_map/ppermute | solution.py:314
  95.4 8.5 %collective-permute-start.6 = (bf16[1024,128]{1,0:T(8,128)(2,1)S(1)}, bf16[1024,128]{1,0:T(8,128)(2,1)S(1)}, u32[]{:S(2)}, u32[]{:S(2)}) collective-permute-start(bf16[1024,128]{1,0:T(8,128)(2,1)S(1)} %add_convert_fusion.2), channel_id=1, source_target_pairs={{0,32},{1,225},{2,34},{3,227},{32,64},{33,1},{34,66},{35,3},{64,96... | collective-permute-start | bytes 786440 | tf_op jit(solution)/shard_map/ppermute | solution.py:314
  99.6 7.8 %collective-permute-start.11 = (bf16[512,128]{1,0:T(8,128)(2,1)S(1)}, bf16[512,128]{1,0:T(8,128)(2,1)S(1)}, u32[]{:S(2)}, u32[]{:S(2)}) collective-permute-start(bf16[512,128]{1,0:T(8,128)(2,1)S(1)} %add_convert_fusion.4), channel_id=1, source_target_pairs={{0,224},{1,33},{2,226},{3,35},{32,0},{33,65},{34,2},{35,67},{64,32... | collective-permute-start | bytes 393224 | tf_op jit(solution)/shard_map/ppermute | solution.py:314
  104.0 5.4 %collective-permute-start.7 = (bf16[512,128]{1,0:T(8,128)(2,1)S(1)}, bf16[512,128]{1,0:T(8,128)(2,1)S(1)}, u32[]{:S(2)}, u32[]{:S(2)}) collective-permute-start(bf16[512,128]{1,0:T(8,128)(2,1)S(1)} %add_convert_fusion.5), channel_id=1, source_target_pairs={{0,32},{1,225},{2,34},{3,227},{32,64},{33,1},{34,66},{35,3},{64,96... | collective-permute-start | bytes 393224 | tf_op jit(solution)/shard_map/ppermute | solution.py:314
  112.8 26.5 %all-to-all-start.2 = ((bf16[8,8,128,128]{3,2,1,0:T(8,128)(2,1)}), bf16[8,8,128,128]{3,2,1,0:T(8,128)(2,1)S(1)}, u32[]{:S(2)}, u32[]{:S(2)}) async-start(bf16[8,8,128,128]{3,2,1,0:T(8,128)(2,1)} %spread0.1), calls=%async_computation.2 | async-start | bytes 4194304 | tf_op jit(solution)/shard_map/all_to_all | solution.py:358
  116.4 5.1 %collective-permute-start.12 = (bf16[512,128]{1,0:T(8,128)(2,1)S(1)}, bf16[512,128]{1,0:T(8,128)(2,1)S(1)}, u32[]{:S(2)}, u32[]{:S(2)}) collective-permute-start(bf16[512,128]{1,0:T(8,128)(2,1)S(1)} %grid1.1.refs_0_), channel_id=1, source_target_pairs={{0,32},{1,225},{2,34},{3,227},{32,64},{33,1},{34,66},{35,3},{64,96... | collective-permute-start | bytes 393224 | tf_op jit(solution)/shard_map/ppermute | solution.py:314
  119.6 5.0 %collective-permute-start.16 = (bf16[512,128]{1,0:T(8,128)(2,1)S(1)}, bf16[512,128]{1,0:T(8,128)(2,1)S(1)}, u32[]{:S(2)}, u32[]{:S(2)}) collective-permute-start(bf16[512,128]{1,0:T(8,128)(2,1)S(1)} %grid1.1.refs_0_), channel_id=1, source_target_pairs={{0,224},{1,33},{2,226},{3,35},{32,0},{33,65},{34,2},{35,67},{64,32... | collective-permute-start | bytes 393224 | tf_op jit(solution)/shard_map/ppermute | solution.py:314
  121.5 5.0 %collective-permute-start.13 = (bf16[512,128]{1,0:T(8,128)(2,1)S(1)}, bf16[512,128]{1,0:T(8,128)(2,1)S(1)}, u32[]{:S(2)}, u32[]{:S(2)}) collective-permute-start(bf16[512,128]{1,0:T(8,128)(2,1)S(1)} %collective-permute-done.12.refs_1_), channel_id=1, source_target_pairs={{0,32},{1,225},{2,34},{3,227},{32,64},{33,1},{34,66},{35,3},{64,96... | collective-permute-start | bytes 393224 | tf_op jit(solution)/shard_map/ppermute | solution.py:314
  124.6 5.3 %collective-permute-start.17 = (bf16[512,128]{1,0:T(8,128)(2,1)S(1)}, bf16[512,128]{1,0:T(8,128)(2,1)S(1)}, u32[]{:S(2)}, u32[]{:S(2)}) collective-permute-start(bf16[512,128]{1,0:T(8,128)(2,1)S(1)} %collective-permute-done.16.refs_7_), channel_id=1, source_target_pairs={{0,224},{1,33},{2,226},{3,35},{32,0},{33,65},{34,2},{35,67},{64,32... | collective-permute-start | bytes 393224 | tf_op jit(solution)/shard_map/ppermute | solution.py:314
  126.6 5.3 %collective-permute-start.14 = (bf16[512,128]{1,0:T(8,128)(2,1)S(1)}, bf16[512,128]{1,0:T(8,128)(2,1)S(1)}, u32[]{:S(2)}, u32[]{:S(2)}) collective-permute-start(bf16[512,128]{1,0:T(8,128)(2,1)S(1)} %collective-permute-done.13.refs_2_), channel_id=1, source_target_pairs={{0,32},{1,225},{2,34},{3,227},{32,64},{33,1},{34,66},{35,3},{64,96... | collective-permute-start | bytes 393224 | tf_op jit(solution)/shard_map/ppermute | solution.py:314
  129.9 6.0 %collective-permute-start.18 = (bf16[512,128]{1,0:T(8,128)(2,1)S(1)}, bf16[512,128]{1,0:T(8,128)(2,1)S(1)}, u32[]{:S(2)}, u32[]{:S(2)}) collective-permute-start(bf16[512,128]{1,0:T(8,128)(2,1)S(1)} %collective-permute-done.17.refs_6_), channel_id=1, source_target_pairs={{0,224},{1,33},{2,226},{3,35},{32,0},{33,65},{34,2},{35,67},{64,32... | collective-permute-start | bytes 393224 | tf_op jit(solution)/shard_map/ppermute | solution.py:314
  131.9 5.3 %collective-permute-start.15 = (bf16[512,128]{1,0:T(8,128)(2,1)S(1)}, bf16[512,128]{1,0:T(8,128)(2,1)S(1)}, u32[]{:S(2)}, u32[]{:S(2)}) collective-permute-start(bf16[512,128]{1,0:T(8,128)(2,1)S(1)} %collective-permute-done.14.refs_3_), channel_id=1, source_target_pairs={{0,32},{1,225},{2,34},{3,227},{32,64},{33,1},{34,66},{35,3},{64,96... | collective-permute-start | bytes 393224 | tf_op jit(solution)/shard_map/ppermute | solution.py:314
  139.3 6.2 %copy-start.3 = (bf16[128,256]{1,0:T(8,128)(2,1)S(1)}, bf16[128,256]{1,0:T(8,128)(2,1)}, u32[]{:S(2)}) copy-start(bf16[128,256]{1,0:T(8,128)(2,1)} %constant.66.clone.table) | copy-start | bytes 196612
  139.3 6.2 %copy-start.5 = (s32[64,1]{0,1:T(1,128)S(1)}, s32[64,1]{0,1:T(1,128)}, u32[]{:S(2)}) copy-start(s32[64,1]{0,1:T(1,128)} %param.12) | copy-start | bytes 772
  139.3 25.7 %all-to-all-start.3 = ((bf16[8,8,128,128]{3,2,1,0:T(8,128)(2,1)}), bf16[8,8,128,128]{3,2,1,0:T(8,128)(2,1)}, u32[]{:S(2)}, u32[]{:S(2)}) async-start(bf16[8,8,128,128]{3,2,1,0:T(8,128)(2,1)} %spread1.1), calls=%async_computation.3 | async-start | bytes 4194304 | tf_op jit(solution)/shard_map/all_to_all | solution.py:358
  150.6 0.8 copy-start.1
  151.4 50.6 %copy-start.2 = (bf16[2048,128]{1,0:T(8,128)(2,1)S(1)}, bf16[2048,128]{1,0:T(8,128)(2,1)}, u32[]{:S(2)}) copy-start(bf16[2048,128]{1,0:T(8,128)(2,1)} %copy-done.1) | copy-start | bytes 1572868
  151.4 33.8 %collective-permute-start.19 = (bf16[2048,128]{1,0:T(8,128)(2,1)}, bf16[2048,128]{1,0:T(8,128)(2,1)S(1)}, u32[]{:S(2)}, u32[]{:S(2)}) collective-permute-start(bf16[2048,128]{1,0:T(8,128)(2,1)} %get-tuple-element.65), channel_id=1, source_target_pairs={{0,1},{1,0},{2,3},{3,2},{4,5},{5,4},{6,7},{7,6},{8,9},{9,8},{10,11... | collective-permute-start | bytes 1572872 | tf_op jit(solution)/shard_map/ppermute | solution.py:318
  161.9 23.4 %collective-permute-start.20 = (bf16[2048,128]{1,0:T(8,128)(2,1)}, bf16[2048,128]{1,0:T(8,128)(2,1)S(1)}, u32[]{:S(2)}, u32[]{:S(2)}) collective-permute-start(bf16[2048,128]{1,0:T(8,128)(2,1)} %get-tuple-element.66), channel_id=1, source_target_pairs={{0,2},{1,3},{2,0},{3,1},{4,6},{5,7},{6,4},{7,5},{8,10},{9,11},{10,... | collective-permute-start | bytes 1572872 | tf_op jit(solution)/shard_map/ppermute | solution.py:318
  164.3 37.6 %collective-permute-start.21 = (bf16[2048,128]{1,0:T(8,128)(2,1)}, bf16[2048,128]{1,0:T(8,128)(2,1)S(1)}, u32[]{:S(2)}, u32[]{:S(2)}) collective-permute-start(bf16[2048,128]{1,0:T(8,128)(2,1)} %get-tuple-element.67), channel_id=1, source_target_pairs={{0,3},{1,2},{2,1},{3,0},{4,7},{5,6},{6,5},{7,4},{8,11},{9,10},{10,... | collective-permute-start | bytes 1572872 | tf_op jit(solution)/shard_map/ppermute | solution.py:318
  169.5 32.5 %collective-permute-start.22 = (bf16[2048,128]{1,0:T(8,128)(2,1)S(1)}, bf16[2048,128]{1,0:T(8,128)(2,1)S(1)}, u32[]{:S(2)}, u32[]{:S(2)}) collective-permute-start(bf16[2048,128]{1,0:T(8,128)(2,1)S(1)} %get-tuple-element.70), channel_id=1, source_target_pairs={{0,1},{1,0},{2,3},{3,2},{4,5},{5,4},{6,7},{7,6},{8,9},{9,8},{10,11... | collective-permute-start | bytes 1572872 | tf_op jit(solution)/shard_map/ppermute | solution.py:318
  182.0 24.4 %collective-permute-start.23 = (bf16[2048,128]{1,0:T(8,128)(2,1)S(1)}, bf16[2048,128]{1,0:T(8,128)(2,1)S(1)}, u32[]{:S(2)}, u32[]{:S(2)}) collective-permute-start(bf16[2048,128]{1,0:T(8,128)(2,1)S(1)} %get-tuple-element.71), channel_id=1, source_target_pairs={{0,2},{1,3},{2,0},{3,1},{4,6},{5,7},{6,4},{7,5},{8,10},{9,11},{10,... | collective-permute-start | bytes 1572872 | tf_op jit(solution)/shard_map/ppermute | solution.py:318
  185.2 32.4 %collective-permute-start.24 = (bf16[2048,128]{1,0:T(8,128)(2,1)S(1)}, bf16[2048,128]{1,0:T(8,128)(2,1)S(1)}, u32[]{:S(2)}, u32[]{:S(2)}) collective-permute-start(bf16[2048,128]{1,0:T(8,128)(2,1)S(1)} %get-tuple-element.72), channel_id=1, source_target_pairs={{0,3},{1,2},{2,1},{3,0},{4,7},{5,6},{6,5},{7,4},{8,11},{9,10},{10,... | collective-permute-start | bytes 1572872 | tf_op jit(solution)/shard_map/ppermute | solution.py:318

commit v4 on v3

--- a/solution.py
+++ b/solution.py
@@ -131,16 +131,17 @@
         send(k).start()
         return 0
 
-    lax.fori_loop(0, depth, one_group, 0, unroll=2)
+    lax.fori_loop(0, depth, one_group, 0, unroll=4)
     for k in range(depth):
         send(k).wait()
 
 
-def gather_kernel(chunk, place, offsets, arrived, *refs):
+def gather_kernel(chunk, ks, place, offsets, arrived, *refs):
     *outs, held, total, sems = refs
     planes, depth = arrived.shape[0], arrived.shape[1]
     grid_len = total.shape[0] - XM
-    owners = [lax.rem(place[chunk] + k * (1 if chunk == 0 else place[3]), depth) for k in range(depth)]
+    stride = 1 if chunk == 0 else place[3]
+    owners = [lax.rem(place[chunk] + k * stride, depth) for k in ks]
 
     def fetch(owner):
         return pltpu.make_async_copy(arrived.at[:, owner], held.at[:, owner], sems.at[owner])
@@ -357,12 +358,13 @@
     def near(c, value):
         return lax.all_to_all(value, NEAR[c], 0, 0, tiled=True)
 
-    def gather(c, arrived, doubled):
-        outs = [(grid_len * (1 + (k in doubled)), LANES) for k in range(depths[c])]
-        return call(
-            bind(gather_kernel, c), f"gather{c}", outs,
-            [SMEM, SMEM, HBM], [held[c], grid_rows, sems[c]], 2, 8,
+    def gather(c, arrived, ks, doubled):
+        outs = [(grid_len * (1 + (k in doubled)), LANES) for k in ks]
+        made = call(
+            lambda *refs: gather_kernel(c, ks, *refs), f"gather{c}{ks[0]}", outs,
+            [SMEM, SMEM, HBM], [held[c], grid_rows, sems[c]], 1, 8,
         )(place, fac_off, arrived)
+        return dict(zip(ks, made))
 
     def image_of(c, parts):
         return call(
@@ -396,13 +398,15 @@
     arrived1 = near(1, payload1)
 
     steps = sorted(range(1, depths[0]), key=lambda k: -min(k, depths[0] - k))
-    parts0 = gather(0, arrived0, ())
+    parts0 = gather(0, arrived0, [*range(depths[0])], ())
     image0 = image_of(0, [parts0[0]] + [shifted(parts0[k], k) for k in steps])
 
     far, near_side = depths[1] // 2, (depths[1] - 1) // 2
     doubled = [*range(2, far), *range(far + 2, depths[1] - 1)]
-    parts1 = gather(1, arrived1, doubled)
-    ups, downs = [turned(image0, 1)], [turned(image0, -1)]
+    first = [far, far + 1]
+    parts1 = gather(1, arrived1, first, ())
+    parts1 |= gather(1, arrived1, [k for k in range(depths[1]) if k not in first], doubled)
+    ups, downs = barrier(([turned(image0, 1)], [turned(image0, -1)]))
     up = jnp.concatenate([ups[0], parts1[far]])
     down = jnp.concatenate([downs[0], parts1[far + 1]])
     for i in range(far - 1):

time: 222 us -> 219 us (0.986)
  waiting for transfers between devices: 82.8 us -> 75.8 us
    all_to_all x4, waiting for transfers between devices: 19.5 us -> 15.4 us  [near(): return lax.all_to_all(value, NEAR[c], 0, 0, tiled=True)]
    pallas_call x2 -> x3, Pallas kernels: 4.62 us -> 4.53 us  [gather(): call(lambda *refs: gather_kernel(c, ks, *refs), f'gather{c}{ks[0]}', outs...]
where the time goes in v4:
time: 219 us; the launch traced here: 218 us
  starting transfers between devices  91.3 us (42%)
  waiting for transfers between devices  75.8 us (35%)
  Pallas kernels  43.4 us (20%)
  other arithmetic  5.42 us (2%)
    ppermute x6, starting transfers between devices, swapped(): lax.ppermute(value, 'col', [(i, i ^ flip) for i in range(lax.axis_size('c...  29.8 us
    ppermute x16, starting transfers between devices, turned(): return lax.ppermute(value, (*FAR[1], 'col'), perm)  29.7 us
    ppermute x6, waiting for transfers between devices, swapped(): lax.ppermute(value, 'col', [(i, i ^ flip) for i in range(lax.axis_size('c...  27.7 us
    ppermute x16, waiting for transfers between devices, turned(): return lax.ppermute(value, (*FAR[1], 'col'), perm)  25.7 us
    all_to_all x4, starting transfers between devices, near(): return lax.all_to_all(value, NEAR[c], 0, 0, tiled=True)  22.1 us
    all_to_all x4, waiting for transfers between devices, near(): return lax.all_to_all(value, NEAR[c], 0, 0, tiled=True)  15.4 us
    pallas_call x2, Pallas kernels, contrib(): call(bind(contrib_kernel, c), f'contrib{c}', [blocks[c]], [SMEM, HBM, VME...  14.4 us
    ppermute x3, starting transfers between devices, shifted(): lax.ppermute(value, 'zq', [(i, (i + step) % size) for i in range(size)])  9.68 us
  transfers between devices with their start and end apart: 29, of which 17 were waited for; matrix products, arithmetic and copies ran while one was open for 2% of the time, Pallas kernels for 13%

profile of v4, /device:TPU:1, one launch (start us, length us, event | category | flops | bytes accessed | tf_op | source)
XLA Modules:
  0.0 218.0 jit_solution(14314436372139601335)
XLA Ops:
  0.0 7.0 %contrib0.1 = bf16[16,4,128,128]{3,2,1,0:T(8,128)(2,1)} custom-call(s32[64]{0:T(128)} %bitcast.25, bf16[2,8192,128]{2,1,0:T(8,128)(2,1)} %bitcast.29, bf16[128,256]{1,0:T(8,128)(2,1)} %constant.65.clone.refs_2_), custom_call_target="tpu_custom_call" | custom-call | bytes 28000000 | tf_op jit(solution)/shard_map/contrib0/pallas_call | solution.py:352
  7.1 7.5 %all-to-all-start = ((bf16[16,4,128,128]{3,2,1,0:T(8,128)(2,1)}), bf16[16,4,128,128]{3,2,1,0:T(8,128)(2,1)}, u32[]{:S(2)}, u32[]{:S(2)}) async-start(bf16[16,4,128,128]{3,2,1,0:T(8,128)(2,1)} %contrib0.1), calls=%async_computation | async-start | bytes 4194304 | tf_op jit(solution)/shard_map/all_to_all | solution.py:359
  14.5 0.1 mul.146
  14.6 7.4 %contrib1.1 = bf16[8,8,128,128]{3,2,1,0:T(8,128)(2,1)} custom-call(s32[64]{0:T(128)} %bitcast.26, bf16[2,8192,128]{2,1,0:T(8,128)(2,1)} %bitcast.30, bf16[128,256]{1,0:T(8,128)(2,1)} %constant.65.clone.refs_2_), custom_call_target="tpu_custom_call" | custom-call | bytes 28000000 | tf_op jit(solution)/shard_map/contrib1/pallas_call | solution.py:352
  22.1 0.4 subtract_convert_fusion
  22.4 1.1 pad_maximum_fusion.refs_1_
  23.6 2.5 %fusion.7 = (bf16[4,2,1,64,256]{4,3,2,0,1:T(8,128)(2,1)S(1)}, bf16[4,2,1,64,256]{4,3,2,0,1:T(8,128)(2,1)S(1)}, bf16[4,2,1,64,256]{4,3,2,0,1:T(8,128)(2,1)S(1)}) fusion(s32[4,2,64]{2,0,1:T(4,128)S(1)} %copy.12), kind=kLoop, calls=%fused_computation.20 | loop fusion | flops 2621440 | bytes 788480 | tf_op jit(solution)/shard_map/concatenate | solution.py:64
  26.1 0.1 maximum_maximum_fusion
  26.2 15.4 %all-to-all-done.refs_2_ = bf16[16,4,128,128]{3,2,1,0:T(8,128)(2,1)} async-done(((bf16[16,4,128,128]{3,2,1,0:T(8,128)(2,1)}), bf16[16,4,128,128]{3,2,1,0:T(8,128)(2,1)}, u32[]{:S(2)}, u32[]{:S(2)}) %all-to-all-start) | async-done | bytes 2097184 | tf_op jit(solution)/shard_map/all_to_all | solution.py:359
  41.6 3.9 %all-to-all-start.1 = ((bf16[8,8,128,128]{3,2,1,0:T(8,128)(2,1)}), bf16[8,8,128,128]{3,2,1,0:T(8,128)(2,1)S(1)}, u32[]{:S(2)}, u32[]{:S(2)}) async-start(bf16[8,8,128,128]{3,2,1,0:T(8,128)(2,1)} %contrib1.1), calls=%async_computation.1 | async-start | bytes 4194304 | tf_op jit(solution)/shard_map/all_to_all | solution.py:359
  45.6 0.1 pad_add_fusion.refs_0_.place
  45.6 2.3 %gather00.1 = (bf16[512,128]{1,0:T(8,128)(2,1)S(1)}, bf16[512,128]{1,0:T(8,128)(2,1)S(1)}, bf16[512,128]{1,0:T(8,128)(2,1)S(1)}, bf16[512,128]{1,0:T(8,128)(2,1)S(1)}) custom-call(s32[4]{0:T(128)S(1)} %pad_add_fusion.refs_0_.place, s32[64]{0:T(128)S(1)} %copy-done.10, bf16[16,4,128,128]{3,2,1,0:T(8,128)(2,1)} %all-to-all-done.refs_2_), custom_call_target="tpu_custom_call" | custom-call | bytes 3500000 | tf_op jit(solution)/shard_map/gather00/pallas_call | solution.py:363
  47.9 6.1 %collective-permute-start = (bf16[512,128]{1,0:T(8,128)(2,1)S(1)}, bf16[512,128]{1,0:T(8,128)(2,1)S(1)}, u32[]{:S(2)}, u32[]{:S(2)}) collective-permute-start(bf16[512,128]{1,0:T(8,128)(2,1)S(1)} %get-tuple-element.51), channel_id=1, source_target_pairs={{0,128},{64,192},{128,0},{192,64},{1,129},{65,193},{129,1},{193,65... | collective-permute-start | bytes 393224 | tf_op jit(solution)/shard_map/ppermute | solution.py:305
  54.0 1.2 collective-permute-start.1
  55.2 2.4 %collective-permute-start.2 = (bf16[512,128]{1,0:T(8,128)(2,1)S(1)}, bf16[512,128]{1,0:T(8,128)(2,1)S(1)}, u32[]{:S(2)}, u32[]{:S(2)}) collective-permute-start(bf16[512,128]{1,0:T(8,128)(2,1)S(1)} %get-tuple-element.53), channel_id=1, source_target_pairs={{0,192},{64,0},{128,64},{192,128},{1,193},{65,1},{129,65},{193,129... | collective-permute-start | bytes 393224 | tf_op jit(solution)/shard_map/ppermute | solution.py:305
  57.6 5.3 %collective-permute-done.1.refs_4_ = bf16[512,128]{1,0:T(8,128)(2,1)S(1)} collective-permute-done((bf16[512,128]{1,0:T(8,128)(2,1)S(1)}, bf16[512,128]{1,0:T(8,128)(2,1)S(1)}, u32[]{:S(2)}, u32[]{:S(2)}) %collective-permute-start.1) | collective-permute-done | bytes 131104 | tf_op jit(solution)/shard_map/ppermute | solution.py:305
  63.0 1.7 collective-permute-done.2.refs_5_
  64.7 1.4 grid0.1.refs_0_
  66.0 3.1 %collective-permute-start.4 = (bf16[512,128]{1,0:T(8,128)(2,1)S(1)}, bf16[512,128]{1,0:T(8,128)(2,1)S(1)}, u32[]{:S(2)}, u32[]{:S(2)}) collective-permute-start(bf16[512,128]{1,0:T(8,128)(2,1)S(1)} %grid0.1.refs_0_), channel_id=1, source_target_pairs={{0,224},{1,33},{2,226},{3,35},{32,0},{33,65},{34,2},{35,67},{64,32... | collective-permute-start | bytes 393224 | tf_op jit(solution)/shard_map/ppermute | solution.py:315
  69.2 0.4 collective-permute-start.3
  69.6 0.7 copy-done.7
  70.3 1.9 collective-permute-done.4.refs_7_
  72.1 1.7 collective-permute-done.3.refs_1_
  73.9 0.9 gather14.1
  74.7 0.9 pad_maximum_fusion.1
  75.7 3.2 %collective-permute-start.5 = (bf16[1024,128]{1,0:T(8,128)(2,1)S(1)}, bf16[1024,128]{1,0:T(8,128)(2,1)S(1)}, u32[]{:S(2)}, u32[]{:S(2)}) collective-permute-start(bf16[1024,128]{1,0:T(8,128)(2,1)S(1)} %pad_maximum_fusion.1), channel_id=1, source_target_pairs={{0,32},{1,225},{2,34},{3,227},{32,64},{33,1},{34,66},{35,3},{64,96... | collective-permute-start | bytes 786440 | tf_op jit(solution)/shard_map/ppermute | solution.py:315
  78.9 0.1 collective-permute-start.9
  79.0 1.4 gather10.1
  80.4 1.8 collective-permute-done.5.refs_2_
  82.3 3.4 %collective-permute-start.6 = (bf16[1024,128]{1,0:T(8,128)(2,1)S(1)}, bf16[1024,128]{1,0:T(8,128)(2,1)S(1)}, u32[]{:S(2)}, u32[]{:S(2)}) collective-permute-start(bf16[1024,128]{1,0:T(8,128)(2,1)S(1)} %add_convert_fusion.3), channel_id=1, source_target_pairs={{0,32},{1,225},{2,34},{3,227},{32,64},{33,1},{34,66},{35,3},{64,96... | collective-permute-start | bytes 786440 | tf_op jit(solution)/shard_map/ppermute | solution.py:315
  85.7 0.7 collective-permute-done.9.refs_6_
  86.5 0.1 collective-permute-start.10
  86.6 3.7 %collective-permute-done.6.refs_3_ = bf16[1024,128]{1,0:T(8,128)(2,1)S(1)} collective-permute-done((bf16[1024,128]{1,0:T(8,128)(2,1)S(1)}, bf16[1024,128]{1,0:T(8,128)(2,1)S(1)}, u32[]{:S(2)}, u32[]{:S(2)}) %collective-permute-start.6) | collective-permute-done | bytes 262176 | tf_op jit(solution)/shard_map/ppermute | solution.py:315
  90.3 3.2 %collective-permute-start.7 = (bf16[1024,128]{1,0:T(8,128)(2,1)S(1)}, bf16[1024,128]{1,0:T(8,128)(2,1)S(1)}, u32[]{:S(2)}, u32[]{:S(2)}) collective-permute-start(bf16[1024,128]{1,0:T(8,128)(2,1)S(1)} %add_convert_fusion.2), channel_id=1, source_target_pairs={{0,32},{1,225},{2,34},{3,227},{32,64},{33,1},{34,66},{35,3},{64,96... | collective-permute-start | bytes 786440 | tf_op jit(solution)/shard_map/ppermute | solution.py:315
  93.6 0.1 collective-permute-start.11
  93.7 5.5 %collective-permute-done.7.refs_4_ = bf16[1024,128]{1,0:T(8,128)(2,1)S(1)} collective-permute-done((bf16[1024,128]{1,0:T(8,128)(2,1)S(1)}, bf16[1024,128]{1,0:T(8,128)(2,1)S(1)}, u32[]{:S(2)}, u32[]{:S(2)}) %collective-permute-start.7) | collective-permute-done | bytes 262176 | tf_op jit(solution)/shard_map/ppermute | solution.py:315
  99.2 3.2 %collective-permute-start.8 = (bf16[512,128]{1,0:T(8,128)(2,1)S(1)}, bf16[512,128]{1,0:T(8,128)(2,1)S(1)}, u32[]{:S(2)}, u32[]{:S(2)}) collective-permute-start(bf16[512,128]{1,0:T(8,128)(2,1)S(1)} %add_convert_fusion.5), channel_id=1, source_target_pairs={{0,32},{1,225},{2,34},{3,227},{32,64},{33,1},{34,66},{35,3},{64,96... | collective-permute-start | bytes 393224 | tf_op jit(solution)/shard_map/ppermute | solution.py:315
  102.4 2.6 %collective-permute-done.8.refs_3_ = bf16[512,128]{1,0:T(8,128)(2,1)S(1)} collective-permute-done((bf16[512,128]{1,0:T(8,128)(2,1)S(1)}, bf16[512,128]{1,0:T(8,128)(2,1)S(1)}, u32[]{:S(2)}, u32[]{:S(2)}) %collective-permute-start.8) | collective-permute-done | bytes 131104 | tf_op jit(solution)/shard_map/ppermute | solution.py:315
  105.0 1.4 grid1.1.refs_0_
  106.4 2.4 %spread0.1 = bf16[8,8,128,128]{3,2,1,0:T(8,128)(2,1)} custom-call(s32[4]{0:T(128)S(1)} %pad_add_fusion.refs_0_.place, s32[64]{0:T(128)S(1)} %copy-done.10, bf16[512,128]{1,0:T(8,128)(2,1)S(1)} %copy-done.8, bf16[512,128]{1,0:T(8,128)(2,1)} %collective-permute-done.3.refs_1_, bf16[1024,128]{1,0:T(8,128)(2,1)S(1)} %collective-permute-done.5.refs_2_, ...), custom_call_target="tpu_custom_call" | custom-call | bytes 7000000 | tf_op jit(solution)/shard_map/spread0/pallas_call | solution.py:376
  108.8 4.5 %all-to-all-start.2 = ((bf16[8,8,128,128]{3,2,1,0:T(8,128)(2,1)}), bf16[8,8,128,128]{3,2,1,0:T(8,128)(2,1)S(1)}, u32[]{:S(2)}, u32[]{:S(2)}) async-start(bf16[8,8,128,128]{3,2,1,0:T(8,128)(2,1)} %spread0.1), calls=%async_computation.2 | async-start | bytes 4194304 | tf_op jit(solution)/shard_map/all_to_all | solution.py:359
  113.3 3.1 %collective-permute-start.12 = (bf16[512,128]{1,0:T(8,128)(2,1)S(1)}, bf16[512,128]{1,0:T(8,128)(2,1)S(1)}, u32[]{:S(2)}, u32[]{:S(2)}) collective-permute-start(bf16[512,128]{1,0:T(8,128)(2,1)S(1)} %grid1.1.refs_0_), channel_id=1, source_target_pairs={{0,32},{1,225},{2,34},{3,227},{32,64},{33,1},{34,66},{35,3},{64,96... | collective-permute-start | bytes 393224 | tf_op jit(solution)/shard_map/ppermute | solution.py:315
  116.3 1.9 collective-permute-done.12.refs_1_
  118.3 3.1 %collective-permute-start.13 = (bf16[512,128]{1,0:T(8,128)(2,1)S(1)}, bf16[512,128]{1,0:T(8,128)(2,1)S(1)}, u32[]{:S(2)}, u32[]{:S(2)}) collective-permute-start(bf16[512,128]{1,0:T(8,128)(2,1)S(1)} %collective-permute-done.12.refs_1_), channel_id=1, source_target_pairs={{0,32},{1,225},{2,34},{3,227},{32,64},{33,1},{34,66},{35,3},{64,96... | collective-permute-start | bytes 393224 | tf_op jit(solution)/shard_map/ppermute | solution.py:315
  121.4 1.9 collective-permute-done.13.refs_2_
  123.3 3.4 %collective-permute-start.14 = (bf16[512,128]{1,0:T(8,128)(2,1)S(1)}, bf16[512,128]{1,0:T(8,128)(2,1)S(1)}, u32[]{:S(2)}, u32[]{:S(2)}) collective-permute-start(bf16[512,128]{1,0:T(8,128)(2,1)S(1)} %collective-permute-done.13.refs_2_), channel_id=1, source_target_pairs={{0,32},{1,225},{2,34},{3,227},{32,64},{33,1},{34,66},{35,3},{64,96... | collective-permute-start | bytes 393224 | tf_op jit(solution)/shard_map/ppermute | solution.py:315
  126.7 1.9 collective-permute-done.14.refs_3_
  128.6 3.4 %collective-permute-start.15 = (bf16[512,128]{1,0:T(8,128)(2,1)S(1)}, bf16[512,128]{1,0:T(8,128)(2,1)S(1)}, u32[]{:S(2)}, u32[]{:S(2)}) collective-permute-start(bf16[512,128]{1,0:T(8,128)(2,1)S(1)} %collective-permute-done.14.refs_3_), channel_id=1, source_target_pairs={{0,32},{1,225},{2,34},{3,227},{32,64},{33,1},{34,66},{35,3},{64,96... | collective-permute-start | bytes 393224 | tf_op jit(solution)/shard_map/ppermute | solution.py:315
  132.0 0.8 collective-permute-done.18.refs_5_
  132.8 1.2 collective-permute-done.15.refs_4_
  134.0 2.0 spread1.1
  136.1 6.2 %all-to-all-start.3 = ((bf16[8,8,128,128]{3,2,1,0:T(8,128)(2,1)}), bf16[8,8,128,128]{3,2,1,0:T(8,128)(2,1)}, u32[]{:S(2)}, u32[]{:S(2)}) async-start(bf16[8,8,128,128]{3,2,1,0:T(8,128)(2,1)} %spread1.1), calls=%async_computation.3 | async-start | bytes 4194304 | tf_op jit(solution)/shard_map/all_to_all | solution.py:359
  142.3 5.1 %accum0.1 = (bf16[2048,128]{1,0:T(8,128)(2,1)S(1)}, bf16[2048,128]{1,0:T(8,128)(2,1)}, bf16[2048,128]{1,0:T(8,128)(2,1)}, bf16[2048,128]{1,0:T(8,128)(2,1)}) custom-call(s32[4]{0:T(128)S(1)} %pad_add_fusion.refs_0_.place, s32[64]{0:T(128)S(1)} %bitcast.27, bf16[8,8,128,128]{3,2,1,0:T(8,128)(2,1)S(1)} %all-to-all-done.2.returned, bf16[128,256]{1,0:T(8,128)(2,1)S(1)} %copy-done.9), custom_call_target="tpu_custom_call" | custom-call | bytes 17500000 | tf_op jit(solution)/shard_map/accum0/pallas_call | solution.py:382
  147.4 0.8 copy-done.3
  148.2 10.7 %collective-permute-start.19 = (bf16[2048,128]{1,0:T(8,128)(2,1)}, bf16[2048,128]{1,0:T(8,128)(2,1)S(1)}, u32[]{:S(2)}, u32[]{:S(2)}) collective-permute-start(bf16[2048,128]{1,0:T(8,128)(2,1)} %get-tuple-element.69), channel_id=1, source_target_pairs={{0,1},{1,0},{2,3},{3,2},{4,5},{5,4},{6,7},{7,6},{8,9},{9,8},{10,11... | collective-permute-start | bytes 1572872 | tf_op jit(solution)/shard_map/ppermute | solution.py:319
  158.9 2.5 %collective-permute-start.20 = (bf16[2048,128]{1,0:T(8,128)(2,1)}, bf16[2048,128]{1,0:T(8,128)(2,1)S(1)}, u32[]{:S(2)}, u32[]{:S(2)}) collective-permute-start(bf16[2048,128]{1,0:T(8,128)(2,1)} %get-tuple-element.70), channel_id=1, source_target_pairs={{0,2},{1,3},{2,0},{3,1},{4,6},{5,7},{6,4},{7,5},{8,10},{9,11},{10,... | collective-permute-start | bytes 1572872 | tf_op jit(solution)/shard_map/ppermute | solution.py:319
  161.4 0.7 collective-permute-start.21
  162.0 4.4 %accum1.1 = (bf16[2048,128]{1,0:T(8,128)(2,1)S(1)}, bf16[2048,128]{1,0:T(8,128)(2,1)S(1)}, bf16[2048,128]{1,0:T(8,128)(2,1)S(1)}, bf16[2048,128]{1,0:T(8,128)(2,1)S(1)}) custom-call(s32[4]{0:T(128)S(1)} %pad_add_fusion.refs_0_.place, s32[64]{0:T(128)S(1)} %bitcast.28, bf16[8,8,128,128]{3,2,1,0:T(8,128)(2,1)} %all-to-all-done.3.returned, ...), custom_call_target="tpu_custom_call" | custom-call | bytes 17500000 | tf_op jit(solution)/shard_map/accum1/pallas_call | solution.py:382
  166.5 12.7 %collective-permute-start.22 = (bf16[2048,128]{1,0:T(8,128)(2,1)S(1)}, bf16[2048,128]{1,0:T(8,128)(2,1)S(1)}, u32[]{:S(2)}, u32[]{:S(2)}) collective-permute-start(bf16[2048,128]{1,0:T(8,128)(2,1)S(1)} %get-tuple-element.74), channel_id=1, source_target_pairs={{0,1},{1,0},{2,3},{3,2},{4,5},{5,4},{6,7},{7,6},{8,9},{9,8},{10,11... | collective-permute-start | bytes 1572872 | tf_op jit(solution)/shard_map/ppermute | solution.py:319
  179.2 3.2 %collective-permute-start.23 = (bf16[2048,128]{1,0:T(8,128)(2,1)S(1)}, bf16[2048,128]{1,0:T(8,128)(2,1)S(1)}, u32[]{:S(2)}, u32[]{:S(2)}) collective-permute-start(bf16[2048,128]{1,0:T(8,128)(2,1)S(1)} %get-tuple-element.75), channel_id=1, source_target_pairs={{0,2},{1,3},{2,0},{3,1},{4,6},{5,7},{6,4},{7,5},{8,10},{9,11},{10,... | collective-permute-start | bytes 1572872 | tf_op jit(solution)/shard_map/ppermute | solution.py:319
  182.5 16.5 %collective-permute-done.21.refs_5_ = bf16[2048,128]{1,0:T(8,128)(2,1)S(1)} collective-permute-done((bf16[2048,128]{1,0:T(8,128)(2,1)}, bf16[2048,128]{1,0:T(8,128)(2,1)S(1)}, u32[]{:S(2)}, u32[]{:S(2)}) %collective-permute-start.21) | collective-permute-done | bytes 524320 | tf_op jit(solution)/shard_map/ppermute | solution.py:319
  199.0 4.4 %half.1.refs_2_ = f32[2048,512]{1,0:T(8,128)S(1)} custom-call(s32[4]{0:T(128)S(1)} %pad_add_fusion.refs_0_.place, bf16[2,4,128,512]{3,2,1,0:T(8,128)(2,1)S(1)} %bitcast.21, bf16[2048,128]{1,0:T(8,128)(2,1)S(1)} %copy-done.4, bf16[2048,128]{1,0:T(8,128)(2,1)S(1)} %collective-permute-done.19.refs_3_, bf16[2048,128]{1,0:T(8,128)(2,1)S(1)} %collective-permute-done.20.refs_4_, ...), custom_call_target="tpu_custom_call" | custom-call | bytes 14000000 | tf_op jit(solution)/shard_map/half/pallas_call | solution.py:448
  203.4 11.2 %collective-permute-done.24.refs_4_ = bf16[2048,128]{1,0:T(8,128)(2,1)S(1)} collective-permute-done((bf16[2048,128]{1,0:T(8,128)(2,1)S(1)}, bf16[2048,128]{1,0:T(8,128)(2,1)S(1)}, u32[]{:S(2)}, u32[]{:S(2)}) %collective-permute-start.24) | collective-permute-done | bytes 524320 | tf_op jit(solution)/shard_map/ppermute | solution.py:319
  214.6 3.4 %finish.1 = bf16[2,2048,256]{2,1,0:T(8,128)(2,1)} custom-call(s32[4]{0:T(128)S(1)} %pad_add_fusion.refs_0_.place, bf16[2,4,128,512]{3,2,1,0:T(8,128)(2,1)S(1)} %bitcast.22, f32[2048,512]{1,0:T(8,128)S(1)} %half.1.refs_2_, bf16[2048,128]{1,0:T(8,128)(2,1)S(1)} %collective-permute-done.23.refs_3_, bf16[2048,128]{1,0:T(8,128)(2,1)S(1)} %collective-permute-done.24.refs_4_), custom_call_target="tpu_custom_call" | custom-call | bytes 14000000 | tf_op jit(solution)/shard_map/finish/pallas_call | solution.py:458
  (55 shorter events, 0.5 us)
Async XLA Ops:
  7.0 7.5 %copy-start.16 = (s32[4,128]{1,0:T(4,128)S(1)}, s32[4,128]{1,0:T(4,128)}, u32[]{:S(2)}) copy-start(s32[4,128]{1,0:T(4,128)} %param.14) | copy-start | bytes 6148
  7.1 34.5 %all-to-all-start = ((bf16[16,4,128,128]{3,2,1,0:T(8,128)(2,1)}), bf16[16,4,128,128]{3,2,1,0:T(8,128)(2,1)}, u32[]{:S(2)}, u32[]{:S(2)}) async-start(bf16[16,4,128,128]{3,2,1,0:T(8,128)(2,1)} %contrib0.1), calls=%async_computation | async-start | bytes 4194304 | tf_op jit(solution)/shard_map/all_to_all | solution.py:359
  14.6 7.4 %copy-start.12 = (f32[32,512]{1,0:T(8,128)S(1)}, f32[32,512]{1,0:T(8,128)}, u32[]{:S(2)}) copy-start(f32[32,512]{1,0:T(8,128)} %constant.62.clone) | copy-start | bytes 196612
  14.6 7.4 %copy-start.13 = (f32[32,512]{1,0:T(8,128)S(1)}, f32[32,512]{1,0:T(8,128)}, u32[]{:S(2)}) copy-start(f32[32,512]{1,0:T(8,128)} %constant.61.clone) | copy-start | bytes 196612
  14.6 7.4 %copy-start.14 = (f32[16,512]{1,0:T(8,128)S(1)}, f32[16,512]{1,0:T(8,128)}, u32[]{:S(2)}) copy-start(f32[16,512]{1,0:T(8,128)} %constant.64.clone) | copy-start | bytes 98308
  14.6 7.4 %copy-start.15 = (f32[16,512]{1,0:T(8,128)S(1)}, f32[16,512]{1,0:T(8,128)}, u32[]{:S(2)}) copy-start(f32[16,512]{1,0:T(8,128)} %constant.63.clone) | copy-start | bytes 98308
  41.6 4.0 %copy-start.10 = (s32[64]{0:T(128)S(1)}, s32[64]{0:T(128)}, u32[]{:S(2)}) copy-start(s32[64]{0:T(128)} %offsets.3) | copy-start | bytes 772
  41.6 32.3 %all-to-all-start.1 = ((bf16[8,8,128,128]{3,2,1,0:T(8,128)(2,1)}), bf16[8,8,128,128]{3,2,1,0:T(8,128)(2,1)S(1)}, u32[]{:S(2)}, u32[]{:S(2)}) async-start(bf16[8,8,128,128]{3,2,1,0:T(8,128)(2,1)} %contrib1.1), calls=%async_computation.1 | async-start | bytes 4194304 | tf_op jit(solution)/shard_map/all_to_all | solution.py:359
  45.5 19.1 %copy-start.2 = (bf16[1,2,512,128]{3,2,1,0:T(8,128)(2,1)S(1)}, bf16[1,2,512,128]{3,2,1,0:T(8,128)(2,1)}, u32[]{:S(2)}) copy-start(bf16[1,2,512,128]{3,2,1,0:T(8,128)(2,1)} %param.15) | copy-start | bytes 786436
  45.6 19.1 %copy-start = (bf16[512,1024]{1,0:T(8,128)(2,1)S(1)}, bf16[512,1024]{1,0:T(8,128)(2,1)}, u32[]{:S(2)}) copy-start(bf16[512,1024]{1,0:T(8,128)(2,1)} %pad_maximum_fusion.refs_1_) | copy-start | bytes 3145732
  47.9 9.7 %collective-permute-start = (bf16[512,128]{1,0:T(8,128)(2,1)S(1)}, bf16[512,128]{1,0:T(8,128)(2,1)S(1)}, u32[]{:S(2)}, u32[]{:S(2)}) collective-permute-start(bf16[512,128]{1,0:T(8,128)(2,1)S(1)} %get-tuple-element.51), channel_id=1, source_target_pairs={{0,128},{64,192},{128,0},{192,64},{1,129},{65,193},{129,1},{193,65... | collective-permute-start | bytes 393224 | tf_op jit(solution)/shard_map/ppermute | solution.py:305
  54.0 8.9 %collective-permute-start.1 = (bf16[512,128]{1,0:T(8,128)(2,1)S(1)}, bf16[512,128]{1,0:T(8,128)(2,1)S(1)}, u32[]{:S(2)}, u32[]{:S(2)}) collective-permute-start(bf16[512,128]{1,0:T(8,128)(2,1)S(1)} %get-tuple-element.52), channel_id=1, source_target_pairs={{0,64},{64,128},{128,192},{192,0},{1,65},{65,129},{129,193},{193,1... | collective-permute-start | bytes 393224 | tf_op jit(solution)/shard_map/ppermute | solution.py:305
  55.2 9.5 %collective-permute-start.2 = (bf16[512,128]{1,0:T(8,128)(2,1)S(1)}, bf16[512,128]{1,0:T(8,128)(2,1)S(1)}, u32[]{:S(2)}, u32[]{:S(2)}) collective-permute-start(bf16[512,128]{1,0:T(8,128)(2,1)S(1)} %get-tuple-element.53), channel_id=1, source_target_pairs={{0,192},{64,0},{128,64},{192,128},{1,193},{65,1},{129,65},{193,129... | collective-permute-start | bytes 393224 | tf_op jit(solution)/shard_map/ppermute | solution.py:305
  66.0 6.1 %collective-permute-start.4 = (bf16[512,128]{1,0:T(8,128)(2,1)S(1)}, bf16[512,128]{1,0:T(8,128)(2,1)S(1)}, u32[]{:S(2)}, u32[]{:S(2)}) collective-permute-start(bf16[512,128]{1,0:T(8,128)(2,1)S(1)} %grid0.1.refs_0_), channel_id=1, source_target_pairs={{0,224},{1,33},{2,226},{3,35},{32,0},{33,65},{34,2},{35,67},{64,32... | collective-permute-start | bytes 393224 | tf_op jit(solution)/shard_map/ppermute | solution.py:315
  69.2 4.7 %collective-permute-start.3 = (bf16[512,128]{1,0:T(8,128)(2,1)S(1)}, bf16[512,128]{1,0:T(8,128)(2,1)}, u32[]{:S(2)}, u32[]{:S(2)}) collective-permute-start(bf16[512,128]{1,0:T(8,128)(2,1)S(1)} %grid0.1.refs_0_), channel_id=1, source_target_pairs={{0,32},{1,225},{2,34},{3,227},{32,64},{33,1},{34,66},{35,3},{64,96... | collective-permute-start | bytes 393224 | tf_op jit(solution)/shard_map/ppermute | solution.py:315
  69.6 0.7 copy-start.7
  72.1 8.3 %copy-start.5 = (bf16[512,128]{1,0:T(8,128)(2,1)}, bf16[512,128]{1,0:T(8,128)(2,1)S(1)}, u32[]{:S(2)}) copy-start(bf16[512,128]{1,0:T(8,128)(2,1)S(1)} %collective-permute-done.4.refs_7_) | copy-start | bytes 393220
  75.7 6.6 %collective-permute-start.5 = (bf16[1024,128]{1,0:T(8,128)(2,1)S(1)}, bf16[1024,128]{1,0:T(8,128)(2,1)S(1)}, u32[]{:S(2)}, u32[]{:S(2)}) collective-permute-start(bf16[1024,128]{1,0:T(8,128)(2,1)S(1)} %pad_maximum_fusion.1), channel_id=1, source_target_pairs={{0,32},{1,225},{2,34},{3,227},{32,64},{33,1},{34,66},{35,3},{64,96... | collective-permute-start | bytes 786440 | tf_op jit(solution)/shard_map/ppermute | solution.py:315
  78.9 7.5 %collective-permute-start.9 = (bf16[1024,128]{1,0:T(8,128)(2,1)S(1)}, bf16[1024,128]{1,0:T(8,128)(2,1)S(1)}, u32[]{:S(2)}, u32[]{:S(2)}) collective-permute-start(bf16[1024,128]{1,0:T(8,128)(2,1)S(1)} %pad_maximum_fusion.2), channel_id=1, source_target_pairs={{0,224},{1,33},{2,226},{3,35},{32,0},{33,65},{34,2},{35,67},{64,32... | collective-permute-start | bytes 786440 | tf_op jit(solution)/shard_map/ppermute | solution.py:315
  80.4 24.6 %copy-start.1 = (bf16[512,1024]{1,0:T(8,128)(2,1)S(1)}, bf16[512,1024]{1,0:T(8,128)(2,1)}, u32[]{:S(2)}) copy-start(bf16[512,1024]{1,0:T(8,128)(2,1)} %pad_maximum_fusion.refs_1_) | copy-start | bytes 3145732
  82.3 8.0 %collective-permute-start.6 = (bf16[1024,128]{1,0:T(8,128)(2,1)S(1)}, bf16[1024,128]{1,0:T(8,128)(2,1)S(1)}, u32[]{:S(2)}, u32[]{:S(2)}) collective-permute-start(bf16[1024,128]{1,0:T(8,128)(2,1)S(1)} %add_convert_fusion.3), channel_id=1, source_target_pairs={{0,32},{1,225},{2,34},{3,227},{32,64},{33,1},{34,66},{35,3},{64,96... | collective-permute-start | bytes 786440 | tf_op jit(solution)/shard_map/ppermute | solution.py:315
  86.4 20.0 %copy-start.6 = (bf16[512,128]{1,0:T(8,128)(2,1)S(1)}, bf16[512,128]{1,0:T(8,128)(2,1)}, u32[]{:S(2)}) copy-start(bf16[512,128]{1,0:T(8,128)(2,1)} %copy-done.5) | copy-start | bytes 393220
  86.4 20.0 %copy-start.8 = (bf16[512,128]{1,0:T(8,128)(2,1)S(1)}, bf16[512,128]{1,0:T(8,128)(2,1)}, u32[]{:S(2)}) copy-start(bf16[512,128]{1,0:T(8,128)(2,1)} %copy-done.7) | copy-start | bytes 393220
  86.5 7.0 %collective-permute-start.10 = (bf16[1024,128]{1,0:T(8,128)(2,1)S(1)}, bf16[1024,128]{1,0:T(8,128)(2,1)S(1)}, u32[]{:S(2)}, u32[]{:S(2)}) collective-permute-start(bf16[1024,128]{1,0:T(8,128)(2,1)S(1)} %add_convert_fusion.1), channel_id=1, source_target_pairs={{0,224},{1,33},{2,226},{3,35},{32,0},{33,65},{34,2},{35,67},{64,32... | collective-permute-start | bytes 786440 | tf_op jit(solution)/shard_map/ppermute | solution.py:315
  90.3 8.9 %collective-permute-start.7 = (bf16[1024,128]{1,0:T(8,128)(2,1)S(1)}, bf16[1024,128]{1,0:T(8,128)(2,1)S(1)}, u32[]{:S(2)}, u32[]{:S(2)}) collective-permute-start(bf16[1024,128]{1,0:T(8,128)(2,1)S(1)} %add_convert_fusion.2), channel_id=1, source_target_pairs={{0,32},{1,225},{2,34},{3,227},{32,64},{33,1},{34,66},{35,3},{64,96... | collective-permute-start | bytes 786440 | tf_op jit(solution)/shard_map/ppermute | solution.py:315
  93.6 8.9 %collective-permute-start.11 = (bf16[512,128]{1,0:T(8,128)(2,1)S(1)}, bf16[512,128]{1,0:T(8,128)(2,1)S(1)}, u32[]{:S(2)}, u32[]{:S(2)}) collective-permute-start(bf16[512,128]{1,0:T(8,128)(2,1)S(1)} %add_convert_fusion.4), channel_id=1, source_target_pairs={{0,224},{1,33},{2,226},{3,35},{32,0},{33,65},{34,2},{35,67},{64,32... | collective-permute-start | bytes 393224 | tf_op jit(solution)/shard_map/ppermute | solution.py:315
  99.2 5.8 %collective-permute-start.8 = (bf16[512,128]{1,0:T(8,128)(2,1)S(1)}, bf16[512,128]{1,0:T(8,128)(2,1)S(1)}, u32[]{:S(2)}, u32[]{:S(2)}) collective-permute-start(bf16[512,128]{1,0:T(8,128)(2,1)S(1)} %add_convert_fusion.5), channel_id=1, source_target_pairs={{0,32},{1,225},{2,34},{3,227},{32,64},{33,1},{34,66},{35,3},{64,96... | collective-permute-start | bytes 393224 | tf_op jit(solution)/shard_map/ppermute | solution.py:315
  108.8 27.3 %all-to-all-start.2 = ((bf16[8,8,128,128]{3,2,1,0:T(8,128)(2,1)}), bf16[8,8,128,128]{3,2,1,0:T(8,128)(2,1)S(1)}, u32[]{:S(2)}, u32[]{:S(2)}) async-start(bf16[8,8,128,128]{3,2,1,0:T(8,128)(2,1)} %spread0.1), calls=%async_computation.2 | async-start | bytes 4194304 | tf_op jit(solution)/shard_map/all_to_all | solution.py:359
  113.3 5.0 %collective-permute-start.12 = (bf16[512,128]{1,0:T(8,128)(2,1)S(1)}, bf16[512,128]{1,0:T(8,128)(2,1)S(1)}, u32[]{:S(2)}, u32[]{:S(2)}) collective-permute-start(bf16[512,128]{1,0:T(8,128)(2,1)S(1)} %grid1.1.refs_0_), channel_id=1, source_target_pairs={{0,32},{1,225},{2,34},{3,227},{32,64},{33,1},{34,66},{35,3},{64,96... | collective-permute-start | bytes 393224 | tf_op jit(solution)/shard_map/ppermute | solution.py:315
  116.3 5.0 %collective-permute-start.16 = (bf16[512,128]{1,0:T(8,128)(2,1)S(1)}, bf16[512,128]{1,0:T(8,128)(2,1)S(1)}, u32[]{:S(2)}, u32[]{:S(2)}) collective-permute-start(bf16[512,128]{1,0:T(8,128)(2,1)S(1)} %grid1.1.refs_0_), channel_id=1, source_target_pairs={{0,224},{1,33},{2,226},{3,35},{32,0},{33,65},{34,2},{35,67},{64,32... | collective-permute-start | bytes 393224 | tf_op jit(solution)/shard_map/ppermute | solution.py:315
  118.3 5.0 %collective-permute-start.13 = (bf16[512,128]{1,0:T(8,128)(2,1)S(1)}, bf16[512,128]{1,0:T(8,128)(2,1)S(1)}, u32[]{:S(2)}, u32[]{:S(2)}) collective-permute-start(bf16[512,128]{1,0:T(8,128)(2,1)S(1)} %collective-permute-done.12.refs_1_), channel_id=1, source_target_pairs={{0,32},{1,225},{2,34},{3,227},{32,64},{33,1},{34,66},{35,3},{64,96... | collective-permute-start | bytes 393224 | tf_op jit(solution)/shard_map/ppermute | solution.py:315
  121.4 5.3 %collective-permute-start.17 = (bf16[512,128]{1,0:T(8,128)(2,1)S(1)}, bf16[512,128]{1,0:T(8,128)(2,1)S(1)}, u32[]{:S(2)}, u32[]{:S(2)}) collective-permute-start(bf16[512,128]{1,0:T(8,128)(2,1)S(1)} %collective-permute-done.16.refs_7_), channel_id=1, source_target_pairs={{0,224},{1,33},{2,226},{3,35},{32,0},{33,65},{34,2},{35,67},{64,32... | collective-permute-start | bytes 393224 | tf_op jit(solution)/shard_map/ppermute | solution.py:315
  123.3 5.3 %collective-permute-start.14 = (bf16[512,128]{1,0:T(8,128)(2,1)S(1)}, bf16[512,128]{1,0:T(8,128)(2,1)S(1)}, u32[]{:S(2)}, u32[]{:S(2)}) collective-permute-start(bf16[512,128]{1,0:T(8,128)(2,1)S(1)} %collective-permute-done.13.refs_2_), channel_id=1, source_target_pairs={{0,32},{1,225},{2,34},{3,227},{32,64},{33,1},{34,66},{35,3},{64,96... | collective-permute-start | bytes 393224 | tf_op jit(solution)/shard_map/ppermute | solution.py:315
  126.7 6.1 %collective-permute-start.18 = (bf16[512,128]{1,0:T(8,128)(2,1)S(1)}, bf16[512,128]{1,0:T(8,128)(2,1)S(1)}, u32[]{:S(2)}, u32[]{:S(2)}) collective-permute-start(bf16[512,128]{1,0:T(8,128)(2,1)S(1)} %collective-permute-done.17.refs_6_), channel_id=1, source_target_pairs={{0,224},{1,33},{2,226},{3,35},{32,0},{33,65},{34,2},{35,67},{64,32... | collective-permute-start | bytes 393224 | tf_op jit(solution)/shard_map/ppermute | solution.py:315
  128.6 5.3 %collective-permute-start.15 = (bf16[512,128]{1,0:T(8,128)(2,1)S(1)}, bf16[512,128]{1,0:T(8,128)(2,1)S(1)}, u32[]{:S(2)}, u32[]{:S(2)}) collective-permute-start(bf16[512,128]{1,0:T(8,128)(2,1)S(1)} %collective-permute-done.14.refs_3_), channel_id=1, source_target_pairs={{0,32},{1,225},{2,34},{3,227},{32,64},{33,1},{34,66},{35,3},{64,96... | collective-permute-start | bytes 393224 | tf_op jit(solution)/shard_map/ppermute | solution.py:315
  136.0 6.3 %copy-start.9 = (bf16[128,256]{1,0:T(8,128)(2,1)S(1)}, bf16[128,256]{1,0:T(8,128)(2,1)}, u32[]{:S(2)}) copy-start(bf16[128,256]{1,0:T(8,128)(2,1)} %constant.66.clone.table) | copy-start | bytes 196612
  136.0 6.3 %copy-start.11 = (s32[64,1]{0,1:T(1,128)S(1)}, s32[64,1]{0,1:T(1,128)}, u32[]{:S(2)}) copy-start(s32[64,1]{0,1:T(1,128)} %param.12) | copy-start | bytes 772
  136.1 26.0 %all-to-all-start.3 = ((bf16[8,8,128,128]{3,2,1,0:T(8,128)(2,1)}), bf16[8,8,128,128]{3,2,1,0:T(8,128)(2,1)}, u32[]{:S(2)}, u32[]{:S(2)}) async-start(bf16[8,8,128,128]{3,2,1,0:T(8,128)(2,1)} %spread1.1), calls=%async_computation.3 | async-start | bytes 4194304 | tf_op jit(solution)/shard_map/all_to_all | solution.py:359
  147.4 0.8 copy-start.3
  148.2 50.8 %copy-start.4 = (bf16[2048,128]{1,0:T(8,128)(2,1)S(1)}, bf16[2048,128]{1,0:T(8,128)(2,1)}, u32[]{:S(2)}) copy-start(bf16[2048,128]{1,0:T(8,128)(2,1)} %copy-done.3) | copy-start | bytes 1572868
  148.2 34.2 %collective-permute-start.19 = (bf16[2048,128]{1,0:T(8,128)(2,1)}, bf16[2048,128]{1,0:T(8,128)(2,1)S(1)}, u32[]{:S(2)}, u32[]{:S(2)}) collective-permute-start(bf16[2048,128]{1,0:T(8,128)(2,1)} %get-tuple-element.69), channel_id=1, source_target_pairs={{0,1},{1,0},{2,3},{3,2},{4,5},{5,4},{6,7},{7,6},{8,9},{9,8},{10,11... | collective-permute-start | bytes 1572872 | tf_op jit(solution)/shard_map/ppermute | solution.py:319
  158.9 23.6 %collective-permute-start.20 = (bf16[2048,128]{1,0:T(8,128)(2,1)}, bf16[2048,128]{1,0:T(8,128)(2,1)S(1)}, u32[]{:S(2)}, u32[]{:S(2)}) collective-permute-start(bf16[2048,128]{1,0:T(8,128)(2,1)} %get-tuple-element.70), channel_id=1, source_target_pairs={{0,2},{1,3},{2,0},{3,1},{4,6},{5,7},{6,4},{7,5},{8,10},{9,11},{10,... | collective-permute-start | bytes 1572872 | tf_op jit(solution)/shard_map/ppermute | solution.py:319
  161.4 37.6 %collective-permute-start.21 = (bf16[2048,128]{1,0:T(8,128)(2,1)}, bf16[2048,128]{1,0:T(8,128)(2,1)S(1)}, u32[]{:S(2)}, u32[]{:S(2)}) collective-permute-start(bf16[2048,128]{1,0:T(8,128)(2,1)} %get-tuple-element.71), channel_id=1, source_target_pairs={{0,3},{1,2},{2,1},{3,0},{4,7},{5,6},{6,5},{7,4},{8,11},{9,10},{10,... | collective-permute-start | bytes 1572872 | tf_op jit(solution)/shard_map/ppermute | solution.py:319
  166.5 32.5 %collective-permute-start.22 = (bf16[2048,128]{1,0:T(8,128)(2,1)S(1)}, bf16[2048,128]{1,0:T(8,128)(2,1)S(1)}, u32[]{:S(2)}, u32[]{:S(2)}) collective-permute-start(bf16[2048,128]{1,0:T(8,128)(2,1)S(1)} %get-tuple-element.74), channel_id=1, source_target_pairs={{0,1},{1,0},{2,3},{3,2},{4,5},{5,4},{6,7},{7,6},{8,9},{9,8},{10,11... | collective-permute-start | bytes 1572872 | tf_op jit(solution)/shard_map/ppermute | solution.py:319
  179.2 24.3 %collective-permute-start.23 = (bf16[2048,128]{1,0:T(8,128)(2,1)S(1)}, bf16[2048,128]{1,0:T(8,128)(2,1)S(1)}, u32[]{:S(2)}, u32[]{:S(2)}) collective-permute-start(bf16[2048,128]{1,0:T(8,128)(2,1)S(1)} %get-tuple-element.75), channel_id=1, source_target_pairs={{0,2},{1,3},{2,0},{3,1},{4,6},{5,7},{6,4},{7,5},{8,10},{9,11},{10,... | collective-permute-start | bytes 1572872 | tf_op jit(solution)/shard_map/ppermute | solution.py:319
  182.4 32.2 %collective-permute-start.24 = (bf16[2048,128]{1,0:T(8,128)(2,1)S(1)}, bf16[2048,128]{1,0:T(8,128)(2,1)S(1)}, u32[]{:S(2)}, u32[]{:S(2)}) collective-permute-start(bf16[2048,128]{1,0:T(8,128)(2,1)S(1)} %get-tuple-element.76), channel_id=1, source_target_pairs={{0,3},{1,2},{2,1},{3,0},{4,7},{5,6},{6,5},{7,4},{8,11},{9,10},{10,... | collective-permute-start | bytes 1572872 | tf_op jit(solution)/shard_map/ppermute | solution.py:319

commit v5 on v4

--- a/solution.py
+++ b/solution.py
@@ -364,7 +364,7 @@
             lambda *refs: gather_kernel(c, ks, *refs), f"gather{c}{ks[0]}", outs,
             [SMEM, SMEM, HBM], [held[c], grid_rows, sems[c]], 1, 8,
         )(place, fac_off, arrived)
-        return dict(zip(ks, made))
+        return dict(zip(ks, made if len(ks) > 1 else [made]))
 
     def image_of(c, parts):
         return call(
@@ -398,7 +398,7 @@
     arrived1 = near(1, payload1)
 
     steps = sorted(range(1, depths[0]), key=lambda k: -min(k, depths[0] - k))
-    parts0 = gather(0, arrived0, [*range(depths[0])], ())
+    parts0 = gather(0, arrived0, steps, ()) | gather(0, arrived0, [0], ())
     image0 = image_of(0, [parts0[0]] + [shifted(parts0[k], k) for k in steps])
 
     far, near_side = depths[1] // 2, (depths[1] - 1) // 2

time: 219 us -> 218 us (level)
    pallas_call x3 -> x4, Pallas kernels: 4.53 us -> 6.12 us  [gather(): call(lambda *refs: gather_kernel(c, ks, *refs), f'gather{c}{ks[0]}', outs...]
  transfers between devices with their start and end apart: 29 -> 29, of which waited for: 17 -> 17; matrix products, arithmetic and copies ran while one was open for 2% -> 2% of each run, Pallas kernels for 13% -> 14%
where the time goes in v5:
time: 218 us
  starting transfers between devices  91.5 us (42%)
  waiting for transfers between devices  73.8 us (34%)
  Pallas kernels  45 us (21%)
  other arithmetic  5.42 us (2%)
    ppermute x16, starting transfers between devices, turned(): return lax.ppermute(value, (*FAR[1], 'col'), perm)  29.9 us
    ppermute x6, starting transfers between devices, swapped(): lax.ppermute(value, 'col', [(i, i ^ flip) for i in range(lax.axis_size('c...  29.8 us
    ppermute x6, waiting for transfers between devices, swapped(): lax.ppermute(value, 'col', [(i, i ^ flip) for i in range(lax.axis_size('c...  27.6 us
    ppermute x16, waiting for transfers between devices, turned(): return lax.ppermute(value, (*FAR[1], 'col'), perm)  25.6 us
    all_to_all x4, starting transfers between devices, near(): return lax.all_to_all(value, NEAR[c], 0, 0, tiled=True)  22.2 us
    all_to_all x4, waiting for transfers between devices, near(): return lax.all_to_all(value, NEAR[c], 0, 0, tiled=True)  15.4 us
    pallas_call x2, Pallas kernels, contrib(): call(bind(contrib_kernel, c), f'contrib{c}', [blocks[c]], [SMEM, HBM, VME...  14.4 us
    ppermute x3, starting transfers between devices, shifted(): lax.ppermute(value, 'zq', [(i, (i + step) % size) for i in range(size)])  9.67 us
  transfers between devices with their start and end apart: 29, of which 17 were waited for; matrix products, arithmetic and copies ran while one was open for 2% of the time, Pallas kernels for 14%

profile of v5, /device:TPU:1, one launch (start us, length us, event | category | flops | bytes accessed | tf_op | source)
XLA Modules:
  0.0 217.8 jit_solution(5940469413355206980)
XLA Ops:
  0.0 7.1 %contrib0.1 = bf16[16,4,128,128]{3,2,1,0:T(8,128)(2,1)} custom-call(s32[64]{0:T(128)} %bitcast.25, bf16[2,8192,128]{2,1,0:T(8,128)(2,1)} %bitcast.29, bf16[128,256]{1,0:T(8,128)(2,1)} %constant.65.clone.refs_2_), custom_call_target="tpu_custom_call" | custom-call | bytes 28000000 | tf_op jit(solution)/shard_map/contrib0/pallas_call | solution.py:352
  7.1 7.5 %all-to-all-start = ((bf16[16,4,128,128]{3,2,1,0:T(8,128)(2,1)}), bf16[16,4,128,128]{3,2,1,0:T(8,128)(2,1)}, u32[]{:S(2)}, u32[]{:S(2)}) async-start(bf16[16,4,128,128]{3,2,1,0:T(8,128)(2,1)} %contrib0.1), calls=%async_computation | async-start | bytes 4194304 | tf_op jit(solution)/shard_map/all_to_all | solution.py:359
  14.7 7.4 %contrib1.1 = bf16[8,8,128,128]{3,2,1,0:T(8,128)(2,1)} custom-call(s32[64]{0:T(128)} %bitcast.26, bf16[2,8192,128]{2,1,0:T(8,128)(2,1)} %bitcast.30, bf16[128,256]{1,0:T(8,128)(2,1)} %constant.65.clone.refs_2_), custom_call_target="tpu_custom_call" | custom-call | bytes 28000000 | tf_op jit(solution)/shard_map/contrib1/pallas_call | solution.py:352
  22.1 0.4 subtract_convert_fusion
  22.5 1.1 pad_maximum_fusion.refs_1_
  23.6 2.5 %fusion.7 = (bf16[4,2,1,64,256]{4,3,2,0,1:T(8,128)(2,1)S(1)}, bf16[4,2,1,64,256]{4,3,2,0,1:T(8,128)(2,1)S(1)}, bf16[4,2,1,64,256]{4,3,2,0,1:T(8,128)(2,1)S(1)}) fusion(s32[4,2,64]{2,0,1:T(4,128)S(1)} %copy.12), kind=kLoop, calls=%fused_computation.20 | loop fusion | flops 2621440 | bytes 788480 | tf_op jit(solution)/shard_map/concatenate | solution.py:64
  26.1 0.1 maximum_maximum_fusion
  26.2 15.4 %all-to-all-done.refs_2_ = bf16[16,4,128,128]{3,2,1,0:T(8,128)(2,1)} async-done(((bf16[16,4,128,128]{3,2,1,0:T(8,128)(2,1)}), bf16[16,4,128,128]{3,2,1,0:T(8,128)(2,1)}, u32[]{:S(2)}, u32[]{:S(2)}) %all-to-all-start) | async-done | bytes 2097184 | tf_op jit(solution)/shard_map/all_to_all | solution.py:359
  41.6 4.0 %all-to-all-start.1 = ((bf16[8,8,128,128]{3,2,1,0:T(8,128)(2,1)}), bf16[8,8,128,128]{3,2,1,0:T(8,128)(2,1)S(1)}, u32[]{:S(2)}, u32[]{:S(2)}) async-start(bf16[8,8,128,128]{3,2,1,0:T(8,128)(2,1)} %contrib1.1), calls=%async_computation.1 | async-start | bytes 4194304 | tf_op jit(solution)/shard_map/all_to_all | solution.py:359
  45.7 2.1 gather02.1
  47.8 6.1 %collective-permute-start = (bf16[512,128]{1,0:T(8,128)(2,1)S(1)}, bf16[512,128]{1,0:T(8,128)(2,1)S(1)}, u32[]{:S(2)}, u32[]{:S(2)}) collective-permute-start(bf16[512,128]{1,0:T(8,128)(2,1)S(1)} %get-tuple-element.49), channel_id=1, source_target_pairs={{0,128},{64,192},{128,0},{192,64},{1,129},{65,193},{129,1},{193,65... | collective-permute-start | bytes 393224 | tf_op jit(solution)/shard_map/ppermute | solution.py:305
  53.9 1.2 collective-permute-start.1
  55.1 2.4 %collective-permute-start.2 = (bf16[512,128]{1,0:T(8,128)(2,1)S(1)}, bf16[512,128]{1,0:T(8,128)(2,1)S(1)}, u32[]{:S(2)}, u32[]{:S(2)}) collective-permute-start(bf16[512,128]{1,0:T(8,128)(2,1)S(1)} %get-tuple-element.51), channel_id=1, source_target_pairs={{0,192},{64,0},{128,64},{192,128},{1,193},{65,1},{129,65},{193,129... | collective-permute-start | bytes 393224 | tf_op jit(solution)/shard_map/ppermute | solution.py:305
  57.5 1.8 gather00.1.refs_2_
  59.3 3.6 %collective-permute-done.1.refs_4_ = bf16[512,128]{1,0:T(8,128)(2,1)S(1)} collective-permute-done((bf16[512,128]{1,0:T(8,128)(2,1)S(1)}, bf16[512,128]{1,0:T(8,128)(2,1)S(1)}, u32[]{:S(2)}, u32[]{:S(2)}) %collective-permute-start.1) | collective-permute-done | bytes 131104 | tf_op jit(solution)/shard_map/ppermute | solution.py:305
  62.9 1.6 collective-permute-done.2.refs_5_
  64.5 1.4 grid0.1.refs_0_
  65.8 3.2 %collective-permute-start.4 = (bf16[512,128]{1,0:T(8,128)(2,1)S(1)}, bf16[512,128]{1,0:T(8,128)(2,1)S(1)}, u32[]{:S(2)}, u32[]{:S(2)}) collective-permute-start(bf16[512,128]{1,0:T(8,128)(2,1)S(1)} %grid0.1.refs_0_), channel_id=1, source_target_pairs={{0,224},{1,33},{2,226},{3,35},{32,0},{33,65},{34,2},{35,67},{64,32... | collective-permute-start | bytes 393224 | tf_op jit(solution)/shard_map/ppermute | solution.py:315
  69.1 0.4 collective-permute-start.3
  69.4 0.7 copy-done.7
  70.1 1.9 collective-permute-done.4.refs_7_
  72.0 1.8 collective-permute-done.3.refs_1_
  73.8 0.9 gather14.1
  74.6 0.9 pad_maximum_fusion.1
  75.6 3.4 %collective-permute-start.5 = (bf16[1024,128]{1,0:T(8,128)(2,1)S(1)}, bf16[1024,128]{1,0:T(8,128)(2,1)S(1)}, u32[]{:S(2)}, u32[]{:S(2)}) collective-permute-start(bf16[1024,128]{1,0:T(8,128)(2,1)S(1)} %pad_maximum_fusion.1), channel_id=1, source_target_pairs={{0,32},{1,225},{2,34},{3,227},{32,64},{33,1},{34,66},{35,3},{64,96... | collective-permute-start | bytes 786440 | tf_op jit(solution)/shard_map/ppermute | solution.py:315
  79.0 0.1 collective-permute-start.9
  79.0 1.4 gather10.1
  80.5 1.8 collective-permute-done.5.refs_2_
  82.3 3.4 %collective-permute-start.6 = (bf16[1024,128]{1,0:T(8,128)(2,1)S(1)}, bf16[1024,128]{1,0:T(8,128)(2,1)S(1)}, u32[]{:S(2)}, u32[]{:S(2)}) collective-permute-start(bf16[1024,128]{1,0:T(8,128)(2,1)S(1)} %add_convert_fusion.3), channel_id=1, source_target_pairs={{0,32},{1,225},{2,34},{3,227},{32,64},{33,1},{34,66},{35,3},{64,96... | collective-permute-start | bytes 786440 | tf_op jit(solution)/shard_map/ppermute | solution.py:315
  85.7 0.9 collective-permute-done.9.refs_6_
  86.7 0.1 collective-permute-start.10
  86.8 3.3 %collective-permute-done.6.refs_3_ = bf16[1024,128]{1,0:T(8,128)(2,1)S(1)} collective-permute-done((bf16[1024,128]{1,0:T(8,128)(2,1)S(1)}, bf16[1024,128]{1,0:T(8,128)(2,1)S(1)}, u32[]{:S(2)}, u32[]{:S(2)}) %collective-permute-start.6) | collective-permute-done | bytes 262176 | tf_op jit(solution)/shard_map/ppermute | solution.py:315
  90.2 3.2 %collective-permute-start.7 = (bf16[1024,128]{1,0:T(8,128)(2,1)S(1)}, bf16[1024,128]{1,0:T(8,128)(2,1)S(1)}, u32[]{:S(2)}, u32[]{:S(2)}) collective-permute-start(bf16[1024,128]{1,0:T(8,128)(2,1)S(1)} %add_convert_fusion.2), channel_id=1, source_target_pairs={{0,32},{1,225},{2,34},{3,227},{32,64},{33,1},{34,66},{35,3},{64,96... | collective-permute-start | bytes 786440 | tf_op jit(solution)/shard_map/ppermute | solution.py:315
  93.4 0.1 collective-permute-start.11
  93.5 5.5 %collective-permute-done.7.refs_4_ = bf16[1024,128]{1,0:T(8,128)(2,1)S(1)} collective-permute-done((bf16[1024,128]{1,0:T(8,128)(2,1)S(1)}, bf16[1024,128]{1,0:T(8,128)(2,1)S(1)}, u32[]{:S(2)}, u32[]{:S(2)}) %collective-permute-start.7) | collective-permute-done | bytes 262176 | tf_op jit(solution)/shard_map/ppermute | solution.py:315
  99.0 3.2 %collective-permute-start.8 = (bf16[512,128]{1,0:T(8,128)(2,1)S(1)}, bf16[512,128]{1,0:T(8,128)(2,1)S(1)}, u32[]{:S(2)}, u32[]{:S(2)}) collective-permute-start(bf16[512,128]{1,0:T(8,128)(2,1)S(1)} %add_convert_fusion.5), channel_id=1, source_target_pairs={{0,32},{1,225},{2,34},{3,227},{32,64},{33,1},{34,66},{35,3},{64,96... | collective-permute-start | bytes 393224 | tf_op jit(solution)/shard_map/ppermute | solution.py:315
  102.2 2.6 %collective-permute-done.8.refs_3_ = bf16[512,128]{1,0:T(8,128)(2,1)S(1)} collective-permute-done((bf16[512,128]{1,0:T(8,128)(2,1)S(1)}, bf16[512,128]{1,0:T(8,128)(2,1)S(1)}, u32[]{:S(2)}, u32[]{:S(2)}) %collective-permute-start.8) | collective-permute-done | bytes 131104 | tf_op jit(solution)/shard_map/ppermute | solution.py:315
  104.8 1.4 grid1.1.refs_0_
  106.2 2.4 %spread0.1 = bf16[8,8,128,128]{3,2,1,0:T(8,128)(2,1)} custom-call(s32[4]{0:T(128)S(1)} %pad_add_fusion.refs_0_.place, s32[64]{0:T(128)S(1)} %copy-done.10, bf16[512,128]{1,0:T(8,128)(2,1)S(1)} %copy-done.8, bf16[512,128]{1,0:T(8,128)(2,1)} %collective-permute-done.3.refs_1_, bf16[1024,128]{1,0:T(8,128)(2,1)S(1)} %collective-permute-done.5.refs_2_, ...), custom_call_target="tpu_custom_call" | custom-call | bytes 7000000 | tf_op jit(solution)/shard_map/spread0/pallas_call | solution.py:376
  108.6 4.5 %all-to-all-start.2 = ((bf16[8,8,128,128]{3,2,1,0:T(8,128)(2,1)}), bf16[8,8,128,128]{3,2,1,0:T(8,128)(2,1)S(1)}, u32[]{:S(2)}, u32[]{:S(2)}) async-start(bf16[8,8,128,128]{3,2,1,0:T(8,128)(2,1)} %spread0.1), calls=%async_computation.2 | async-start | bytes 4194304 | tf_op jit(solution)/shard_map/all_to_all | solution.py:359
  113.1 3.1 %collective-permute-start.12 = (bf16[512,128]{1,0:T(8,128)(2,1)S(1)}, bf16[512,128]{1,0:T(8,128)(2,1)S(1)}, u32[]{:S(2)}, u32[]{:S(2)}) collective-permute-start(bf16[512,128]{1,0:T(8,128)(2,1)S(1)} %grid1.1.refs_0_), channel_id=1, source_target_pairs={{0,32},{1,225},{2,34},{3,227},{32,64},{33,1},{34,66},{35,3},{64,96... | collective-permute-start | bytes 393224 | tf_op jit(solution)/shard_map/ppermute | solution.py:315
  116.2 1.9 collective-permute-done.12.refs_1_
  118.1 3.1 %collective-permute-start.13 = (bf16[512,128]{1,0:T(8,128)(2,1)S(1)}, bf16[512,128]{1,0:T(8,128)(2,1)S(1)}, u32[]{:S(2)}, u32[]{:S(2)}) collective-permute-start(bf16[512,128]{1,0:T(8,128)(2,1)S(1)} %collective-permute-done.12.refs_1_), channel_id=1, source_target_pairs={{0,32},{1,225},{2,34},{3,227},{32,64},{33,1},{34,66},{35,3},{64,96... | collective-permute-start | bytes 393224 | tf_op jit(solution)/shard_map/ppermute | solution.py:315
  121.2 1.9 collective-permute-done.13.refs_2_
  123.1 3.4 %collective-permute-start.14 = (bf16[512,128]{1,0:T(8,128)(2,1)S(1)}, bf16[512,128]{1,0:T(8,128)(2,1)S(1)}, u32[]{:S(2)}, u32[]{:S(2)}) collective-permute-start(bf16[512,128]{1,0:T(8,128)(2,1)S(1)} %collective-permute-done.13.refs_2_), channel_id=1, source_target_pairs={{0,32},{1,225},{2,34},{3,227},{32,64},{33,1},{34,66},{35,3},{64,96... | collective-permute-start | bytes 393224 | tf_op jit(solution)/shard_map/ppermute | solution.py:315
  126.5 1.9 collective-permute-done.14.refs_3_
  128.5 3.4 %collective-permute-start.15 = (bf16[512,128]{1,0:T(8,128)(2,1)S(1)}, bf16[512,128]{1,0:T(8,128)(2,1)S(1)}, u32[]{:S(2)}, u32[]{:S(2)}) collective-permute-start(bf16[512,128]{1,0:T(8,128)(2,1)S(1)} %collective-permute-done.14.refs_3_), channel_id=1, source_target_pairs={{0,32},{1,225},{2,34},{3,227},{32,64},{33,1},{34,66},{35,3},{64,96... | collective-permute-start | bytes 393224 | tf_op jit(solution)/shard_map/ppermute | solution.py:315
  131.8 0.8 collective-permute-done.18.refs_5_
  132.6 1.2 collective-permute-done.15.refs_4_
  133.8 2.0 spread1.1
  135.9 6.2 %all-to-all-start.3 = ((bf16[8,8,128,128]{3,2,1,0:T(8,128)(2,1)}), bf16[8,8,128,128]{3,2,1,0:T(8,128)(2,1)}, u32[]{:S(2)}, u32[]{:S(2)}) async-start(bf16[8,8,128,128]{3,2,1,0:T(8,128)(2,1)} %spread1.1), calls=%async_computation.3 | async-start | bytes 4194304 | tf_op jit(solution)/shard_map/all_to_all | solution.py:359
  142.1 5.1 %accum0.1 = (bf16[2048,128]{1,0:T(8,128)(2,1)S(1)}, bf16[2048,128]{1,0:T(8,128)(2,1)}, bf16[2048,128]{1,0:T(8,128)(2,1)}, bf16[2048,128]{1,0:T(8,128)(2,1)}) custom-call(s32[4]{0:T(128)S(1)} %pad_add_fusion.refs_0_.place, s32[64]{0:T(128)S(1)} %bitcast.27, bf16[8,8,128,128]{3,2,1,0:T(8,128)(2,1)S(1)} %all-to-all-done.2.returned, bf16[128,256]{1,0:T(8,128)(2,1)S(1)} %copy-done.9), custom_call_target="tpu_custom_call" | custom-call | bytes 17500000 | tf_op jit(solution)/shard_map/accum0/pallas_call | solution.py:382
  147.2 0.8 copy-done.3
  148.0 10.7 %collective-permute-start.19 = (bf16[2048,128]{1,0:T(8,128)(2,1)}, bf16[2048,128]{1,0:T(8,128)(2,1)S(1)}, u32[]{:S(2)}, u32[]{:S(2)}) collective-permute-start(bf16[2048,128]{1,0:T(8,128)(2,1)} %get-tuple-element.67), channel_id=1, source_target_pairs={{0,1},{1,0},{2,3},{3,2},{4,5},{5,4},{6,7},{7,6},{8,9},{9,8},{10,11... | collective-permute-start | bytes 1572872 | tf_op jit(solution)/shard_map/ppermute | solution.py:319
  158.7 2.4 %collective-permute-start.20 = (bf16[2048,128]{1,0:T(8,128)(2,1)}, bf16[2048,128]{1,0:T(8,128)(2,1)S(1)}, u32[]{:S(2)}, u32[]{:S(2)}) collective-permute-start(bf16[2048,128]{1,0:T(8,128)(2,1)} %get-tuple-element.68), channel_id=1, source_target_pairs={{0,2},{1,3},{2,0},{3,1},{4,6},{5,7},{6,4},{7,5},{8,10},{9,11},{10,... | collective-permute-start | bytes 1572872 | tf_op jit(solution)/shard_map/ppermute | solution.py:319
  161.2 0.7 collective-permute-start.21
  161.9 4.4 %accum1.1 = (bf16[2048,128]{1,0:T(8,128)(2,1)S(1)}, bf16[2048,128]{1,0:T(8,128)(2,1)S(1)}, bf16[2048,128]{1,0:T(8,128)(2,1)S(1)}, bf16[2048,128]{1,0:T(8,128)(2,1)S(1)}) custom-call(s32[4]{0:T(128)S(1)} %pad_add_fusion.refs_0_.place, s32[64]{0:T(128)S(1)} %bitcast.28, bf16[8,8,128,128]{3,2,1,0:T(8,128)(2,1)} %all-to-all-done.3.returned, ...), custom_call_target="tpu_custom_call" | custom-call | bytes 17500000 | tf_op jit(solution)/shard_map/accum1/pallas_call | solution.py:382
  166.3 12.7 %collective-permute-start.22 = (bf16[2048,128]{1,0:T(8,128)(2,1)S(1)}, bf16[2048,128]{1,0:T(8,128)(2,1)S(1)}, u32[]{:S(2)}, u32[]{:S(2)}) collective-permute-start(bf16[2048,128]{1,0:T(8,128)(2,1)S(1)} %get-tuple-element.72), channel_id=1, source_target_pairs={{0,1},{1,0},{2,3},{3,2},{4,5},{5,4},{6,7},{7,6},{8,9},{9,8},{10,11... | collective-permute-start | bytes 1572872 | tf_op jit(solution)/shard_map/ppermute | solution.py:319
  179.1 3.1 %collective-permute-start.23 = (bf16[2048,128]{1,0:T(8,128)(2,1)S(1)}, bf16[2048,128]{1,0:T(8,128)(2,1)S(1)}, u32[]{:S(2)}, u32[]{:S(2)}) collective-permute-start(bf16[2048,128]{1,0:T(8,128)(2,1)S(1)} %get-tuple-element.73), channel_id=1, source_target_pairs={{0,2},{1,3},{2,0},{3,1},{4,6},{5,7},{6,4},{7,5},{8,10},{9,11},{10,... | collective-permute-start | bytes 1572872 | tf_op jit(solution)/shard_map/ppermute | solution.py:319
  182.2 0.1 collective-permute-start.24
  182.3 16.4 %collective-permute-done.21.refs_5_ = bf16[2048,128]{1,0:T(8,128)(2,1)S(1)} collective-permute-done((bf16[2048,128]{1,0:T(8,128)(2,1)}, bf16[2048,128]{1,0:T(8,128)(2,1)S(1)}, u32[]{:S(2)}, u32[]{:S(2)}) %collective-permute-start.21) | collective-permute-done | bytes 524320 | tf_op jit(solution)/shard_map/ppermute | solution.py:319
  198.7 4.4 %half.1.refs_2_ = f32[2048,512]{1,0:T(8,128)S(1)} custom-call(s32[4]{0:T(128)S(1)} %pad_add_fusion.refs_0_.place, bf16[2,4,128,512]{3,2,1,0:T(8,128)(2,1)S(1)} %bitcast.21, bf16[2048,128]{1,0:T(8,128)(2,1)S(1)} %copy-done.4, bf16[2048,128]{1,0:T(8,128)(2,1)S(1)} %collective-permute-done.19.refs_3_, bf16[2048,128]{1,0:T(8,128)(2,1)S(1)} %collective-permute-done.20.refs_4_, ...), custom_call_target="tpu_custom_call" | custom-call | bytes 14000000 | tf_op jit(solution)/shard_map/half/pallas_call | solution.py:448
  203.1 11.3 %collective-permute-done.24.refs_4_ = bf16[2048,128]{1,0:T(8,128)(2,1)S(1)} collective-permute-done((bf16[2048,128]{1,0:T(8,128)(2,1)S(1)}, bf16[2048,128]{1,0:T(8,128)(2,1)S(1)}, u32[]{:S(2)}, u32[]{:S(2)}) %collective-permute-start.24) | collective-permute-done | bytes 524320 | tf_op jit(solution)/shard_map/ppermute | solution.py:319
  214.4 3.4 %finish.1 = bf16[2,2048,256]{2,1,0:T(8,128)(2,1)} custom-call(s32[4]{0:T(128)S(1)} %pad_add_fusion.refs_0_.place, bf16[2,4,128,512]{3,2,1,0:T(8,128)(2,1)S(1)} %bitcast.22, f32[2048,512]{1,0:T(8,128)S(1)} %half.1.refs_2_, bf16[2048,128]{1,0:T(8,128)(2,1)S(1)} %collective-permute-done.23.refs_3_, bf16[2048,128]{1,0:T(8,128)(2,1)S(1)} %collective-permute-done.24.refs_4_), custom_call_target="tpu_custom_call" | custom-call | bytes 14000000 | tf_op jit(solution)/shard_map/finish/pallas_call | solution.py:458
  (56 shorter events, 0.6 us)
Async XLA Ops:
  7.1 7.5 %copy-start.16 = (s32[4,128]{1,0:T(4,128)S(1)}, s32[4,128]{1,0:T(4,128)}, u32[]{:S(2)}) copy-start(s32[4,128]{1,0:T(4,128)} %param.14) | copy-start | bytes 6148
  7.1 34.6 %all-to-all-start = ((bf16[16,4,128,128]{3,2,1,0:T(8,128)(2,1)}), bf16[16,4,128,128]{3,2,1,0:T(8,128)(2,1)}, u32[]{:S(2)}, u32[]{:S(2)}) async-start(bf16[16,4,128,128]{3,2,1,0:T(8,128)(2,1)} %contrib0.1), calls=%async_computation | async-start | bytes 4194304 | tf_op jit(solution)/shard_map/all_to_all | solution.py:359
  14.6 7.4 %copy-start.12 = (f32[32,512]{1,0:T(8,128)S(1)}, f32[32,512]{1,0:T(8,128)}, u32[]{:S(2)}) copy-start(f32[32,512]{1,0:T(8,128)} %constant.62.clone) | copy-start | bytes 196612
  14.6 7.4 %copy-start.13 = (f32[32,512]{1,0:T(8,128)S(1)}, f32[32,512]{1,0:T(8,128)}, u32[]{:S(2)}) copy-start(f32[32,512]{1,0:T(8,128)} %constant.61.clone) | copy-start | bytes 196612
  14.7 7.4 %copy-start.14 = (f32[16,512]{1,0:T(8,128)S(1)}, f32[16,512]{1,0:T(8,128)}, u32[]{:S(2)}) copy-start(f32[16,512]{1,0:T(8,128)} %constant.64.clone) | copy-start | bytes 98308
  14.7 7.4 %copy-start.15 = (f32[16,512]{1,0:T(8,128)S(1)}, f32[16,512]{1,0:T(8,128)}, u32[]{:S(2)}) copy-start(f32[16,512]{1,0:T(8,128)} %constant.63.clone) | copy-start | bytes 98308
  41.6 4.1 %copy-start.10 = (s32[64]{0:T(128)S(1)}, s32[64]{0:T(128)}, u32[]{:S(2)}) copy-start(s32[64]{0:T(128)} %offsets.3) | copy-start | bytes 772
  41.6 32.1 %all-to-all-start.1 = ((bf16[8,8,128,128]{3,2,1,0:T(8,128)(2,1)}), bf16[8,8,128,128]{3,2,1,0:T(8,128)(2,1)S(1)}, u32[]{:S(2)}, u32[]{:S(2)}) async-start(bf16[8,8,128,128]{3,2,1,0:T(8,128)(2,1)} %contrib1.1), calls=%async_computation.1 | async-start | bytes 4194304 | tf_op jit(solution)/shard_map/all_to_all | solution.py:359
  45.7 18.8 %copy-start = (bf16[512,1024]{1,0:T(8,128)(2,1)S(1)}, bf16[512,1024]{1,0:T(8,128)(2,1)}, u32[]{:S(2)}) copy-start(bf16[512,1024]{1,0:T(8,128)(2,1)} %pad_maximum_fusion.refs_1_) | copy-start | bytes 3145732
  45.7 18.8 %copy-start.2 = (bf16[1,2,512,128]{3,2,1,0:T(8,128)(2,1)S(1)}, bf16[1,2,512,128]{3,2,1,0:T(8,128)(2,1)}, u32[]{:S(2)}) copy-start(bf16[1,2,512,128]{3,2,1,0:T(8,128)(2,1)} %param.15) | copy-start | bytes 786436
  47.8 11.5 %collective-permute-start = (bf16[512,128]{1,0:T(8,128)(2,1)S(1)}, bf16[512,128]{1,0:T(8,128)(2,1)S(1)}, u32[]{:S(2)}, u32[]{:S(2)}) collective-permute-start(bf16[512,128]{1,0:T(8,128)(2,1)S(1)} %get-tuple-element.49), channel_id=1, source_target_pairs={{0,128},{64,192},{128,0},{192,64},{1,129},{65,193},{129,1},{193,65... | collective-permute-start | bytes 393224 | tf_op jit(solution)/shard_map/ppermute | solution.py:305
  53.9 8.9 %collective-permute-start.1 = (bf16[512,128]{1,0:T(8,128)(2,1)S(1)}, bf16[512,128]{1,0:T(8,128)(2,1)S(1)}, u32[]{:S(2)}, u32[]{:S(2)}) collective-permute-start(bf16[512,128]{1,0:T(8,128)(2,1)S(1)} %get-tuple-element.50), channel_id=1, source_target_pairs={{0,64},{64,128},{128,192},{192,0},{1,65},{65,129},{129,193},{193,1... | collective-permute-start | bytes 393224 | tf_op jit(solution)/shard_map/ppermute | solution.py:305
  55.1 9.4 %collective-permute-start.2 = (bf16[512,128]{1,0:T(8,128)(2,1)S(1)}, bf16[512,128]{1,0:T(8,128)(2,1)S(1)}, u32[]{:S(2)}, u32[]{:S(2)}) collective-permute-start(bf16[512,128]{1,0:T(8,128)(2,1)S(1)} %get-tuple-element.51), channel_id=1, source_target_pairs={{0,192},{64,0},{128,64},{192,128},{1,193},{65,1},{129,65},{193,129... | collective-permute-start | bytes 393224 | tf_op jit(solution)/shard_map/ppermute | solution.py:305
  65.8 6.2 %collective-permute-start.4 = (bf16[512,128]{1,0:T(8,128)(2,1)S(1)}, bf16[512,128]{1,0:T(8,128)(2,1)S(1)}, u32[]{:S(2)}, u32[]{:S(2)}) collective-permute-start(bf16[512,128]{1,0:T(8,128)(2,1)S(1)} %grid0.1.refs_0_), channel_id=1, source_target_pairs={{0,224},{1,33},{2,226},{3,35},{32,0},{33,65},{34,2},{35,67},{64,32... | collective-permute-start | bytes 393224 | tf_op jit(solution)/shard_map/ppermute | solution.py:315
  69.1 4.7 %collective-permute-start.3 = (bf16[512,128]{1,0:T(8,128)(2,1)S(1)}, bf16[512,128]{1,0:T(8,128)(2,1)}, u32[]{:S(2)}, u32[]{:S(2)}) collective-permute-start(bf16[512,128]{1,0:T(8,128)(2,1)S(1)} %grid0.1.refs_0_), channel_id=1, source_target_pairs={{0,32},{1,225},{2,34},{3,227},{32,64},{33,1},{34,66},{35,3},{64,96... | collective-permute-start | bytes 393224 | tf_op jit(solution)/shard_map/ppermute | solution.py:315
  69.4 0.7 copy-start.7
  72.0 8.4 %copy-start.5 = (bf16[512,128]{1,0:T(8,128)(2,1)}, bf16[512,128]{1,0:T(8,128)(2,1)S(1)}, u32[]{:S(2)}) copy-start(bf16[512,128]{1,0:T(8,128)(2,1)S(1)} %collective-permute-done.4.refs_7_) | copy-start | bytes 393220
  75.6 6.7 %collective-permute-start.5 = (bf16[1024,128]{1,0:T(8,128)(2,1)S(1)}, bf16[1024,128]{1,0:T(8,128)(2,1)S(1)}, u32[]{:S(2)}, u32[]{:S(2)}) collective-permute-start(bf16[1024,128]{1,0:T(8,128)(2,1)S(1)} %pad_maximum_fusion.1), channel_id=1, source_target_pairs={{0,32},{1,225},{2,34},{3,227},{32,64},{33,1},{34,66},{35,3},{64,96... | collective-permute-start | bytes 786440 | tf_op jit(solution)/shard_map/ppermute | solution.py:315
  79.0 7.7 %collective-permute-start.9 = (bf16[1024,128]{1,0:T(8,128)(2,1)S(1)}, bf16[1024,128]{1,0:T(8,128)(2,1)S(1)}, u32[]{:S(2)}, u32[]{:S(2)}) collective-permute-start(bf16[1024,128]{1,0:T(8,128)(2,1)S(1)} %pad_maximum_fusion.2), channel_id=1, source_target_pairs={{0,224},{1,33},{2,226},{3,35},{32,0},{33,65},{34,2},{35,67},{64,32... | collective-permute-start | bytes 786440 | tf_op jit(solution)/shard_map/ppermute | solution.py:315
  80.4 24.4 %copy-start.1 = (bf16[512,1024]{1,0:T(8,128)(2,1)S(1)}, bf16[512,1024]{1,0:T(8,128)(2,1)}, u32[]{:S(2)}) copy-start(bf16[512,1024]{1,0:T(8,128)(2,1)} %pad_maximum_fusion.refs_1_) | copy-start | bytes 3145732
  82.3 7.7 %collective-permute-start.6 = (bf16[1024,128]{1,0:T(8,128)(2,1)S(1)}, bf16[1024,128]{1,0:T(8,128)(2,1)S(1)}, u32[]{:S(2)}, u32[]{:S(2)}) collective-permute-start(bf16[1024,128]{1,0:T(8,128)(2,1)S(1)} %add_convert_fusion.3), channel_id=1, source_target_pairs={{0,32},{1,225},{2,34},{3,227},{32,64},{33,1},{34,66},{35,3},{64,96... | collective-permute-start | bytes 786440 | tf_op jit(solution)/shard_map/ppermute | solution.py:315
  86.6 19.6 %copy-start.6 = (bf16[512,128]{1,0:T(8,128)(2,1)S(1)}, bf16[512,128]{1,0:T(8,128)(2,1)}, u32[]{:S(2)}) copy-start(bf16[512,128]{1,0:T(8,128)(2,1)} %copy-done.5) | copy-start | bytes 393220
  86.6 19.6 %copy-start.8 = (bf16[512,128]{1,0:T(8,128)(2,1)S(1)}, bf16[512,128]{1,0:T(8,128)(2,1)}, u32[]{:S(2)}) copy-start(bf16[512,128]{1,0:T(8,128)(2,1)} %copy-done.7) | copy-start | bytes 393220
  86.7 6.6 %collective-permute-start.10 = (bf16[1024,128]{1,0:T(8,128)(2,1)S(1)}, bf16[1024,128]{1,0:T(8,128)(2,1)S(1)}, u32[]{:S(2)}, u32[]{:S(2)}) collective-permute-start(bf16[1024,128]{1,0:T(8,128)(2,1)S(1)} %add_convert_fusion.1), channel_id=1, source_target_pairs={{0,224},{1,33},{2,226},{3,35},{32,0},{33,65},{34,2},{35,67},{64,32... | collective-permute-start | bytes 786440 | tf_op jit(solution)/shard_map/ppermute | solution.py:315
  90.2 8.9 %collective-permute-start.7 = (bf16[1024,128]{1,0:T(8,128)(2,1)S(1)}, bf16[1024,128]{1,0:T(8,128)(2,1)S(1)}, u32[]{:S(2)}, u32[]{:S(2)}) collective-permute-start(bf16[1024,128]{1,0:T(8,128)(2,1)S(1)} %add_convert_fusion.2), channel_id=1, source_target_pairs={{0,32},{1,225},{2,34},{3,227},{32,64},{33,1},{34,66},{35,3},{64,96... | collective-permute-start | bytes 786440 | tf_op jit(solution)/shard_map/ppermute | solution.py:315
  93.4 8.8 %collective-permute-start.11 = (bf16[512,128]{1,0:T(8,128)(2,1)S(1)}, bf16[512,128]{1,0:T(8,128)(2,1)S(1)}, u32[]{:S(2)}, u32[]{:S(2)}) collective-permute-start(bf16[512,128]{1,0:T(8,128)(2,1)S(1)} %add_convert_fusion.4), channel_id=1, source_target_pairs={{0,224},{1,33},{2,226},{3,35},{32,0},{33,65},{34,2},{35,67},{64,32... | collective-permute-start | bytes 393224 | tf_op jit(solution)/shard_map/ppermute | solution.py:315
  99.0 5.8 %collective-permute-start.8 = (bf16[512,128]{1,0:T(8,128)(2,1)S(1)}, bf16[512,128]{1,0:T(8,128)(2,1)S(1)}, u32[]{:S(2)}, u32[]{:S(2)}) collective-permute-start(bf16[512,128]{1,0:T(8,128)(2,1)S(1)} %add_convert_fusion.5), channel_id=1, source_target_pairs={{0,32},{1,225},{2,34},{3,227},{32,64},{33,1},{34,66},{35,3},{64,96... | collective-permute-start | bytes 393224 | tf_op jit(solution)/shard_map/ppermute | solution.py:315
  108.6 27.3 %all-to-all-start.2 = ((bf16[8,8,128,128]{3,2,1,0:T(8,128)(2,1)}), bf16[8,8,128,128]{3,2,1,0:T(8,128)(2,1)S(1)}, u32[]{:S(2)}, u32[]{:S(2)}) async-start(bf16[8,8,128,128]{3,2,1,0:T(8,128)(2,1)} %spread0.1), calls=%async_computation.2 | async-start | bytes 4194304 | tf_op jit(solution)/shard_map/all_to_all | solution.py:359
  113.1 5.0 %collective-permute-start.12 = (bf16[512,128]{1,0:T(8,128)(2,1)S(1)}, bf16[512,128]{1,0:T(8,128)(2,1)S(1)}, u32[]{:S(2)}, u32[]{:S(2)}) collective-permute-start(bf16[512,128]{1,0:T(8,128)(2,1)S(1)} %grid1.1.refs_0_), channel_id=1, source_target_pairs={{0,32},{1,225},{2,34},{3,227},{32,64},{33,1},{34,66},{35,3},{64,96... | collective-permute-start | bytes 393224 | tf_op jit(solution)/shard_map/ppermute | solution.py:315
  116.2 5.0 %collective-permute-start.16 = (bf16[512,128]{1,0:T(8,128)(2,1)S(1)}, bf16[512,128]{1,0:T(8,128)(2,1)S(1)}, u32[]{:S(2)}, u32[]{:S(2)}) collective-permute-start(bf16[512,128]{1,0:T(8,128)(2,1)S(1)} %grid1.1.refs_0_), channel_id=1, source_target_pairs={{0,224},{1,33},{2,226},{3,35},{32,0},{33,65},{34,2},{35,67},{64,32... | collective-permute-start | bytes 393224 | tf_op jit(solution)/shard_map/ppermute | solution.py:315
  118.1 5.0 %collective-permute-start.13 = (bf16[512,128]{1,0:T(8,128)(2,1)S(1)}, bf16[512,128]{1,0:T(8,128)(2,1)S(1)}, u32[]{:S(2)}, u32[]{:S(2)}) collective-permute-start(bf16[512,128]{1,0:T(8,128)(2,1)S(1)} %collective-permute-done.12.refs_1_), channel_id=1, source_target_pairs={{0,32},{1,225},{2,34},{3,227},{32,64},{33,1},{34,66},{35,3},{64,96... | collective-permute-start | bytes 393224 | tf_op jit(solution)/shard_map/ppermute | solution.py:315
  121.2 5.3 %collective-permute-start.17 = (bf16[512,128]{1,0:T(8,128)(2,1)S(1)}, bf16[512,128]{1,0:T(8,128)(2,1)S(1)}, u32[]{:S(2)}, u32[]{:S(2)}) collective-permute-start(bf16[512,128]{1,0:T(8,128)(2,1)S(1)} %collective-permute-done.16.refs_7_), channel_id=1, source_target_pairs={{0,224},{1,33},{2,226},{3,35},{32,0},{33,65},{34,2},{35,67},{64,32... | collective-permute-start | bytes 393224 | tf_op jit(solution)/shard_map/ppermute | solution.py:315
  123.1 5.3 %collective-permute-start.14 = (bf16[512,128]{1,0:T(8,128)(2,1)S(1)}, bf16[512,128]{1,0:T(8,128)(2,1)S(1)}, u32[]{:S(2)}, u32[]{:S(2)}) collective-permute-start(bf16[512,128]{1,0:T(8,128)(2,1)S(1)} %collective-permute-done.13.refs_2_), channel_id=1, source_target_pairs={{0,32},{1,225},{2,34},{3,227},{32,64},{33,1},{34,66},{35,3},{64,96... | collective-permute-start | bytes 393224 | tf_op jit(solution)/shard_map/ppermute | solution.py:315
  126.5 6.1 %collective-permute-start.18 = (bf16[512,128]{1,0:T(8,128)(2,1)S(1)}, bf16[512,128]{1,0:T(8,128)(2,1)S(1)}, u32[]{:S(2)}, u32[]{:S(2)}) collective-permute-start(bf16[512,128]{1,0:T(8,128)(2,1)S(1)} %collective-permute-done.17.refs_6_), channel_id=1, source_target_pairs={{0,224},{1,33},{2,226},{3,35},{32,0},{33,65},{34,2},{35,67},{64,32... | collective-permute-start | bytes 393224 | tf_op jit(solution)/shard_map/ppermute | solution.py:315
  128.5 5.3 %collective-permute-start.15 = (bf16[512,128]{1,0:T(8,128)(2,1)S(1)}, bf16[512,128]{1,0:T(8,128)(2,1)S(1)}, u32[]{:S(2)}, u32[]{:S(2)}) collective-permute-start(bf16[512,128]{1,0:T(8,128)(2,1)S(1)} %collective-permute-done.14.refs_3_), channel_id=1, source_target_pairs={{0,32},{1,225},{2,34},{3,227},{32,64},{33,1},{34,66},{35,3},{64,96... | collective-permute-start | bytes 393224 | tf_op jit(solution)/shard_map/ppermute | solution.py:315
  135.8 6.3 %copy-start.9 = (bf16[128,256]{1,0:T(8,128)(2,1)S(1)}, bf16[128,256]{1,0:T(8,128)(2,1)}, u32[]{:S(2)}) copy-start(bf16[128,256]{1,0:T(8,128)(2,1)} %constant.66.clone.table) | copy-start | bytes 196612
  135.9 6.3 %copy-start.11 = (s32[64,1]{0,1:T(1,128)S(1)}, s32[64,1]{0,1:T(1,128)}, u32[]{:S(2)}) copy-start(s32[64,1]{0,1:T(1,128)} %param.12) | copy-start | bytes 772
  135.9 26.0 %all-to-all-start.3 = ((bf16[8,8,128,128]{3,2,1,0:T(8,128)(2,1)}), bf16[8,8,128,128]{3,2,1,0:T(8,128)(2,1)}, u32[]{:S(2)}, u32[]{:S(2)}) async-start(bf16[8,8,128,128]{3,2,1,0:T(8,128)(2,1)} %spread1.1), calls=%async_computation.3 | async-start | bytes 4194304 | tf_op jit(solution)/shard_map/all_to_all | solution.py:359
  147.2 0.8 copy-start.3
  148.0 50.6 %copy-start.4 = (bf16[2048,128]{1,0:T(8,128)(2,1)S(1)}, bf16[2048,128]{1,0:T(8,128)(2,1)}, u32[]{:S(2)}) copy-start(bf16[2048,128]{1,0:T(8,128)(2,1)} %copy-done.3) | copy-start | bytes 1572868
  148.0 34.1 %collective-permute-start.19 = (bf16[2048,128]{1,0:T(8,128)(2,1)}, bf16[2048,128]{1,0:T(8,128)(2,1)S(1)}, u32[]{:S(2)}, u32[]{:S(2)}) collective-permute-start(bf16[2048,128]{1,0:T(8,128)(2,1)} %get-tuple-element.67), channel_id=1, source_target_pairs={{0,1},{1,0},{2,3},{3,2},{4,5},{5,4},{6,7},{7,6},{8,9},{9,8},{10,11... | collective-permute-start | bytes 1572872 | tf_op jit(solution)/shard_map/ppermute | solution.py:319
  158.7 23.6 %collective-permute-start.20 = (bf16[2048,128]{1,0:T(8,128)(2,1)}, bf16[2048,128]{1,0:T(8,128)(2,1)S(1)}, u32[]{:S(2)}, u32[]{:S(2)}) collective-permute-start(bf16[2048,128]{1,0:T(8,128)(2,1)} %get-tuple-element.68), channel_id=1, source_target_pairs={{0,2},{1,3},{2,0},{3,1},{4,6},{5,7},{6,4},{7,5},{8,10},{9,11},{10,... | collective-permute-start | bytes 1572872 | tf_op jit(solution)/shard_map/ppermute | solution.py:319
  161.2 37.5 %collective-permute-start.21 = (bf16[2048,128]{1,0:T(8,128)(2,1)}, bf16[2048,128]{1,0:T(8,128)(2,1)S(1)}, u32[]{:S(2)}, u32[]{:S(2)}) collective-permute-start(bf16[2048,128]{1,0:T(8,128)(2,1)} %get-tuple-element.69), channel_id=1, source_target_pairs={{0,3},{1,2},{2,1},{3,0},{4,7},{5,6},{6,5},{7,4},{8,11},{9,10},{10,... | collective-permute-start | bytes 1572872 | tf_op jit(solution)/shard_map/ppermute | solution.py:319
  166.3 32.3 %collective-permute-start.22 = (bf16[2048,128]{1,0:T(8,128)(2,1)S(1)}, bf16[2048,128]{1,0:T(8,128)(2,1)S(1)}, u32[]{:S(2)}, u32[]{:S(2)}) collective-permute-start(bf16[2048,128]{1,0:T(8,128)(2,1)S(1)} %get-tuple-element.72), channel_id=1, source_target_pairs={{0,1},{1,0},{2,3},{3,2},{4,5},{5,4},{6,7},{7,6},{8,9},{9,8},{10,11... | collective-permute-start | bytes 1572872 | tf_op jit(solution)/shard_map/ppermute | solution.py:319
  179.1 24.0 %collective-permute-start.23 = (bf16[2048,128]{1,0:T(8,128)(2,1)S(1)}, bf16[2048,128]{1,0:T(8,128)(2,1)S(1)}, u32[]{:S(2)}, u32[]{:S(2)}) collective-permute-start(bf16[2048,128]{1,0:T(8,128)(2,1)S(1)} %get-tuple-element.73), channel_id=1, source_target_pairs={{0,2},{1,3},{2,0},{3,1},{4,6},{5,7},{6,4},{7,5},{8,10},{9,11},{10,... | collective-permute-start | bytes 1572872 | tf_op jit(solution)/shard_map/ppermute | solution.py:319
  182.2 32.2 %collective-permute-start.24 = (bf16[2048,128]{1,0:T(8,128)(2,1)S(1)}, bf16[2048,128]{1,0:T(8,128)(2,1)S(1)}, u32[]{:S(2)}, u32[]{:S(2)}) collective-permute-start(bf16[2048,128]{1,0:T(8,128)(2,1)S(1)} %get-tuple-element.74), channel_id=1, source_target_pairs={{0,3},{1,2},{2,1},{3,0},{4,7},{5,6},{6,5},{7,4},{8,11},{9,10},{10,... | collective-permute-start | bytes 1572872 | tf_op jit(solution)/shard_map/ppermute | solution.py:319
